TPU v7x, 256 devices: a whole 4x4x8 slice. The times are simulated.
256 devices in a mesh: face: 32 (over y_hi, z, core), level: 4 (over x), ens: 2 (over y_lo).
Axes of the slice: x: 4, y: 4 (y_hi: 2, y_lo: 2; y = y_hi * 2 + y_lo), z: 8, core: 2. Of those that a mesh axis runs over, the one named last changes fastest.
Arguments:
- state: bfloat16 [256, 16, 16, 512], P(('ens', 'face'), None, None, 'level'), parts along dimension 0, may hold values from -6 to 6
- conv_weight: bfloat16 [2, 2, 9, 64, 64], replicated, may hold values from -0.25 to 0.25
- mix_in: bfloat16 [2, 512, 512], replicated, may hold values from -0.25 to 0.25
- mix_out: bfloat16 [2, 512, 512], replicated, may hold values from -0.25 to 0.25
- edge_source: int32 [128, 4], replicated, may hold values from 0 to 511, as said below
- corner_source: int32 [128, 4], replicated, may hold values from -1 to 511, as said below
Outputs:
- forecast: bfloat16 [256, 16, 16, 512], P(('ens', 'face'), None, None, 'level'), parts along dimension 0
There are 2 independent parts, one for each index of `ens`. A program takes and returns all parts, laid end to end along the dimension named above; an argument that names none is the same for every part. Nothing has to cross between parts.
Inputs may be any that keep to these rules, and one draw needn't show every extreme that they name: Each strip number 0 to 511 appears exactly once. Tiles 4 d to 4 d + 3 lie on index d of face; the tile u of edge_source[t, s] lies on the device of t, on the device whose index differs from it in the lowest bit, or on the device two indices away in either direction (cyclically). Exactly 4 strips of one device border tiles of the device whose index differs in the lowest bit; when 32 > 4 exactly 2 border tiles of a device two indices away. `corner_source`: each entry is -1 or a corner pixel number; a corner pixel number appears at most once. Its tile lies on a device allowed for edge_source, or on a device two indices (cyclically) away from the one whose index differs from t's device in the lowest bit.
All inputs are finite; a program needn't handle non-finite values.
Results may differ from a plain program's by a relative error of at most 0.022.
Values may be sent and summed in bfloat16 or wider, within the bound.
No kernel may reach another device: no remote copies, remote signals or barrier semaphores. Data moves between devices by JAX's collectives and lax.ppermute only.
A program may use at most 64 MiB of HBM per device.

v0:
```python
import functools

import jax
import jax.numpy as jnp
import numpy as np
from jax import lax
from jax.experimental import pallas as pl
from jax.experimental.pallas import tpu as pltpu
from jax.sharding import PartitionSpec as P

BF16, F32, I32 = jnp.bfloat16, jnp.float32, jnp.int32
SIDE = 16
PIXELS = SIDE * SIDE
HERE = 4
STRIPS = 4 * HERE
ZERO_ROW = 6 * STRIPS
VMEM_LIMIT = 48 * 1024 * 1024


def one_hot(columns, width):
    table = np.zeros((len(columns), width), np.float32)
    for row, column in enumerate(columns):
        table[row, column] = 1.0
    return table.astype(jnp.bfloat16)


def strip_table():
    rising, falling = range(SIDE), range(SIDE - 1, -1, -1)
    last = SIDE - 1
    return one_hot(
        [k for k in rising]
        + [k * SIDE + last for k in rising]
        + [last * SIDE + k for k in falling]
        + [k * SIDE for k in falling],
        PIXELS,
    )


def corner_table():
    return one_hot([SIDE * strip for strip in range(STRIPS)], SIDE * STRIPS)


def shift_table():
    half, rim = SIDE // 2, PIXELS // 2
    groups = []
    for group in range(2):
        columns = []
        for i in range(half):
            for j in range(SIDE):
                columns.append(i * SIDE + j - 1 if j else rim + 48 + group * half + i)
        for i in range(half):
            for j in range(SIDE):
                columns.append(i * SIDE + j + 1 if j < SIDE - 1 else rim + 16 + SIDE - 1 - group * half - i)
        groups.append(one_hot(columns, rim + 80))
    return np.stack(groups)


def cap_table():
    last, columns = SIDE - 1, []
    columns += [64 if j == 0 else last - (j - 1) for j in range(SIDE)]
    columns += [67 if j == 0 else 32 + j - 1 for j in range(SIDE)]
    columns += [last - j for j in range(SIDE)]
    columns += [32 + j for j in range(SIDE)]
    columns += [65 if j == last else last - (j + 1) for j in range(SIDE)]
    columns += [66 if j == last else 32 + j + 1 for j in range(SIDE)]
    return one_hot(columns, 80)


def dot(a, b):
    return jnp.dot(a, b, preferred_element_type=F32)


def gelu(z):
    return 0.5 * z * (1.0 + jnp.tanh(0.7978845608028654 * (z + 0.044715 * (z * z * z))))


def export(field_ref, strips_ref, send_ref, up_ref, down_ref, pair_ref, picks_ref, corners_ref):
    features = field_ref.shape[-1]
    for tile in range(HERE):
        strips = dot(picks_ref[...], field_ref[tile].reshape(PIXELS, features)).astype(BF16)
        strips_ref[4 * tile : 4 * tile + 4] = strips.reshape(4, SIDE, features)
    address(strips_ref, send_ref, up_ref, down_ref, pair_ref, corners_ref)


def address(strips_ref, send_ref, up_ref, down_ref, pair_ref, corners_ref):
    features = strips_ref.shape[-1]
    corners = dot(corners_ref[...], strips_ref[...].reshape(STRIPS * SIDE, features)).astype(BF16)
    for slot in range(4):
        pair_ref[slot] = strips_ref[send_ref[slot]]
    for slot in range(2):
        up_ref[slot] = strips_ref[send_ref[4 + slot]]
        down_ref[slot] = strips_ref[send_ref[6 + slot]]
    pair_ref[4] = corners
    up_ref[2] = corners
    down_ref[2] = corners


def first_kernel(faces, field_ref, edge_ref, picks_ref, corners_ref, strips_ref, up_ref, down_ref, pair_ref, table_ref, send_ref):
    own = lax.axis_index("face")
    paired, ahead, behind = own ^ 1, lax.rem(own + 2, faces), lax.rem(own + faces - 2, faces)
    for target, start, capacity in ((paired, 0, 4), (ahead, 4, 2), (behind, 6, 2)):
        taken = jnp.int32(0)
        for strip in range(STRIPS):
            wanted = edge_ref[strip % 4, target * HERE + strip // 4]
            fits = jnp.logical_and(wanted // STRIPS == own, taken < capacity)
            send_ref[jnp.where(fits, start + taken, 8)] = wanted % STRIPS
            taken = taken + fits.astype(I32)
    for slot in range(8):
        table_ref[slot] = send_ref[slot]
    export(field_ref, strips_ref, send_ref, up_ref, down_ref, pair_ref, picks_ref, corners_ref)


def side_kernel(faces, edge_ref, corner_ref, conv_ref, table_ref, narrow1_ref, narrow2_ref, wide1_ref, wide2_ref):
    own = lax.axis_index("face")
    paired, ahead, behind = own ^ 1, lax.rem(own + 2, faces), lax.rem(own + faces - 2, faces)
    from_pair, from_behind, from_ahead = jnp.int32(0), jnp.int32(0), jnp.int32(0)
    for strip in range(STRIPS):
        wanted = edge_ref[strip % 4, own * HERE + strip // 4]
        holder, place = wanted // STRIPS, wanted % STRIPS
        by_pair, by_behind, mine = holder == paired, holder == behind, holder == own
        by_ahead = jnp.logical_not(mine | by_pair | by_behind)
        table_ref[strip] = jnp.where(
            mine,
            place,
            jnp.where(
                by_pair,
                STRIPS + jnp.minimum(from_pair, 3),
                jnp.where(
                    by_behind,
                    STRIPS + 4 + jnp.minimum(from_behind, 1),
                    STRIPS + 6 + jnp.minimum(from_ahead, 1),
                ),
            ),
        )
        from_pair = from_pair + by_pair.astype(I32)
        from_behind = from_behind + by_behind.astype(I32)
        from_ahead = from_ahead + by_ahead.astype(I32)
    for corner in range(STRIPS):
        wanted = corner_ref[corner % 4, own * HERE + corner // 4]
        safe = jnp.maximum(wanted, 0)
        holder, place = safe // STRIPS, safe % STRIPS
        source = jnp.where(
            holder == own,
            0,
            jnp.where(
                holder == paired,
                1,
                jnp.where(holder == behind, 2, jnp.where(holder == (behind ^ 1), 3, jnp.where(holder == ahead, 4, 5))),
            ),
        )
        table_ref[STRIPS + corner] = jnp.where(wanted < 0, ZERO_ROW, source * STRIPS + place)
    for conv, (narrow, wide) in enumerate(((narrow1_ref, wide1_ref), (narrow2_ref, wide2_ref))):
        narrow[...] = jnp.zeros_like(narrow)
        wide[...] = jnp.zeros_like(wide)
        for tap in range(9):
            for level in range(2):
                narrow[pl.ds(128 * tap + 64 * level, 64), pl.ds(64 * level, 64)] = conv_ref[0, conv, tap]
            for level in range(4):
                wide[pl.ds(256 * tap + 64 * level, 64), pl.ds(64 * level, 64)] = conv_ref[1, conv, tap]


def gather_rims(strips_ref, behind_ref, ahead_ref, pair_ref, behind2_ref, ahead2_ref, table_ref, held, corners, row, rims):
    features = strips_ref.shape[-1]
    for strip in range(STRIPS):
        held[strip] = strips_ref[strip]
        corners[strip : strip + 1] = strips_ref[strip, 0:1].astype(F32)
    for slot in range(4):
        held[STRIPS + slot] = pair_ref[slot]
    for slot in range(2):
        held[STRIPS + 4 + slot] = behind_ref[slot]
        held[STRIPS + 6 + slot] = ahead_ref[slot]
    for source, ref in enumerate((pair_ref.at[4], behind_ref.at[2], behind2_ref.at[2], ahead_ref.at[2], ahead2_ref.at[2])):
        corners[(source + 1) * STRIPS : (source + 2) * STRIPS] = ref[...].astype(F32)
    corners[ZERO_ROW : ZERO_ROW + 8] = jnp.zeros((8, features), F32)
    row[...] = jnp.zeros_like(row)
    for tile in range(HERE):
        for side in range(4):
            rims[tile, SIDE * side : SIDE * (side + 1)] = held[table_ref[4 * tile + side]]
            pick = table_ref[STRIPS + 4 * tile + side]
            row[tile, side : side + 1] = corners[pl.ds(pick, 1)]
        rims[tile, 64:80] = row[tile].astype(BF16)


def padded(field_ref, tile, rims, shift_ref, cap_ref, shifted):
    features = field_ref.shape[-1]
    rim = rims[tile]
    caps = dot(cap_ref[...], rim).astype(BF16).reshape(6, SIDE, features)
    for b in range(3):
        shifted[b, 0] = caps[2 * b]
        shifted[b, SIDE + 1] = caps[2 * b + 1]
    half = SIDE // 2
    for group in range(2):
        rows = field_ref[tile, half * group : half * (group + 1)]
        shifted[1, 1 + half * group : 1 + half * (group + 1)] = rows
        known = jnp.concatenate([rows.reshape(half * SIDE, features), rim], 0)
        moved = dot(shift_ref[group], known).astype(BF16).reshape(2, half, SIDE, features)
        shifted[0, 1 + half * group : 1 + half * (group + 1)] = moved[0]
        shifted[2, 1 + half * group : 1 + half * (group + 1)] = moved[1]


def windows(shifted, lanes):
    return jnp.concatenate(
        [shifted[b, a : a + SIDE, :, lanes].reshape(PIXELS, -1) for a in range(3) for b in range(3)], 1
    )


def conv_kernel(last, narrow, *refs):
    field_ref, strips_ref, behind_ref, ahead_ref, pair_ref, behind2_ref, ahead2_ref = refs[:7]
    table_ref, send_ref, weight_ref, shift_ref, cap_ref, picks_ref, corners_ref = refs[7:14]
    rest = list(refs[14:])
    state_ref = rest.pop(0) if last else None
    out_ref, out_strips_ref = rest[:2]
    messages, scratch = (rest[2:5], rest[5:]) if not (last and narrow) else ((), rest[2:])
    held, corners, row, rims, shifted = scratch
    features = field_ref.shape[-1]
    gather_rims(strips_ref, behind_ref, ahead_ref, pair_ref, behind2_ref, ahead2_ref, table_ref, held, corners, row, rims)
    width = weight_ref.shape[-1]
    for tile in range(HERE):
        window = shifted.at[tile]
        padded(field_ref, tile, rims, shift_ref, cap_ref, window)
        for group in range(features // width):
            lanes = slice(width * group, width * (group + 1))
            total = dot(windows(window, lanes), weight_ref[...])
            if last:
                total = total + state_ref[tile, :, :, lanes].reshape(PIXELS, width).astype(F32)
            else:
                total = gelu(total)
            out_ref[tile, :, :, lanes] = total.astype(BF16).reshape(SIDE, SIDE, width)
        strips = dot(picks_ref[...], out_ref[tile].reshape(PIXELS, features)).astype(BF16)
        out_strips_ref[4 * tile : 4 * tile + 4] = strips.reshape(4, SIDE, features)
    if messages:
        up_ref, down_ref, to_pair_ref = messages
        address(out_strips_ref, send_ref, up_ref, down_ref, to_pair_ref, corners_ref)


def mix_rows(block, level, parts, mix_in_ref, mix_out_ref, outs):
    levels = mix_in_ref.shape[1] // 128
    order = [lax.rem(level + levels - back, levels) for back in range(levels)]
    first = jnp.concatenate([mix_in_ref[block, pl.ds(pl.multiple_of(128 * place, 128), 128), :] for place in order], 0)
    hidden = gelu(dot(jnp.concatenate(parts, 1), first)).astype(BF16)
    mixed = []
    for back in range(outs):
        columns = pl.ds(pl.multiple_of(128 * order[back], 128), 128)
        mixed.append((parts[back].astype(F32) + dot(hidden, mix_out_ref[block, :, columns])).astype(BF16))
    return mixed


def mix_strips_kernel(block, own_ref, one_ref, two_ref, three_ref, mix_in_ref, mix_out_ref, send_ref, corners_ref, strips_ref, up_ref, down_ref, pair_ref):
    level = lax.axis_index("level")
    parts = [ref[...].reshape(STRIPS * SIDE, 128) for ref in (own_ref, one_ref, two_ref, three_ref)]
    mixed = jnp.concatenate(mix_rows(block, level, parts, mix_in_ref, mix_out_ref, 4), 1)
    strips_ref[...] = mixed.reshape(STRIPS, SIDE, 512)
    address(strips_ref, send_ref, up_ref, down_ref, pair_ref, corners_ref)


def mix_tiles_kernel(block, own_ref, one_ref, two_ref, three_ref, mix_in_ref, mix_out_ref, out_ref):
    level = lax.axis_index("level")
    for tile in range(HERE):
        parts = [ref[tile].reshape(PIXELS, 128) for ref in (own_ref, one_ref, two_ref, three_ref)]
        mixed = mix_rows(block, level, parts, mix_in_ref, mix_out_ref, 4)
        for back in range(4):
            out_ref[tile, :, :, 128 * back : 128 * (back + 1)] = mixed[back].reshape(SIDE, SIDE, 128)


def final_kernel(block, *refs):
    field_ref, strips_ref, behind_ref, ahead_ref, pair_ref, behind2_ref, ahead2_ref = refs[:7]
    table_ref, weight_ref, shift_ref, cap_ref, state_ref, mix_in_ref, mix_out_ref, out_ref = refs[7:15]
    held, corners, row, rims, shifted = refs[15:]
    level = lax.axis_index("level")
    gather_rims(strips_ref, behind_ref, ahead_ref, pair_ref, behind2_ref, ahead2_ref, table_ref, held, corners, row, rims)
    width = weight_ref.shape[-1]
    for tile in range(HERE):
        window = shifted.at[tile]
        padded(field_ref, tile, rims, shift_ref, cap_ref, window)
        parts = []
        for group in range(field_ref.shape[-1] // width):
            lanes = slice(width * group, width * (group + 1))
            total = dot(windows(window, lanes), weight_ref[...])
            total = (total + state_ref[tile, :, :, lanes].reshape(PIXELS, width).astype(F32)).astype(BF16)
            parts += [total[:, 128 * part : 128 * (part + 1)] for part in range(width // 128)]
        (mixed,) = mix_rows(block, level, parts, mix_in_ref, mix_out_ref, 1)
        out_ref[tile] = mixed.reshape(SIDE, SIDE, 128)


V = pl.BlockSpec(memory_space=pltpu.VMEM)
S = pl.BlockSpec(memory_space=pltpu.SMEM)


def call(kernel, name, in_specs, out_specs, out_shape, scratch, args):
    return pl.pallas_call(
        kernel,
        name=name,
        in_specs=in_specs,
        out_specs=out_specs,
        out_shape=out_shape,
        scratch_shapes=scratch,
        compiler_params=pltpu.CompilerParams(vmem_limit_bytes=VMEM_LIMIT),
    )(*args)


def arrays(*shapes):
    return [jax.ShapeDtypeStruct(shape, BF16) for shape in shapes]


def message_shapes(features):
    return (3, SIDE, features), (3, SIDE, features), (5, SIDE, features)


def halo_scratch(features):
    return [
        pltpu.VMEM((STRIPS + 8, SIDE, features), BF16),
        pltpu.VMEM((ZERO_ROW + 8, features), F32),
        pltpu.VMEM((HERE, SIDE, features), F32),
        pltpu.VMEM((HERE, 80, features), BF16),
        pltpu.VMEM((HERE, 3, SIDE + 2, SIDE, features), BF16),
    ]


def exchange(up, down, to_pair):
    faces = lax.axis_size("face")
    pairs = [(i, i ^ 1) for i in range(faces)]
    behind = lax.ppermute(up, "face", [(i, (i + 2) % faces) for i in range(faces)])
    ahead = lax.ppermute(down, "face", [(i, (i - 2) % faces) for i in range(faces)])
    paired = lax.ppermute(to_pair, "face", pairs)
    return behind, ahead, paired, lax.ppermute(behind, "face", pairs), lax.ppermute(ahead, "face", pairs)


def from_level(shard, distance):
    levels = lax.axis_size("level")
    return lax.ppermute(shard, "level", [(i, (i + distance) % levels) for i in range(levels)])


def shards(state, conv_weight, mix_in, mix_out, edge_source, corner_source):
    faces = lax.axis_size("face")
    features = state.shape[-1]
    wide = 4 * features
    picks, corners, shift, cap = (jnp.asarray(t) for t in (strip_table(), corner_table(), shift_table(), cap_table()))
    edges, cornered = edge_source.T, corner_source.T
    tile_shape, wide_shape = (HERE, SIDE, SIDE, features), (HERE, SIDE, SIDE, wide)
    strip_shape, wide_strips = (STRIPS, SIDE, features), (STRIPS, SIDE, wide)

    strips, up, down, to_pair, send = call(
        functools.partial(first_kernel, faces), "first",
        [V, S, V, V], [V, V, V, V, S],
        arrays(strip_shape, *message_shapes(features)) + [jax.ShapeDtypeStruct((8,), I32)],
        [pltpu.SMEM((16,), I32)],
        (state, edges, picks, corners),
    )
    table, narrow1, narrow2, wide1, wide2 = call(
        functools.partial(side_kernel, faces), "side",
        [S, S, V], [S, V, V, V, V],
        [jax.ShapeDtypeStruct((2 * STRIPS,), I32)] + arrays((1152, 128), (1152, 128), (2304, 256), (2304, 256)),
        [],
        (edges, cornered, conv_weight),
    )

    def conv(last, narrow, field, strips, received, weight, residual):
        size = field.shape[-1]
        shapes = [field.shape, (STRIPS, SIDE, size)] + ([] if last and narrow else list(message_shapes(size)))
        return call(
            functools.partial(conv_kernel, last, narrow), f"conv_{size}_{int(last)}",
            [V] * 7 + [S, S] + [V] * 5 + ([V] if last else []), [V] * len(shapes),
            arrays(*shapes), halo_scratch(size),
            (field, strips, *received, table, send, weight, shift, cap, picks, corners) + ((residual,) if last else ()),
        )

    inner, strips, up, down, to_pair = conv(False, True, state, strips, exchange(up, down, to_pair), narrow1, None)
    field, strips = conv(True, True, inner, strips, exchange(up, down, to_pair), narrow2, state)

    others = [from_level(strips, d) for d in (1, 2, 3)]
    tiles = [from_level(field, d) for d in (1, 2, 3)]
    strips, up, down, to_pair = call(
        functools.partial(mix_strips_kernel, 0), "mix_strips",
        [V] * 6 + [S, V], [V] * 4,
        arrays(wide_strips, *message_shapes(wide)), [],
        (strips, *others, mix_in, mix_out, send, corners),
    )
    received = exchange(up, down, to_pair)
    field = call(
        functools.partial(mix_tiles_kernel, 0), "mix_tiles",
        [V] * 6, V, arrays(wide_shape)[0], [],
        (field, *tiles, mix_in, mix_out),
    )
    inner, strips, up, down, to_pair = conv(False, False, field, strips, received, wide1, None)
    return call(
        functools.partial(final_kernel, 1), "final",
        [V] * 7 + [S] + [V] * 6, V, arrays(tile_shape)[0], halo_scratch(wide),
        (inner, strips, *exchange(up, down, to_pair), table, wide2, shift, cap, field, mix_in, mix_out),
    )


def solution(mesh):
    return jax.shard_map(
        shards,
        mesh=mesh,
        in_specs=(P(("ens", "face"), None, None, "level"), P(), P(), P(), P(), P()),
        out_specs=P(("ens", "face"), None, None, "level"),
        check_vma=False,
    )
```

profile of v0, /device:TPU:1, one launch (start us, length us, event | category | flops | bytes accessed | tf_op | source)
XLA Modules:
  0.0 96.4 jit_solution(10568969208094915621)
XLA Ops:
  3.1 1.6 %first.1 = (bf16[16,16,128]{2,1,0:T(8,128)(2,1)S(1)}, bf16[3,16,128]{2,1,0:T(8,128)(2,1)S(1)}, bf16[3,16,128]{2,1,0:T(8,128)(2,1)S(1)}, bf16[5,16,128]{2,1,0:T(8,128)(2,1)S(1)}, s32[8]{0:T(128)S(1)}) custom-call(bf16[4,16,16,128]{3,2,1,0:T(8,128)(2,1)S(1)} %copy-done.4, s32[4,128]{1,0:T(4,128)S(1)} %bitcast.2, bf16[64,256]{1,0:T(8,128)(2,1)S(1)} %copy-done.7, ...), custom_call_target="tpu_custom_call" | custom-call | tf_op jit(solution)/shard_map/first/pallas_call | solution.py:290
  4.8 2.5 %collective-permute-start = (bf16[3,16,128]{2,1,0:T(8,128)(2,1)S(1)}, bf16[3,16,128]{2,1,0:T(8,128)(2,1)S(1)}, u32[]{:S(2)}, u32[]{:S(2)}) collective-permute-start(bf16[3,16,128]{2,1,0:T(8,128)(2,1)S(1)} %get-tuple-element.32), channel_id=1, source_target_pairs={{0,16},{8,24},{16,32},{24,40},{32,48},{40,56},{48,64},{56,72},{64,... | collective-permute-start | bytes 36872 | tf_op jit(solution)/shard_map/ppermute | solution.py:322
  7.3 6.7 %collective-permute-start.1 = (bf16[3,16,128]{2,1,0:T(8,128)(2,1)S(1)}, bf16[3,16,128]{2,1,0:T(8,128)(2,1)S(1)}, u32[]{:S(2)}, u32[]{:S(2)}) collective-permute-start(bf16[3,16,128]{2,1,0:T(8,128)(2,1)S(1)} %get-tuple-element.33), channel_id=1, source_target_pairs={{0,240},{8,248},{16,0},{24,8},{32,16},{40,24},{48,32},{56,40},{64,... | collective-permute-start | bytes 36872 | tf_op jit(solution)/shard_map/ppermute | solution.py:323
  15.0 1.5 %collective-permute-start.3 = (bf16[3,16,128]{2,1,0:T(8,128)(2,1)S(1)}, bf16[3,16,128]{2,1,0:T(8,128)(2,1)S(1)}, u32[]{:S(2)}, u32[]{:S(2)}) collective-permute-start(bf16[3,16,128]{2,1,0:T(8,128)(2,1)S(1)} %collective-permute-done.refs_2_), channel_id=1, source_target_pairs={{0,8},{8,0},{16,24},{24,16},{32,40},{40,32},{48,56},{56,48},{64,72... | collective-permute-start | bytes 36872 | tf_op jit(solution)/shard_map/ppermute | solution.py:325
  18.9 2.2 %side.1 = (s32[32]{0:T(128)S(1)}, bf16[1152,128]{1,0:T(8,128)(2,1)S(1)}, bf16[1152,128]{1,0:T(8,128)(2,1)S(1)}, bf16[2304,256]{1,0:T(8,128)(2,1)S(1)}, bf16[2304,256]{1,0:T(8,128)(2,1)S(1)}) custom-call(s32[4,128]{1,0:T(4,128)S(1)} %bitcast.3, s32[4,128]{1,0:T(4,128)S(1)} %bitcast.4, bf16[2,2,9,64,64]{4,3,2,1,0:T(8,128)(2,1)S(1)} %copy-done.6), custom_call_target="tpu_custom_call" | custom-call | tf_op jit(solution)/shard_map/side/pallas_call | solution.py:290
  21.2 1.1 %copy-done.2 = bf16[2,256,208]{2,1,0:T(8,128)(2,1)S(1)} copy-done((bf16[2,256,208]{2,1,0:T(8,128)(2,1)S(1)}, bf16[2,256,208]{2,1,0:T(8,128)(2,1)}, u32[]{:S(2)}) %copy-start.2) | copy-done | bytes 213016
  25.4 2.9 %conv_128_0.1 = (bf16[4,16,16,128]{3,2,1,0:T(8,128)(2,1)S(1)}, bf16[16,16,128]{2,1,0:T(8,128)(2,1)S(1)}, bf16[3,16,128]{2,1,0:T(8,128)(2,1)S(1)}, bf16[3,16,128]{2,1,0:T(8,128)(2,1)S(1)}, bf16[5,16,128]{2,1,0:T(8,128)(2,1)S(1)}) custom-call(bf16[4,16,16,128]{3,2,1,0:T(8,128)(2,1)S(1)} %copy-done.5, bf16[16,16,128]{2,1,0:T(8,128)(2,1)S(1)} %get-tuple-element.31.refs_1_, ...), custom_call_target="tpu_custom_call" | custom-call | tf_op jit(solution)/shard_map/conv_128_0/pallas_call | solution.py:290
  28.3 5.5 %collective-permute-start.6 = (bf16[3,16,128]{2,1,0:T(8,128)(2,1)S(1)}, bf16[3,16,128]{2,1,0:T(8,128)(2,1)S(1)}, u32[]{:S(2)}, u32[]{:S(2)}) collective-permute-start(bf16[3,16,128]{2,1,0:T(8,128)(2,1)S(1)} %get-tuple-element.41), channel_id=1, source_target_pairs={{0,240},{8,248},{16,0},{24,8},{32,16},{40,24},{48,32},{56,40},{64,... | collective-permute-start | bytes 36872 | tf_op jit(solution)/shard_map/ppermute | solution.py:323
  34.8 1.3 %collective-permute-start.8 = (bf16[3,16,128]{2,1,0:T(8,128)(2,1)S(1)}, bf16[3,16,128]{2,1,0:T(8,128)(2,1)S(1)}, u32[]{:S(2)}, u32[]{:S(2)}) collective-permute-start(bf16[3,16,128]{2,1,0:T(8,128)(2,1)S(1)} %collective-permute-done.5.refs_2_), channel_id=1, source_target_pairs={{0,8},{8,0},{16,24},{24,16},{32,40},{40,32},{48,56},{56,48},{64,72... | collective-permute-start | bytes 36872 | tf_op jit(solution)/shard_map/ppermute | solution.py:325
  37.3 2.6 %conv_128_1.1 = (bf16[4,16,16,128]{3,2,1,0:T(8,128)(2,1)S(1)}, bf16[16,16,128]{2,1,0:T(8,128)(2,1)S(1)}) custom-call(bf16[4,16,16,128]{3,2,1,0:T(8,128)(2,1)S(1)} %get-tuple-element.38.refs_0_, bf16[16,16,128]{2,1,0:T(8,128)(2,1)S(1)} %get-tuple-element.39.refs_1_, bf16[3,16,128]{2,1,0:T(8,128)(2,1)S(1)} %collective-permute-done.5.refs_2_, ...), custom_call_target="tpu_custom_call" | custom-call | tf_op jit(solution)/shard_map/conv_128_1/pallas_call | solution.py:290
  39.9 2.6 %collective-permute-start.12 = (bf16[4,16,16,128]{3,2,1,0:T(8,128)(2,1)S(1)}, bf16[4,16,16,128]{3,2,1,0:T(8,128)(2,1)S(1)}, u32[]{:S(2)}, u32[]{:S(2)}) collective-permute-start(bf16[4,16,16,128]{3,2,1,0:T(8,128)(2,1)S(1)} %get-tuple-element.44.own_ref), channel_id=1, source_target_pairs={{0,6},{2,0},{4,2},{6,4},{1,7},{3,1},{5,3},{7,5},{8,14},{10,8},{12,... | collective-permute-start | bytes 786440 | tf_op jit(solution)/shard_map/ppermute | solution.py:330
  44.0 3.6 %collective-permute-start.14 = (bf16[16,16,128]{2,1,0:T(8,128)(2,1)S(1)}, bf16[16,16,128]{2,1,0:T(8,128)(2,1)S(1)}, u32[]{:S(2)}, u32[]{:S(2)}) collective-permute-start(bf16[16,16,128]{2,1,0:T(8,128)(2,1)S(1)} %get-tuple-element.45.own_ref), channel_id=1, source_target_pairs={{0,4},{2,6},{4,0},{6,2},{1,5},{3,7},{5,1},{7,3},{8,12},{10,14},{12... | collective-permute-start | bytes 196616 | tf_op jit(solution)/shard_map/ppermute | solution.py:330
  47.5 8.8 %collective-permute-done.15.three_ref = bf16[16,16,128]{2,1,0:T(8,128)(2,1)S(1)} collective-permute-done((bf16[16,16,128]{2,1,0:T(8,128)(2,1)S(1)}, bf16[16,16,128]{2,1,0:T(8,128)(2,1)S(1)}, u32[]{:S(2)}, u32[]{:S(2)}) %collective-permute-start.15) | collective-permute-done | bytes 65568 | tf_op jit(solution)/shard_map/ppermute | solution.py:330
  56.3 2.1 %collective-permute-done.14.two_ref = bf16[16,16,128]{2,1,0:T(8,128)(2,1)S(1)} collective-permute-done((bf16[16,16,128]{2,1,0:T(8,128)(2,1)S(1)}, bf16[16,16,128]{2,1,0:T(8,128)(2,1)S(1)}, u32[]{:S(2)}, u32[]{:S(2)}) %collective-permute-start.14) | collective-permute-done | bytes 65568 | tf_op jit(solution)/shard_map/ppermute | solution.py:330
  58.4 3.1 %collective-permute-done.13.one_ref = bf16[16,16,128]{2,1,0:T(8,128)(2,1)S(1)} collective-permute-done((bf16[16,16,128]{2,1,0:T(8,128)(2,1)S(1)}, bf16[16,16,128]{2,1,0:T(8,128)(2,1)S(1)}, u32[]{:S(2)}, u32[]{:S(2)}) %collective-permute-start.13) | collective-permute-done | bytes 65568 | tf_op jit(solution)/shard_map/ppermute | solution.py:330
  61.5 1.4 %mix_strips.1 = (bf16[16,16,512]{2,1,0:T(8,128)(2,1)S(1)}, bf16[3,16,512]{2,1,0:T(8,128)(2,1)S(1)}, bf16[3,16,512]{2,1,0:T(8,128)(2,1)S(1)}, bf16[5,16,512]{2,1,0:T(8,128)(2,1)S(1)}) custom-call(bf16[16,16,128]{2,1,0:T(8,128)(2,1)S(1)} %get-tuple-element.45.own_ref, bf16[16,16,128]{2,1,0:T(8,128)(2,1)S(1)} %collective-permute-done.13.one_ref, ...), custom_call_target="tpu_custom_call" | custom-call | tf_op jit(solution)/shard_map/mix_strips/pallas_call | solution.py:290
  63.0 5.1 %collective-permute-start.17 = (bf16[3,16,512]{2,1,0:T(8,128)(2,1)S(1)}, bf16[3,16,512]{2,1,0:T(8,128)(2,1)S(1)}, u32[]{:S(2)}, u32[]{:S(2)}) collective-permute-start(bf16[3,16,512]{2,1,0:T(8,128)(2,1)S(1)} %get-tuple-element.48), channel_id=1, source_target_pairs={{0,240},{8,248},{16,0},{24,8},{32,16},{40,24},{48,32},{56,40},{64,... | collective-permute-start | bytes 147464 | tf_op jit(solution)/shard_map/ppermute | solution.py:323
  68.0 1.5 %collective-permute-done.16.refs_2_ = bf16[3,16,512]{2,1,0:T(8,128)(2,1)S(1)} collective-permute-done((bf16[3,16,512]{2,1,0:T(8,128)(2,1)S(1)}, bf16[3,16,512]{2,1,0:T(8,128)(2,1)S(1)}, u32[]{:S(2)}, u32[]{:S(2)}) %collective-permute-start.16) | collective-permute-done | bytes 49184 | tf_op jit(solution)/shard_map/ppermute | solution.py:322
  69.5 3.0 %collective-permute-start.18 = (bf16[5,16,512]{2,1,0:T(8,128)(2,1)S(1)}, bf16[5,16,512]{2,1,0:T(8,128)(2,1)S(1)}, u32[]{:S(2)}, u32[]{:S(2)}) collective-permute-start(bf16[5,16,512]{2,1,0:T(8,128)(2,1)S(1)} %get-tuple-element.49), channel_id=1, source_target_pairs={{0,8},{8,0},{16,24},{24,16},{32,40},{40,32},{48,56},{56,48},{64,72... | collective-permute-start | bytes 245768 | tf_op jit(solution)/shard_map/ppermute | solution.py:324
  73.0 2.5 %mix_tiles.1.refs_0_.refs_11_ = bf16[4,16,16,512]{3,2,1,0:T(8,128)(2,1)S(1)} custom-call(bf16[4,16,16,128]{3,2,1,0:T(8,128)(2,1)S(1)} %get-tuple-element.44.own_ref, bf16[4,16,16,128]{3,2,1,0:T(8,128)(2,1)S(1)} %collective-permute-done.10.one_ref, bf16[4,16,16,128]{3,2,1,0:T(8,128)(2,1)S(1)} %collective-permute-done.11.two_ref, ...), custom_call_target="tpu_custom_call" | custom-call | tf_op jit(solution)/shard_map/mix_tiles/pallas_call | solution.py:290
  75.5 5.1 %conv_512_0.1 = (bf16[4,16,16,512]{3,2,1,0:T(8,128)(2,1)S(1)}, bf16[16,16,512]{2,1,0:T(8,128)(2,1)S(1)}, bf16[3,16,512]{2,1,0:T(8,128)(2,1)S(1)}, bf16[3,16,512]{2,1,0:T(8,128)(2,1)S(1)}, bf16[5,16,512]{2,1,0:T(8,128)(2,1)S(1)}) custom-call(bf16[4,16,16,512]{3,2,1,0:T(8,128)(2,1)S(1)} %mix_tiles.1.refs_0_.refs_11_, ...), custom_call_target="tpu_custom_call" | custom-call | tf_op jit(solution)/shard_map/conv_512_0/pallas_call | solution.py:290
  80.6 5.1 %collective-permute-start.22 = (bf16[3,16,512]{2,1,0:T(8,128)(2,1)S(1)}, bf16[3,16,512]{2,1,0:T(8,128)(2,1)S(1)}, u32[]{:S(2)}, u32[]{:S(2)}) collective-permute-start(bf16[3,16,512]{2,1,0:T(8,128)(2,1)S(1)} %get-tuple-element.54), channel_id=1, source_target_pairs={{0,240},{8,248},{16,0},{24,8},{32,16},{40,24},{48,32},{56,40},{64,... | collective-permute-start | bytes 147464 | tf_op jit(solution)/shard_map/ppermute | solution.py:323
  87.2 1.5 %collective-permute-start.24 = (bf16[3,16,512]{2,1,0:T(8,128)(2,1)S(1)}, bf16[3,16,512]{2,1,0:T(8,128)(2,1)S(1)}, u32[]{:S(2)}, u32[]{:S(2)}) collective-permute-start(bf16[3,16,512]{2,1,0:T(8,128)(2,1)S(1)} %collective-permute-done.21.refs_2_), channel_id=1, source_target_pairs={{0,8},{8,0},{16,24},{24,16},{32,40},{40,32},{48,56},{56,48},{64,72... | collective-permute-start | bytes 147464 | tf_op jit(solution)/shard_map/ppermute | solution.py:325
  89.9 6.5 %final.1 = bf16[4,16,16,128]{3,2,1,0:T(8,128)(2,1)} custom-call(bf16[4,16,16,512]{3,2,1,0:T(8,128)(2,1)S(1)} %get-tuple-element.51.refs_0_, bf16[16,16,512]{2,1,0:T(8,128)(2,1)S(1)} %get-tuple-element.52.refs_1_, bf16[3,16,512]{2,1,0:T(8,128)(2,1)S(1)} %collective-permute-done.21.refs_2_, bf16[3,16,512]{2,1,0:T(8,128)(2,1)S(1)} %collective-permute-done.22.refs_3_, ...), custom_call_target="tpu_custom_call" | custom-call | tf_op jit(solution)/shard_map/final/pallas_call | solution.py:290
  (70 shorter events, 16.7 us)
Async XLA Ops:
  4.8 10.2 %collective-permute-start = (bf16[3,16,128]{2,1,0:T(8,128)(2,1)S(1)}, bf16[3,16,128]{2,1,0:T(8,128)(2,1)S(1)}, u32[]{:S(2)}, u32[]{:S(2)}) collective-permute-start(bf16[3,16,128]{2,1,0:T(8,128)(2,1)S(1)} %get-tuple-element.32), channel_id=1, source_target_pairs={{0,16},{8,24},{16,32},{24,40},{32,48},{40,56},{48,64},{56,72},{64,... | collective-permute-start | bytes 36872 | tf_op jit(solution)/shard_map/ppermute | solution.py:322
  7.3 9.2 %collective-permute-start.1 = (bf16[3,16,128]{2,1,0:T(8,128)(2,1)S(1)}, bf16[3,16,128]{2,1,0:T(8,128)(2,1)S(1)}, u32[]{:S(2)}, u32[]{:S(2)}) collective-permute-start(bf16[3,16,128]{2,1,0:T(8,128)(2,1)S(1)} %get-tuple-element.33), channel_id=1, source_target_pairs={{0,240},{8,248},{16,0},{24,8},{32,16},{40,24},{48,32},{56,40},{64,... | collective-permute-start | bytes 36872 | tf_op jit(solution)/shard_map/ppermute | solution.py:323
  14.0 7.2 %collective-permute-start.2 = (bf16[5,16,128]{2,1,0:T(8,128)(2,1)S(1)}, bf16[5,16,128]{2,1,0:T(8,128)(2,1)S(1)}, u32[]{:S(2)}, u32[]{:S(2)}) collective-permute-start(bf16[5,16,128]{2,1,0:T(8,128)(2,1)S(1)} %get-tuple-element.34), channel_id=1, source_target_pairs={{0,8},{8,0},{16,24},{24,16},{32,40},{40,32},{48,56},{56,48},{64,72... | collective-permute-start | bytes 61448 | tf_op jit(solution)/shard_map/ppermute | solution.py:324
  15.0 6.2 %collective-permute-start.3 = (bf16[3,16,128]{2,1,0:T(8,128)(2,1)S(1)}, bf16[3,16,128]{2,1,0:T(8,128)(2,1)S(1)}, u32[]{:S(2)}, u32[]{:S(2)}) collective-permute-start(bf16[3,16,128]{2,1,0:T(8,128)(2,1)S(1)} %collective-permute-done.refs_2_), channel_id=1, source_target_pairs={{0,8},{8,0},{16,24},{24,16},{32,40},{40,32},{48,56},{56,48},{64,72... | collective-permute-start | bytes 36872 | tf_op jit(solution)/shard_map/ppermute | solution.py:325
  16.5 4.7 %collective-permute-start.4 = (bf16[3,16,128]{2,1,0:T(8,128)(2,1)S(1)}, bf16[3,16,128]{2,1,0:T(8,128)(2,1)S(1)}, u32[]{:S(2)}, u32[]{:S(2)}) collective-permute-start(bf16[3,16,128]{2,1,0:T(8,128)(2,1)S(1)} %collective-permute-done.1.refs_3_), channel_id=1, source_target_pairs={{0,8},{8,0},{16,24},{24,16},{32,40},{40,32},{48,56},{56,48},{64,72... | collective-permute-start | bytes 36872 | tf_op jit(solution)/shard_map/ppermute | solution.py:325
  28.3 6.5 %collective-permute-start.5 = (bf16[3,16,128]{2,1,0:T(8,128)(2,1)S(1)}, bf16[3,16,128]{2,1,0:T(8,128)(2,1)S(1)}, u32[]{:S(2)}, u32[]{:S(2)}) collective-permute-start(bf16[3,16,128]{2,1,0:T(8,128)(2,1)S(1)} %get-tuple-element.40), channel_id=1, source_target_pairs={{0,16},{8,24},{16,32},{24,40},{32,48},{40,56},{48,64},{56,72},{64,... | collective-permute-start | bytes 36872 | tf_op jit(solution)/shard_map/ppermute | solution.py:322
  28.3 7.8 %collective-permute-start.6 = (bf16[3,16,128]{2,1,0:T(8,128)(2,1)S(1)}, bf16[3,16,128]{2,1,0:T(8,128)(2,1)S(1)}, u32[]{:S(2)}, u32[]{:S(2)}) collective-permute-start(bf16[3,16,128]{2,1,0:T(8,128)(2,1)S(1)} %get-tuple-element.41), channel_id=1, source_target_pairs={{0,240},{8,248},{16,0},{24,8},{32,16},{40,24},{48,32},{56,40},{64,... | collective-permute-start | bytes 36872 | tf_op jit(solution)/shard_map/ppermute | solution.py:323
  33.8 2.3 %collective-permute-start.7 = (bf16[5,16,128]{2,1,0:T(8,128)(2,1)S(1)}, bf16[5,16,128]{2,1,0:T(8,128)(2,1)S(1)}, u32[]{:S(2)}, u32[]{:S(2)}) collective-permute-start(bf16[5,16,128]{2,1,0:T(8,128)(2,1)S(1)} %get-tuple-element.42), channel_id=1, source_target_pairs={{0,8},{8,0},{16,24},{24,16},{32,40},{40,32},{48,56},{56,48},{64,72... | collective-permute-start | bytes 61448 | tf_op jit(solution)/shard_map/ppermute | solution.py:324
  34.8 2.1 %collective-permute-start.8 = (bf16[3,16,128]{2,1,0:T(8,128)(2,1)S(1)}, bf16[3,16,128]{2,1,0:T(8,128)(2,1)S(1)}, u32[]{:S(2)}, u32[]{:S(2)}) collective-permute-start(bf16[3,16,128]{2,1,0:T(8,128)(2,1)S(1)} %collective-permute-done.5.refs_2_), channel_id=1, source_target_pairs={{0,8},{8,0},{16,24},{24,16},{32,40},{40,32},{48,56},{56,48},{64,72... | collective-permute-start | bytes 36872 | tf_op jit(solution)/shard_map/ppermute | solution.py:325
  39.9 32.7 %collective-permute-start.12 = (bf16[4,16,16,128]{3,2,1,0:T(8,128)(2,1)S(1)}, bf16[4,16,16,128]{3,2,1,0:T(8,128)(2,1)S(1)}, u32[]{:S(2)}, u32[]{:S(2)}) collective-permute-start(bf16[4,16,16,128]{3,2,1,0:T(8,128)(2,1)S(1)} %get-tuple-element.44.own_ref), channel_id=1, source_target_pairs={{0,6},{2,0},{4,2},{6,4},{1,7},{3,1},{5,3},{7,5},{8,14},{10,8},{12,... | collective-permute-start | bytes 786440 | tf_op jit(solution)/shard_map/ppermute | solution.py:330
  42.5 13.8 %collective-permute-start.15 = (bf16[16,16,128]{2,1,0:T(8,128)(2,1)S(1)}, bf16[16,16,128]{2,1,0:T(8,128)(2,1)S(1)}, u32[]{:S(2)}, u32[]{:S(2)}) collective-permute-start(bf16[16,16,128]{2,1,0:T(8,128)(2,1)S(1)} %get-tuple-element.45.own_ref), channel_id=1, source_target_pairs={{0,6},{2,0},{4,2},{6,4},{1,7},{3,1},{5,3},{7,5},{8,14},{10,8},{12,... | collective-permute-start | bytes 196616 | tf_op jit(solution)/shard_map/ppermute | solution.py:330
  43.0 30.0 %collective-permute-start.11 = (bf16[4,16,16,128]{3,2,1,0:T(8,128)(2,1)S(1)}, bf16[4,16,16,128]{3,2,1,0:T(8,128)(2,1)S(1)}, u32[]{:S(2)}, u32[]{:S(2)}) collective-permute-start(bf16[4,16,16,128]{3,2,1,0:T(8,128)(2,1)S(1)} %get-tuple-element.44.own_ref), channel_id=1, source_target_pairs={{0,4},{2,6},{4,0},{6,2},{1,5},{3,7},{5,1},{7,3},{8,12},{10,14},{12... | collective-permute-start | bytes 786440 | tf_op jit(solution)/shard_map/ppermute | solution.py:330
  43.3 29.7 %collective-permute-start.10 = (bf16[4,16,16,128]{3,2,1,0:T(8,128)(2,1)S(1)}, bf16[4,16,16,128]{3,2,1,0:T(8,128)(2,1)S(1)}, u32[]{:S(2)}, u32[]{:S(2)}) collective-permute-start(bf16[4,16,16,128]{3,2,1,0:T(8,128)(2,1)S(1)} %get-tuple-element.44.own_ref), channel_id=1, source_target_pairs={{0,2},{2,4},{4,6},{6,0},{1,3},{3,5},{5,7},{7,1},{8,10},{10,12},{12... | collective-permute-start | bytes 786440 | tf_op jit(solution)/shard_map/ppermute | solution.py:330
  44.0 14.5 %collective-permute-start.14 = (bf16[16,16,128]{2,1,0:T(8,128)(2,1)S(1)}, bf16[16,16,128]{2,1,0:T(8,128)(2,1)S(1)}, u32[]{:S(2)}, u32[]{:S(2)}) collective-permute-start(bf16[16,16,128]{2,1,0:T(8,128)(2,1)S(1)} %get-tuple-element.45.own_ref), channel_id=1, source_target_pairs={{0,4},{2,6},{4,0},{6,2},{1,5},{3,7},{5,1},{7,3},{8,12},{10,14},{12... | collective-permute-start | bytes 196616 | tf_op jit(solution)/shard_map/ppermute | solution.py:330
  56.3 5.2 %collective-permute-start.13 = (bf16[16,16,128]{2,1,0:T(8,128)(2,1)S(1)}, bf16[16,16,128]{2,1,0:T(8,128)(2,1)S(1)}, u32[]{:S(2)}, u32[]{:S(2)}) collective-permute-start(bf16[16,16,128]{2,1,0:T(8,128)(2,1)S(1)} %get-tuple-element.45.own_ref), channel_id=1, source_target_pairs={{0,2},{2,4},{4,6},{6,0},{1,3},{3,5},{5,7},{7,1},{8,10},{10,12},{12... | collective-permute-start | bytes 196616 | tf_op jit(solution)/shard_map/ppermute | solution.py:330
  63.0 6.6 %collective-permute-start.16 = (bf16[3,16,512]{2,1,0:T(8,128)(2,1)S(1)}, bf16[3,16,512]{2,1,0:T(8,128)(2,1)S(1)}, u32[]{:S(2)}, u32[]{:S(2)}) collective-permute-start(bf16[3,16,512]{2,1,0:T(8,128)(2,1)S(1)} %get-tuple-element.47), channel_id=1, source_target_pairs={{0,16},{8,24},{16,32},{24,40},{32,48},{40,56},{48,64},{56,72},{64,... | collective-permute-start | bytes 147464 | tf_op jit(solution)/shard_map/ppermute | solution.py:322
  63.0 9.5 %collective-permute-start.17 = (bf16[3,16,512]{2,1,0:T(8,128)(2,1)S(1)}, bf16[3,16,512]{2,1,0:T(8,128)(2,1)S(1)}, u32[]{:S(2)}, u32[]{:S(2)}) collective-permute-start(bf16[3,16,512]{2,1,0:T(8,128)(2,1)S(1)} %get-tuple-element.48), channel_id=1, source_target_pairs={{0,240},{8,248},{16,0},{24,8},{32,16},{40,24},{48,32},{56,40},{64,... | collective-permute-start | bytes 147464 | tf_op jit(solution)/shard_map/ppermute | solution.py:323
  69.5 6.0 %collective-permute-start.18 = (bf16[5,16,512]{2,1,0:T(8,128)(2,1)S(1)}, bf16[5,16,512]{2,1,0:T(8,128)(2,1)S(1)}, u32[]{:S(2)}, u32[]{:S(2)}) collective-permute-start(bf16[5,16,512]{2,1,0:T(8,128)(2,1)S(1)} %get-tuple-element.49), channel_id=1, source_target_pairs={{0,8},{8,0},{16,24},{24,16},{32,40},{40,32},{48,56},{56,48},{64,72... | collective-permute-start | bytes 245768 | tf_op jit(solution)/shard_map/ppermute | solution.py:324
  72.5 3.0 %collective-permute-start.19 = (bf16[3,16,512]{2,1,0:T(8,128)(2,1)S(1)}, bf16[3,16,512]{2,1,0:T(8,128)(2,1)S(1)}, u32[]{:S(2)}, u32[]{:S(2)}) collective-permute-start(bf16[3,16,512]{2,1,0:T(8,128)(2,1)S(1)} %collective-permute-done.16.refs_2_), channel_id=1, source_target_pairs={{0,8},{8,0},{16,24},{24,16},{32,40},{40,32},{48,56},{56,48},{64,72... | collective-permute-start | bytes 147464 | tf_op jit(solution)/shard_map/ppermute | solution.py:325
  72.6 2.9 %collective-permute-start.20 = (bf16[3,16,512]{2,1,0:T(8,128)(2,1)S(1)}, bf16[3,16,512]{2,1,0:T(8,128)(2,1)S(1)}, u32[]{:S(2)}, u32[]{:S(2)}) collective-permute-start(bf16[3,16,512]{2,1,0:T(8,128)(2,1)S(1)} %collective-permute-done.17.refs_3_), channel_id=1, source_target_pairs={{0,8},{8,0},{16,24},{24,16},{32,40},{40,32},{48,56},{56,48},{64,72... | collective-permute-start | bytes 147464 | tf_op jit(solution)/shard_map/ppermute | solution.py:325
  80.6 6.6 %collective-permute-start.21 = (bf16[3,16,512]{2,1,0:T(8,128)(2,1)S(1)}, bf16[3,16,512]{2,1,0:T(8,128)(2,1)S(1)}, u32[]{:S(2)}, u32[]{:S(2)}) collective-permute-start(bf16[3,16,512]{2,1,0:T(8,128)(2,1)S(1)} %get-tuple-element.53), channel_id=1, source_target_pairs={{0,16},{8,24},{16,32},{24,40},{32,48},{40,56},{48,64},{56,72},{64,... | collective-permute-start | bytes 147464 | tf_op jit(solution)/shard_map/ppermute | solution.py:322
  80.6 8.0 %collective-permute-start.22 = (bf16[3,16,512]{2,1,0:T(8,128)(2,1)S(1)}, bf16[3,16,512]{2,1,0:T(8,128)(2,1)S(1)}, u32[]{:S(2)}, u32[]{:S(2)}) collective-permute-start(bf16[3,16,512]{2,1,0:T(8,128)(2,1)S(1)} %get-tuple-element.54), channel_id=1, source_target_pairs={{0,240},{8,248},{16,0},{24,8},{32,16},{40,24},{48,32},{56,40},{64,... | collective-permute-start | bytes 147464 | tf_op jit(solution)/shard_map/ppermute | solution.py:323
  85.7 2.9 %collective-permute-start.23 = (bf16[5,16,512]{2,1,0:T(8,128)(2,1)S(1)}, bf16[5,16,512]{2,1,0:T(8,128)(2,1)S(1)}, u32[]{:S(2)}, u32[]{:S(2)}) collective-permute-start(bf16[5,16,512]{2,1,0:T(8,128)(2,1)S(1)} %get-tuple-element.55), channel_id=1, source_target_pairs={{0,8},{8,0},{16,24},{24,16},{32,40},{40,32},{48,56},{56,48},{64,72... | collective-permute-start | bytes 245768 | tf_op jit(solution)/shard_map/ppermute | solution.py:324
  87.2 2.3 %collective-permute-start.24 = (bf16[3,16,512]{2,1,0:T(8,128)(2,1)S(1)}, bf16[3,16,512]{2,1,0:T(8,128)(2,1)S(1)}, u32[]{:S(2)}, u32[]{:S(2)}) collective-permute-start(bf16[3,16,512]{2,1,0:T(8,128)(2,1)S(1)} %collective-permute-done.21.refs_2_), channel_id=1, source_target_pairs={{0,8},{8,0},{16,24},{24,16},{32,40},{40,32},{48,56},{56,48},{64,72... | collective-permute-start | bytes 147464 | tf_op jit(solution)/shard_map/ppermute | solution.py:325
  (19 other events, 170.5 us)
where the time goes:
time: 96.9 us; the launch traced here: 96.4 us
  starting transfers between devices  42.8 us (44%)
  Pallas kernels  24.7 us (25%)
  waiting for transfers between devices  18.9 us (20%)
  local copies, waits for them, and re-layouts  9.8 us (10%)
    pallas_call x8, Pallas kernels, call(): pl.pallas_call(kernel, name=name, in_specs=in_specs, out_specs=out_specs,...  24.7 us
    ppermute x4, starting transfers between devices, exchange(): lax.ppermute(down, 'face', [(i, (i - 2) % faces) for i in range(faces)])  22.3 us
    ppermute x6, waiting for transfers between devices, from_level(): lax.ppermute(shard, 'level', [(i, (i + distance) % levels) for i in range...  14 us
    unnamed x34, local copies, waits for them, and re-layouts  9.8 us
    ppermute x6, starting transfers between devices, from_level(): lax.ppermute(shard, 'level', [(i, (i + distance) % levels) for i in range...  7.6 us
    ppermute x4, starting transfers between devices, exchange(): paired = lax.ppermute(to_pair, 'face', pairs)  5.46 us
    ppermute x4, starting transfers between devices, exchange(): lax.ppermute(behind, 'face', pairs)  4.39 us
    ppermute x4, starting transfers between devices, exchange(): lax.ppermute(up, 'face', [(i, (i + 2) % faces) for i in range(faces)])  2.57 us
  transfers between devices with their start and end apart: 26, of which 10 were waited for; matrix products, arithmetic and copies ran while one was open for 0% of the time, Pallas kernels for 6%

commit v1 on v0

v1 whole, which is shorter than its diff:
```python
import functools

import jax
import jax.numpy as jnp
import numpy as np
from jax import lax
from jax.experimental import pallas as pl
from jax.experimental.pallas import tpu as pltpu
from jax.sharding import PartitionSpec as P

BF16, F32, I32 = jnp.bfloat16, jnp.float32, jnp.int32
SIDE = 16
INNER = SIDE - 2
PIXELS = SIDE * SIDE
HERE = 4
STRIPS = 4 * HERE
BORDER = 4 * SIDE
ZERO_ROW = 6 * STRIPS
VMEM_LIMIT = 16 * 1024 * 1024


def one_hot(columns, width):
    table = np.zeros((len(columns), width), np.float32)
    for row, column in enumerate(columns):
        if column is not None:
            table[row, column] = 1.0
    return table.astype(jnp.bfloat16)


def strip_pixel(side, k, depth=0):
    last = SIDE - 1
    return ((depth, k), (k, last - depth), (last - depth, last - k), (last - k, depth))[side]


def ring(depth):
    places = {}
    for side in range(4):
        for k in range(depth, SIDE - depth):
            places.setdefault(strip_pixel(side, k, depth), SIDE * side + k)
    return places


def border_table():
    outer, inner, last = ring(0), ring(1), SIDE - 1
    corner = {(-1, -1): 0, (-1, SIDE): 1, (SIDE, SIDE): 2, (SIDE, -1): 3}
    columns = []
    for a in range(3):
        for b in range(3):
            for side in range(4):
                for k in range(SIDE):
                    i, j = strip_pixel(side, k)
                    i, j = i + a - 1, j + b - 1
                    if (i, j) in corner:
                        columns.append(3 * BORDER + corner[i, j])
                    elif i < 0:
                        columns.append(2 * BORDER + last - j)
                    elif j > last:
                        columns.append(2 * BORDER + SIDE + last - i)
                    elif i > last:
                        columns.append(2 * BORDER + 2 * SIDE + j)
                    elif j < 0:
                        columns.append(2 * BORDER + 3 * SIDE + i)
                    elif (i, j) in outer:
                        columns.append(outer[i, j])
                    else:
                        columns.append(BORDER + inner[i, j])
    return one_hot(columns, 3 * BORDER + SIDE)


def tile_table():
    outer, half = ring(0), INNER // 2
    groups = []
    for group in range(2):
        columns = []
        for b in range(3):
            for i in range(SIDE // 2 * group, SIDE // 2 * (group + 1)):
                for j in range(SIDE):
                    column = j + b - 1
                    if column < 0 or column >= SIDE:
                        columns.append(None)
                    elif (i, column) in outer:
                        columns.append(half * SIDE + outer[i, column])
                    else:
                        columns.append((i - 1 - half * group) * SIDE + column)
        groups.append(one_hot(columns, half * SIDE + BORDER))
    return np.stack(groups)


def inner_table():
    columns = []
    for side in range(4):
        for k in range(SIDE):
            i, j = strip_pixel(side, k, 1)
            columns.append((i - 1) * SIDE + j if 1 <= k < SIDE - 1 else None)
    return one_hot(columns, INNER * SIDE)


def dot(a, b):
    return jnp.dot(a, b, preferred_element_type=F32)


def gelu(z):
    return 0.5 * z * (1.0 + jnp.tanh(0.7978845608028654 * (z + 0.044715 * (z * z * z))))


def copies(sems, *pairs):
    started = [pltpu.make_async_copy(source, target, sems.at[n]) for n, (source, target) in enumerate(pairs)]
    for copy in started:
        copy.start()
    return started


def address(strips_ref, send_ref, near_ref, far_ref, pair_ref, corners_ref):
    features = strips_ref.shape[-1]
    corners = dot(corners_ref[...], strips_ref[...].reshape(STRIPS * SIDE, features)).astype(BF16)
    for slot in range(4):
        pair_ref[slot] = strips_ref[send_ref[slot]]
    for slot in range(2):
        near_ref[slot] = strips_ref[send_ref[4 + slot]]
        far_ref[slot] = strips_ref[send_ref[6 + slot]]
    pair_ref[4] = corners
    near_ref[2] = corners
    far_ref[2] = corners


def neighbours(faces):
    own = lax.axis_index("face")
    ahead, behind = lax.rem(own + 2, faces), lax.rem(own + faces - 2, faces)
    return own, own ^ 1, own ^ 2, jnp.where(own & 2 == 0, behind, ahead)


def first_kernel(faces, state_ref, edge_ref, strips_ref, near_ref, far_ref, pair_ref, table_ref, held_ref, corners_ref, edges, send, sems):
    edge_copy, state_copy = copies(sems, (edge_ref, edges), (state_ref, held_ref))
    row = lax.broadcasted_iota(I32, (BORDER, PIXELS), 0)
    column = lax.broadcasted_iota(I32, (BORDER, PIXELS), 1)
    side, k, last = row // SIDE, row % SIDE, SIDE - 1
    place = jnp.where(
        side == 0,
        k,
        jnp.where(side == 1, k * SIDE + last, jnp.where(side == 2, last * SIDE + last - k, (last - k) * SIDE)),
    )
    picks = (place == column).astype(F32).astype(BF16)
    row = lax.broadcasted_iota(I32, (STRIPS, STRIPS * SIDE), 0)
    column = lax.broadcasted_iota(I32, (STRIPS, STRIPS * SIDE), 1)
    corners_ref[...] = (row * SIDE == column).astype(F32).astype(BF16)
    own, paired, near, far = neighbours(faces)
    edge_copy.wait()
    for target, start, capacity in ((paired, 0, 4), (near, 4, 2), (far, 6, 2)):
        taken = jnp.int32(0)
        for strip in range(STRIPS):
            wanted = edges[strip % 4, target * HERE + strip // 4]
            fits = jnp.logical_and(wanted // STRIPS == own, taken < capacity)
            send[jnp.where(fits, start + taken, 8)] = wanted % STRIPS
            taken = taken + fits.astype(I32)
    for slot in range(8):
        table_ref[slot] = send[slot]
    state_copy.wait()
    features = state_ref.shape[-1]
    for tile in range(HERE):
        strips = dot(picks, held_ref[tile].reshape(PIXELS, features)).astype(BF16)
        strips_ref[4 * tile : 4 * tile + 4] = strips.reshape(4, SIDE, features)
    address(strips_ref, send, near_ref, far_ref, pair_ref, corners_ref)


def side_kernel(faces, *refs):
    edge_ref, corner_ref, conv_ref, border_ref, tile_ref, inner_ref, send_ref, state_ref = refs[:8]
    table_ref, narrow1_ref, narrow2_ref, border_held, tile_held, inner_held, strips_ref = refs[8:15]
    edges, cornered, conv, sems = refs[15:]
    started = copies(
        sems,
        (edge_ref, edges),
        (corner_ref, cornered),
        (conv_ref.at[0], conv),
        (inner_ref, inner_held),
        (border_ref, border_held),
        (tile_ref, tile_held),
    )
    for narrow in (narrow1_ref, narrow2_ref):
        narrow[...] = jnp.zeros_like(narrow)
    own, paired, near, far = neighbours(faces)
    from_pair, from_near, from_far = jnp.int32(0), jnp.int32(0), jnp.int32(0)
    for copy in started[:4]:
        copy.wait()
    for slot in range(8):
        table_ref[2 * STRIPS + slot] = send_ref[slot]
    for strip in range(STRIPS):
        wanted = edges[strip % 4, own * HERE + strip // 4]
        holder, place = wanted // STRIPS, wanted % STRIPS
        by_pair, by_near, mine = holder == paired, holder == near, holder == own
        by_far = jnp.logical_not(mine | by_pair | by_near)
        table_ref[strip] = jnp.where(
            mine,
            place,
            jnp.where(
                by_pair,
                STRIPS + jnp.minimum(from_pair, 3),
                jnp.where(
                    by_near,
                    STRIPS + 4 + jnp.minimum(from_near, 1),
                    STRIPS + 6 + jnp.minimum(from_far, 1),
                ),
            ),
        )
        from_pair = from_pair + by_pair.astype(I32)
        from_near = from_near + by_near.astype(I32)
        from_far = from_far + by_far.astype(I32)
    for corner in range(STRIPS):
        wanted = cornered[corner % 4, own * HERE + corner // 4]
        safe = jnp.maximum(wanted, 0)
        holder, place = safe // STRIPS, safe % STRIPS
        source = jnp.where(
            holder == own,
            0,
            jnp.where(
                holder == paired,
                1,
                jnp.where(holder == near, 2, jnp.where(holder == (near ^ 1), 3, jnp.where(holder == far, 4, 5))),
            ),
        )
        table_ref[STRIPS + corner] = jnp.where(wanted < 0, ZERO_ROW, source * STRIPS + place)
    for layer, narrow in enumerate((narrow1_ref, narrow2_ref)):
        spread(conv, layer, narrow)
    inner_strips(state_ref, 1, inner_held, strips_ref)
    for copy in started[4:]:
        copy.wait()


def spread(conv, layer, weight):
    width = weight.shape[-1]
    for tap in range(9):
        for level in range(width // 64):
            weight[pl.ds(width * tap + 64 * level, 64), pl.ds(64 * level, 64)] = conv[layer, tap]


def weights_kernel(*refs):
    conv_ref, mix_in_ref, mix_out_ref, _, narrow1_ref, narrow2_ref, wide1_ref, wide2_ref, mix_in_held, mix_out_held, conv, sems = refs
    started = copies(sems, (conv_ref.at[1], conv), (mix_in_ref, mix_in_held), (mix_out_ref, mix_out_held))
    for weight in (narrow1_ref, narrow2_ref, wide1_ref, wide2_ref):
        weight[...] = jnp.zeros_like(weight)
    started[0].wait()
    for layer, weights in enumerate(((narrow1_ref, wide1_ref), (narrow2_ref, wide2_ref))):
        for weight in weights:
            spread(conv, layer, weight)
    for copy in started[1:]:
        copy.wait()


def inner_strips(field_ref, top, inner_ref, strips_ref):
    features = field_ref.shape[-1]
    for tile in range(HERE):
        rows = field_ref[tile, top : top + INNER].reshape(INNER * SIDE, features)
        strips = dot(inner_ref[...], rows).astype(BF16)
        strips_ref[4 * tile : 4 * tile + 4] = strips.reshape(4, SIDE, features)


def gather_rims(received, strips_ref, inner_ref, table_ref, held, corners, row, known):
    near_ref, far_ref, pair_ref, near2_ref, far2_ref = received
    features = strips_ref.shape[-1]
    for strip in range(STRIPS):
        held[strip] = strips_ref[strip]
        corners[strip : strip + 1] = strips_ref[strip, 0:1].astype(F32)
    for slot in range(4):
        held[STRIPS + slot] = pair_ref[slot]
    for slot in range(2):
        held[STRIPS + 4 + slot] = near_ref[slot]
        held[STRIPS + 6 + slot] = far_ref[slot]
    for source, ref in enumerate((pair_ref.at[4], near_ref.at[2], near2_ref.at[2], far_ref.at[2], far2_ref.at[2])):
        corners[(source + 1) * STRIPS : (source + 2) * STRIPS] = ref[...].astype(F32)
    corners[ZERO_ROW : ZERO_ROW + 8] = jnp.zeros((8, features), F32)
    row[...] = jnp.zeros_like(row)
    for tile in range(HERE):
        for side in range(4):
            strip = 4 * tile + side
            known[tile, SIDE * side : SIDE * (side + 1)] = strips_ref[strip]
            known[tile, BORDER + SIDE * side : BORDER + SIDE * (side + 1)] = inner_ref[strip]
            known[tile, 2 * BORDER + SIDE * side : 2 * BORDER + SIDE * (side + 1)] = held[table_ref[strip]]
            row[tile, side : side + 1] = corners[pl.ds(table_ref[STRIPS + strip], 1)]
        known[tile, 3 * BORDER :] = row[tile].astype(BF16)


def border_conv(received, strips_ref, inner_ref, table_ref, weight_ref, border_ref, scratch):
    held, corners, row, known, patches = scratch
    gather_rims(received, strips_ref, inner_ref, table_ref, held, corners, row, known)
    features, width = strips_ref.shape[-1], weight_ref.shape[-1]
    for tile in range(HERE):
        moved = dot(border_ref[...], known[tile]).astype(BF16)
        for tap in range(9):
            patches[tap, BORDER * tile : BORDER * (tile + 1)] = moved[BORDER * tap : BORDER * (tap + 1)]
    for group in range(features // width):
        lanes = slice(width * group, width * (group + 1))
        yield lanes, dot(jnp.concatenate([patches[tap, :, lanes] for tap in range(9)], 1), weight_ref[...])


def border_kernel(last, sends, *refs):
    strips_ref, inner_ref, *received = refs[:7]
    table_ref, weight_ref, border_ref, corners_ref = refs[7:11]
    rest = list(refs[11:])
    state_ref = rest.pop(0) if last else None
    out_ref = rest.pop(0)
    messages = [rest.pop(0) for _ in range(3 if sends else 0)]
    for lanes, total in border_conv(received, strips_ref, inner_ref, table_ref, weight_ref, border_ref, rest):
        if last:
            total = total + state_ref[:, :, lanes].reshape(total.shape).astype(F32)
        else:
            total = gelu(total)
        out_ref[:, :, lanes] = total.astype(BF16).reshape(STRIPS, SIDE, -1)
    if sends:
        address(out_ref, table_ref.at[pl.ds(2 * STRIPS, 8)], *messages, corners_ref)


def tile_conv(field_ref, top, strips_ref, weight_ref, tile_ref, shifted, tile):
    features, width = field_ref.shape[-1], weight_ref.shape[-1]
    strips = strips_ref[4 * tile : 4 * tile + 4].reshape(BORDER, features)
    half, rows = SIDE // 2, INNER // 2
    for group in range(2):
        inner = field_ref[tile, top + rows * group : top + rows * (group + 1)].reshape(rows * SIDE, features)
        moved = dot(tile_ref[group], jnp.concatenate([inner, strips], 0)).astype(BF16)
        shifted[:, half * group : half * (group + 1)] = moved.reshape(3, half, SIDE, features)
    for group in range(features // width):
        lanes = slice(width * group, width * (group + 1))
        windows = [shifted[b, a : a + INNER, :, lanes].reshape(INNER * SIDE, width) for a in range(3) for b in range(3)]
        yield lanes, dot(jnp.concatenate(windows, 1), weight_ref[...])


def inner_kernel(last, top, field_ref, strips_ref, weight_ref, tile_ref, other_ref, out_ref, *rest):
    shifted = rest[-1]
    for tile in range(HERE):
        for lanes, total in tile_conv(field_ref, top, strips_ref, weight_ref, tile_ref, shifted.at[tile], tile):
            if last:
                total = total + other_ref[tile, 1 : 1 + INNER, :, lanes].reshape(total.shape).astype(F32)
            else:
                total = gelu(total)
            out_ref[tile, :, :, lanes] = total.astype(BF16).reshape(INNER, SIDE, -1)
    if not last:
        inner_strips(out_ref, 0, other_ref, rest[0])


def mixer(block, level, mix_in_ref, mix_out_ref, outs):
    levels = mix_in_ref.shape[1] // 128
    order = [level ^ back for back in range(levels)]
    first = jnp.concatenate([mix_in_ref[block, pl.ds(pl.multiple_of(128 * place, 128), 128), :] for place in order], 0)
    second = [mix_out_ref[block, :, pl.ds(pl.multiple_of(128 * place, 128), 128)] for place in order[:outs]]
    second = jnp.concatenate(second, 1) if outs > 1 else second[0]

    def mix(column):
        hidden = gelu(dot(column, first)).astype(BF16)
        return (column[:, : 128 * outs].astype(F32) + dot(hidden, second)).astype(BF16)

    return mix


def mix_strips_kernel(block, own_ref, one_ref, two_ref, three_ref, mix_in_ref, mix_out_ref, table_ref, corners_ref, strips_ref, near_ref, far_ref, pair_ref):
    mix = mixer(block, lax.axis_index("level"), mix_in_ref, mix_out_ref, 4)
    column = jnp.concatenate([ref[...].reshape(STRIPS * SIDE, 128) for ref in (own_ref, one_ref, two_ref, three_ref)], 1)
    strips_ref[...] = mix(column).reshape(STRIPS, SIDE, 512)
    address(strips_ref, table_ref.at[pl.ds(2 * STRIPS, 8)], near_ref, far_ref, pair_ref, corners_ref)


def mix_tiles_kernel(block, own_ref, one_ref, two_ref, three_ref, mix_in_ref, mix_out_ref, inner_ref, out_ref, strips_ref):
    mix = mixer(block, lax.axis_index("level"), mix_in_ref, mix_out_ref, 4)
    for tile in range(HERE):
        column = jnp.concatenate([ref[tile].reshape(INNER * SIDE, 128) for ref in (own_ref, one_ref, two_ref, three_ref)], 1)
        out_ref[tile] = mix(column).reshape(INNER, SIDE, 512)
    inner_strips(out_ref, 0, inner_ref, strips_ref)


def last_inner_kernel(block, field_ref, strips_ref, weight_ref, tile_ref, state_ref, mix_in_ref, mix_out_ref, out_ref, shifted):
    mix = mixer(block, lax.axis_index("level"), mix_in_ref, mix_out_ref, 1)
    for tile in range(HERE):
        columns = []
        for lanes, total in tile_conv(field_ref, 0, strips_ref, weight_ref, tile_ref, shifted.at[tile], tile):
            columns.append((total + state_ref[tile, :, :, lanes].reshape(total.shape).astype(F32)).astype(BF16))
        out_ref[tile] = mix(jnp.concatenate(columns, 1)).reshape(INNER, SIDE, 128)


def last_border_kernel(block, *refs):
    strips_ref, inner_ref, *received = refs[:7]
    table_ref, weight_ref, border_ref, state_ref, mix_in_ref, mix_out_ref, tiles_ref, tile_ref, out_ref = refs[7:16]
    mix = mixer(block, lax.axis_index("level"), mix_in_ref, mix_out_ref, 1)
    columns = []
    for lanes, total in border_conv(received, strips_ref, inner_ref, table_ref, weight_ref, border_ref, refs[16:]):
        columns.append((total + state_ref[:, :, lanes].reshape(total.shape).astype(F32)).astype(BF16))
    mixed = mix(jnp.concatenate(columns, 1))
    half, rows = SIDE // 2, INNER // 2
    for tile in range(HERE):
        strips = mixed[BORDER * tile : BORDER * (tile + 1)]
        for group in range(2):
            inner = tiles_ref[tile, rows * group : rows * (group + 1)].reshape(rows * SIDE, 128)
            place = tile_ref[group, half * SIDE : 2 * half * SIDE]
            merged = dot(place, jnp.concatenate([inner, strips], 0)).astype(BF16)
            out_ref[tile, half * group : half * (group + 1)] = merged.reshape(half, SIDE, 128)


V = pl.BlockSpec(memory_space=pltpu.VMEM)
S = pl.BlockSpec(memory_space=pltpu.SMEM)
H = pl.BlockSpec(memory_space=pltpu.HBM)


def call(kernel, name, in_specs, out_specs, out_shape, scratch, args):
    return pl.pallas_call(
        kernel,
        name=name,
        in_specs=in_specs,
        out_specs=out_specs,
        out_shape=out_shape,
        scratch_shapes=scratch,
        compiler_params=pltpu.CompilerParams(vmem_limit_bytes=VMEM_LIMIT),
    )(*(pltpu.with_memory_space_constraint(arg, pltpu.HBM) if spec is H else arg for spec, arg in zip(in_specs, args)))


def arrays(*shapes):
    return [jax.ShapeDtypeStruct(shape, BF16) for shape in shapes]


def strip_shape(features):
    return STRIPS, SIDE, features


def message_shapes(features):
    return (3, SIDE, features), (3, SIDE, features), (5, SIDE, features)


def border_scratch(features):
    return [
        pltpu.VMEM((STRIPS + 8, SIDE, features), BF16),
        pltpu.VMEM((ZERO_ROW + 8, features), F32),
        pltpu.VMEM((HERE, SIDE, features), F32),
        pltpu.VMEM((HERE, 3 * BORDER + SIDE, features), BF16),
        pltpu.VMEM((9, STRIPS * SIDE, features), BF16),
    ]


def tile_scratch(features):
    return [pltpu.VMEM((HERE, 3, SIDE, SIDE, features), BF16)]


def send(near, far, to_pair):
    faces = lax.axis_size("face")
    apart = [(i, (i + 2) % faces if i & 2 else (i - 2) % faces) for i in range(faces)]
    from_far = lax.ppermute(far, "face", apart)
    from_near = lax.ppermute(near, "face", [(i, i ^ 2) for i in range(faces)])
    return from_near, from_far, lax.ppermute(to_pair, "face", [(i, i ^ 1) for i in range(faces)])


def receive(sent, *beside):
    near, far, paired = sent
    near, far, *beside = lax.optimization_barrier((near, far, *beside))
    pairs = [(i, i ^ 1) for i in range(lax.axis_size("face"))]
    arrived = near, far, paired, lax.ppermute(near, "face", pairs), lax.ppermute(far, "face", pairs)
    return arrived, *beside


def from_level(shard, distance):
    levels = lax.axis_size("level")
    return lax.ppermute(shard, "level", [(i, i ^ distance) for i in range(levels)])


def shards(state, conv_weight, mix_in, mix_out, edge_source, corner_source):
    faces = lax.axis_size("face")
    thin = state.shape[-1]
    wide = 4 * thin
    border_hbm, tile_hbm, inner_hbm = (jnp.asarray(t) for t in (border_table(), tile_table(), inner_table()))
    edges, cornered = edge_source.T, corner_source.T
    edge_scratch = pltpu.SMEM(edges.shape, I32)

    strips, *messages, sends, state, corners = call(
        functools.partial(first_kernel, faces), "first",
        [H, H], [V, V, V, V, S, V, V],
        arrays(strip_shape(thin), *message_shapes(thin))
        + [jax.ShapeDtypeStruct((8,), I32)]
        + arrays(state.shape, (STRIPS, STRIPS * SIDE)),
        [edge_scratch, pltpu.SMEM((16,), I32), pltpu.SemaphoreType.DMA((2,))],
        (state, edges),
    )
    sent = send(*messages)
    table, narrow1, narrow2, borders, tiled, inner_places, state_inner = call(
        functools.partial(side_kernel, faces), "side",
        [H] * 6 + [S, V], [S] + [V] * 6,
        [jax.ShapeDtypeStruct((2 * STRIPS + 8,), I32)]
        + arrays((1152, 128), (1152, 128), border_hbm.shape, tile_hbm.shape, inner_hbm.shape, strip_shape(thin)),
        [edge_scratch, edge_scratch, pltpu.VMEM(conv_weight.shape[1:], BF16), pltpu.SemaphoreType.DMA((6,))],
        (edges, cornered, conv_weight, border_hbm, tile_hbm, inner_hbm, sends, state),
    )

    def border(last, sending, strips, inner_strips, received, weight, residual=()):
        size = strips.shape[-1]
        shapes = [strip_shape(size), *(message_shapes(size) if sending else ())]
        return call(
            functools.partial(border_kernel, last, sending), f"border_{size}_{int(last)}",
            [V] * 7 + [S] + [V] * 3 + [V] * len(residual), [V] * len(shapes),
            arrays(*shapes), border_scratch(size),
            (strips, inner_strips, *received, table, weight, borders, corners, *residual),
        )

    def interior(last, top, field, strips, weight, other):
        size = field.shape[-1]
        shapes = [(HERE, INNER, SIDE, size)] + ([] if last else [strip_shape(size)])
        return call(
            functools.partial(inner_kernel, last, top), f"inner_{size}_{int(last)}",
            [V] * 5, [V] * len(shapes), arrays(*shapes), tile_scratch(size),
            (field, strips, weight, tiled, other),
        )

    inner, inner_ring = interior(False, 1, state, strips, narrow1, inner_places)
    received, inner, inner_ring = receive(sent, inner, inner_ring)
    inner_edge, *messages = border(False, True, strips, state_inner, received, narrow1)

    sent = send(*messages)
    (field,) = interior(True, 0, inner, inner_edge, narrow2, state)
    one, three = from_level(field, 1), from_level(field, 3)
    received, _ = receive(sent, field)
    (edge,) = border(True, False, inner_edge, inner_ring, received, narrow2, (strips,))

    narrow3, narrow4, wide1, wide2, mix_in, mix_out = call(
        weights_kernel, "weights", [H] * 3 + [V], [V] * 6,
        arrays((1152, 128), (1152, 128), (2304, 256), (2304, 256), mix_in.shape, mix_out.shape),
        [pltpu.VMEM(conv_weight.shape[1:], BF16), pltpu.SemaphoreType.DMA((3,))],
        (conv_weight, mix_in, mix_out, edge),
    )
    three, edge = lax.optimization_barrier((three, edge))
    fields = [field, one, from_level(three, 1), three]
    edge_parts = [edge] + [from_level(edge, d) for d in (1, 2, 3)]
    strips, *messages = call(
        functools.partial(mix_strips_kernel, 0), "mix_strips",
        [V] * 6 + [S, V], [V] * 4,
        arrays(strip_shape(wide), *message_shapes(wide)), [],
        (*edge_parts, mix_in, mix_out, table, corners),
    )
    sent = send(*messages)
    field, ring1 = call(
        functools.partial(mix_tiles_kernel, 0), "mix_tiles",
        [V] * 7, [V] * 2, arrays((HERE, INNER, SIDE, wide), strip_shape(wide)), [],
        (*fields, mix_in, mix_out, inner_places),
    )
    inner, inner_ring = interior(False, 0, field, strips, wide1, inner_places)
    received, inner, inner_ring = receive(sent, inner, inner_ring)
    inner_edge, *messages = border(False, True, strips, ring1, received, narrow3)

    sent = send(*messages)
    tiles = call(
        functools.partial(last_inner_kernel, 1), "last_inner",
        [V] * 7, V, arrays((HERE, INNER, SIDE, thin))[0], tile_scratch(wide),
        (inner, inner_edge, wide2, tiled, field, mix_in, mix_out),
    )
    received, tiles = receive(sent, tiles)
    return call(
        functools.partial(last_border_kernel, 1), "last_border",
        [V] * 7 + [S] + [V] * 7, V, arrays((HERE, SIDE, SIDE, thin))[0], border_scratch(wide),
        (inner_edge, inner_ring, *received, table, narrow4, borders, strips, mix_in, mix_out, tiles, tiled),
    )


def solution(mesh):
    return jax.shard_map(
        shards,
        mesh=mesh,
        in_specs=(P(("ens", "face"), None, None, "level"), P(), P(), P(), P(), P()),
        out_specs=P(("ens", "face"), None, None, "level"),
        check_vma=False,
    )
```

time: 96.9 us -> 73.9 us (0.76)
  starting transfers between devices: 42.8 us -> 31.6 us
  local copies, waits for them, and re-layouts: 9.8 us -> 0 us
  waiting for transfers between devices: 18.9 us -> 13.4 us
  Pallas kernels: 24.7 us -> 28.6 us
    ppermute x26, starting transfers between devices: 42.8 us -> 31.6 us  [the longest x4 14.9 us: send(): from_far = lax.ppermute(far, 'face', apart)]
    unnamed x34 -> x0, local copies, waits for them, and re-layouts: 9.8 us -> none
    ppermute x26, waiting for transfers between devices: 18.9 us -> 13.4 us  [the longest x6 6.48 us: from_level(): lax.ppermute(shard, 'level', [(i, i ^ distance) for i in range(levels)])]
    pallas_call x8 -> x13, Pallas kernels: 24.7 us -> 28.6 us  [call(): pl.pallas_call(kernel, name=name, in_specs=in_specs, out_specs=out_specs,...]
  transfers between devices with their start and end apart: 26 -> 26, of which waited for: 10 -> 11; matrix products, arithmetic and copies ran while one was open for 0% -> 0% of each run, Pallas kernels for 6% -> 25%
where the time goes in v1:
time: 73.9 us; the launch traced here: 73.8 us
  starting transfers between devices  31.6 us (43%)
  Pallas kernels  28.6 us (39%)
  waiting for transfers between devices  13.4 us (18%)
    pallas_call x13, Pallas kernels, call(): pl.pallas_call(kernel, name=name, in_specs=in_specs, out_specs=out_specs,...  28.6 us
    ppermute x4, starting transfers between devices, send(): from_far = lax.ppermute(far, 'face', apart)  14.9 us
    ppermute x6, waiting for transfers between devices, from_level(): lax.ppermute(shard, 'level', [(i, i ^ distance) for i in range(levels)])  6.48 us
    ppermute x6, starting transfers between devices, from_level(): lax.ppermute(shard, 'level', [(i, i ^ distance) for i in range(levels)])  6.4 us
    ppermute x4, starting transfers between devices, send(): lax.ppermute(to_pair, 'face', [(i, i ^ 1) for i in range(faces)])  4.23 us
    ppermute x4, waiting for transfers between devices, send(): from_far = lax.ppermute(far, 'face', apart)  3.1 us
    ppermute x4, waiting for transfers between devices, receive(): lax.ppermute(near, 'face', pairs)  2.92 us
    ppermute x4, starting transfers between devices, send(): from_near = lax.ppermute(near, 'face', [(i, i ^ 2) for i in range(faces)])  2.57 us
  transfers between devices with their start and end apart: 26, of which 11 were waited for; matrix products, arithmetic and copies ran while one was open for 0% of the time, Pallas kernels for 25%

profile of v1, /device:TPU:1, one launch (start us, length us, event | category | flops | bytes accessed | tf_op | source)
XLA Modules:
  0.0 73.8 jit_solution(16049052149424920370)
XLA Ops:
  0.0 1.7 %first.1 = (bf16[16,16,128]{2,1,0:T(8,128)(2,1)S(1)}, bf16[3,16,128]{2,1,0:T(8,128)(2,1)S(1)}, bf16[3,16,128]{2,1,0:T(8,128)(2,1)S(1)}, bf16[5,16,128]{2,1,0:T(8...) custom-call(bf16[4,16,16,128]{3,2,1,0:T(8,128)(2,1)} %state_ref.1, ...), custom_call_target="tpu_custom_call" | custom-call | tf_op jit(solution)/shard_map/first/pallas_call | solution.py:400
  1.7 2.6 %collective-permute-start = (bf16[3,16,128]{2,1,0:T(8,128)(2,1)S(1)}, bf16[3,16,128]{2,1,0:T(8,128)(2,1)S(1)}, u32[]{:S(2)}, u32[]{:S(2)}) collective-permute-start(bf16[3,16,128]{2,1,0:T(8,128)(2,1)S(1)} %get-tuple-element.58), channel_id=1, source_target_pairs={{0,16},{8,24},{16,0},{24,8},{32,48},{40,56},{48,32},{56,40},{64,80... | collective-permute-start | bytes 36872 | tf_op jit(solution)/shard_map/ppermute | solution.py:441
  4.3 7.3 %collective-permute-start.1 = (bf16[3,16,128]{2,1,0:T(8,128)(2,1)S(1)}, bf16[3,16,128]{2,1,0:T(8,128)(2,1)S(1)}, u32[]{:S(2)}, u32[]{:S(2)}) collective-permute-start(bf16[3,16,128]{2,1,0:T(8,128)(2,1)S(1)} %get-tuple-element.59), channel_id=1, source_target_pairs={{0,240},{8,248},{16,32},{24,40},{32,16},{40,24},{48,64},{56,72},{6... | collective-permute-start | bytes 36872 | tf_op jit(solution)/shard_map/ppermute | solution.py:440
  12.8 2.7 %side.1 = (s32[40]{0:T(128)S(1)}, bf16[1152,128]{1,0:T(8,128)(2,1)S(1)}, bf16[1152,128]{1,0:T(8,128)(2,1)S(1)}, bf16[576,208]{1,0:T(8,128)(2,1)S(1)}, bf16[2,384...) custom-call(s32[4,128]{1,0:T(4,128)} %bitcast.3, s32[4,128]{1,0:T(4,128)} %bitcast.4, ...), custom_call_target="tpu_custom_call" | custom-call | tf_op jit(solution)/shard_map/side/pallas_call | solution.py:400
  15.6 1.7 %inner_128_0.1 = (bf16[4,14,16,128]{3,2,1,0:T(8,128)(2,1)S(1)}, bf16[16,16,128]{2,1,0:T(8,128)(2,1)S(1)}) custom-call(bf16[4,16,16,128]{3,2,1,0:T(8,128)(2,1)S(1)} %get-tuple-element.60.refs_7_.field_ref.other_ref, bf16[16,16,128]{2,1,0:T(8,128)(2,1)S(1)} %get-tuple-element.61.strips_ref.refs_0_.refs_11_, ...), custom_call_target="tpu_custom_call" | custom-call | tf_op jit(solution)/shard_map/inner_128_0/pallas_call | solution.py:400
  18.7 1.4 %border_128_0.1 = (bf16[16,16,128]{2,1,0:T(8,128)(2,1)S(1)}, bf16[3,16,128]{2,1,0:T(8,128)(2,1)S(1)}, bf16[3,16,128]{2,1,0:T(8,128)(2,1)S(1)}, bf16[5,16,128]{2,1,0:T(8,128)(2,1)S(1)}) custom-call(bf16[16,16,128]{2,1,0:T(8,128)(2,1)S(1)} %get-tuple-element.61.strips_ref.refs_0_.refs_11_, bf16[16,16,128]{2,1,0:T(8,128)(2,1)S(1)} %get-tuple-element.69.refs_1_, ...), custom_call_target="tpu_custom_call" | custom-call | tf_op jit(solution)/shard_map/border_128_0/pallas_call | solution.py:400
  20.1 1.5 %inner_128_1.1.own_ref = bf16[4,14,16,128]{3,2,1,0:T(8,128)(2,1)S(1)} custom-call(bf16[4,14,16,128]{3,2,1,0:T(8,128)(2,1)S(1)} %get-tuple-element.68.field_ref, bf16[16,16,128]{2,1,0:T(8,128)(2,1)S(1)} %get-tuple-element.76.strips_ref.refs_0_, bf16[1152,128]{1,0:T(8,128)(2,1)S(1)} %get-tuple-element.77.weight_ref.refs_8_, ...), custom_call_target="tpu_custom_call" | custom-call | tf_op jit(solution)/shard_map/inner_128_1/pallas_call | solution.py:400
  21.6 2.6 %collective-permute-start.5 = (bf16[4,14,16,128]{3,2,1,0:T(8,128)(2,1)S(1)}, bf16[4,14,16,128]{3,2,1,0:T(8,128)(2,1)S(1)}, u32[]{:S(2)}, u32[]{:S(2)}) collective-permute-start(bf16[4,14,16,128]{3,2,1,0:T(8,128)(2,1)S(1)} %inner_128_1.1.own_ref), channel_id=1, source_target_pairs={{0,6},{2,4},{4,2},{6,0},{1,7},{3,5},{5,3},{7,1},{8,14},{10,12},{12... | collective-permute-start | bytes 688136 | tf_op jit(solution)/shard_map/ppermute | solution.py:455
  24.1 2.3 %collective-permute-start.7 = (bf16[3,16,128]{2,1,0:T(8,128)(2,1)S(1)}, bf16[3,16,128]{2,1,0:T(8,128)(2,1)S(1)}, u32[]{:S(2)}, u32[]{:S(2)}) collective-permute-start(bf16[3,16,128]{2,1,0:T(8,128)(2,1)S(1)} %get-tuple-element.80), channel_id=1, source_target_pairs={{0,240},{8,248},{16,32},{24,40},{32,16},{40,24},{48,64},{56,72},{6... | collective-permute-start | bytes 36872 | tf_op jit(solution)/shard_map/ppermute | solution.py:440
  27.2 3.1 %collective-permute-done.7.refs_3_ = bf16[3,16,128]{2,1,0:T(8,128)(2,1)S(1)} collective-permute-done((bf16[3,16,128]{2,1,0:T(8,128)(2,1)S(1)}, bf16[3,16,128]{2,1,0:T(8,128)(2,1)S(1)}, u32[]{:S(2)}, u32[]{:S(2)}) %collective-permute-start.7) | collective-permute-done | bytes 12320 | tf_op jit(solution)/shard_map/ppermute | solution.py:440
  30.3 1.8 %collective-permute-start.9 = (bf16[3,16,128]{2,1,0:T(8,128)(2,1)S(1)}, bf16[3,16,128]{2,1,0:T(8,128)(2,1)S(1)}, u32[]{:S(2)}, u32[]{:S(2)}) collective-permute-start(bf16[3,16,128]{2,1,0:T(8,128)(2,1)S(1)} %collective-permute-done.6.refs_2_), channel_id=1, source_target_pairs={{0,8},{8,0},{16,24},{24,16},{32,40},{40,32},{48,56},{56,48},{64,72... | collective-permute-start | bytes 36872 | tf_op jit(solution)/shard_map/ppermute | solution.py:449
  35.6 2.5 %collective-permute-start.12 = (bf16[16,16,128]{2,1,0:T(8,128)(2,1)S(1)}, bf16[16,16,128]{2,1,0:T(8,128)(2,1)S(1)}, u32[]{:S(2)}, u32[]{:S(2)}) collective-permute-start(bf16[16,16,128]{2,1,0:T(8,128)(2,1)S(1)} %border_128_1.1.refs_3_.own_ref), channel_id=1, source_target_pairs={{0,4},{2,6},{4,0},{6,2},{1,5},{3,7},{5,1},{7,3},{8,12},{10,14},{12... | collective-permute-start | bytes 196616 | tf_op jit(solution)/shard_map/ppermute | solution.py:455
  38.3 1.7 %weights.1 = (bf16[1152,128]{1,0:T(8,128)(2,1)S(1)}, bf16[1152,128]{1,0:T(8,128)(2,1)S(1)}, bf16[2304,256]{1,0:T(8,128)(2,1)S(1)}, bf16[2304,256]{1,0:T(8,128)(2...) custom-call(bf16[2,2,9,64,64]{4,3,2,1,0:T(8,128)(2,1)} %refs_0_.1, ...), custom_call_target="tpu_custom_call" | custom-call | tf_op jit(solution)/shard_map/weights/pallas_call | solution.py:400
  40.0 4.7 %collective-permute-done.12.two_ref = bf16[16,16,128]{2,1,0:T(8,128)(2,1)S(1)} collective-permute-done((bf16[16,16,128]{2,1,0:T(8,128)(2,1)S(1)}, bf16[16,16,128]{2,1,0:T(8,128)(2,1)S(1)}, u32[]{:S(2)}, u32[]{:S(2)}) %collective-permute-start.12) | collective-permute-done | bytes 65568 | tf_op jit(solution)/shard_map/ppermute | solution.py:455
  44.7 1.8 %collective-permute-done.11.one_ref = bf16[16,16,128]{2,1,0:T(8,128)(2,1)S(1)} collective-permute-done((bf16[16,16,128]{2,1,0:T(8,128)(2,1)S(1)}, bf16[16,16,128]{2,1,0:T(8,128)(2,1)S(1)}, u32[]{:S(2)}, u32[]{:S(2)}) %collective-permute-start.11) | collective-permute-done | bytes 65568 | tf_op jit(solution)/shard_map/ppermute | solution.py:455
  46.5 1.3 %mix_strips.1 = (bf16[16,16,512]{2,1,0:T(8,128)(2,1)S(1)}, bf16[3,16,512]{2,1,0:T(8,128)(2,1)S(1)}, bf16[3,16,512]{2,1,0:T(8,128)(2,1)S(1)}, bf16[5,16,512]{2,1,0:T(8,128)(2,1)S(1)}) custom-call(bf16[16,16,128]{2,1,0:T(8,128)(2,1)S(1)} %border_128_1.1.refs_3_.own_ref, bf16[16,16,128]{2,1,0:T(8,128)(2,1)S(1)} %collective-permute-done.11.one_ref, ...), custom_call_target="tpu_custom_call" | custom-call | tf_op jit(solution)/shard_map/mix_strips/pallas_call | solution.py:400
  47.7 2.2 %collective-permute-start.17 = (bf16[3,16,512]{2,1,0:T(8,128)(2,1)S(1)}, bf16[3,16,512]{2,1,0:T(8,128)(2,1)S(1)}, u32[]{:S(2)}, u32[]{:S(2)}) collective-permute-start(bf16[3,16,512]{2,1,0:T(8,128)(2,1)S(1)} %get-tuple-element.91), channel_id=1, source_target_pairs={{0,240},{8,248},{16,32},{24,40},{32,16},{40,24},{48,64},{56,72},{6... | collective-permute-start | bytes 147464 | tf_op jit(solution)/shard_map/ppermute | solution.py:440
  50.0 1.6 %collective-permute-start.18 = (bf16[5,16,512]{2,1,0:T(8,128)(2,1)S(1)}, bf16[5,16,512]{2,1,0:T(8,128)(2,1)S(1)}, u32[]{:S(2)}, u32[]{:S(2)}) collective-permute-start(bf16[5,16,512]{2,1,0:T(8,128)(2,1)S(1)} %get-tuple-element.98), channel_id=1, source_target_pairs={{0,8},{8,0},{16,24},{24,16},{32,40},{40,32},{48,56},{56,48},{64,72... | collective-permute-start | bytes 245768 | tf_op jit(solution)/shard_map/ppermute | solution.py:442
  51.6 1.9 %mix_tiles.1 = (bf16[4,14,16,512]{3,2,1,0:T(8,128)(2,1)S(1)}, bf16[16,16,512]{2,1,0:T(8,128)(2,1)S(1)}) custom-call(bf16[4,14,16,128]{3,2,1,0:T(8,128)(2,1)S(1)} %inner_128_1.1.own_ref, bf16[4,14,16,128]{3,2,1,0:T(8,128)(2,1)S(1)} %collective-permute-done.14.one_ref, bf16[4,14,16,128]{3,2,1,0:T(8,128)(2,1)S(1)} %collective-permute-done.15.two_ref, ...), custom_call_target="tpu_custom_call" | custom-call | tf_op jit(solution)/shard_map/mix_tiles/pallas_call | solution.py:400
  53.5 3.4 %inner_512_0.1 = (bf16[4,14,16,512]{3,2,1,0:T(8,128)(2,1)S(1)}, bf16[16,16,512]{2,1,0:T(8,128)(2,1)S(1)}) custom-call(bf16[4,14,16,512]{3,2,1,0:T(8,128)(2,1)S(1)} %get-tuple-element.92.field_ref.state_ref, bf16[16,16,512]{2,1,0:T(8,128)(2,1)S(1)} %get-tuple-element.87.strips_ref.refs_0_.refs_10_, bf16[2304,256]{1,0:T(8,128)(2,1)S(1)} %get-tuple-element.93.weight_ref, ...), custom_call_target="tpu_custom_call" | custom-call | tf_op jit(solution)/shard_map/inner_512_0/pallas_call | solution.py:400
  58.4 2.2 %border_512_0.1 = (bf16[16,16,512]{2,1,0:T(8,128)(2,1)S(1)}, bf16[3,16,512]{2,1,0:T(8,128)(2,1)S(1)}, bf16[3,16,512]{2,1,0:T(8,128)(2,1)S(1)}, bf16[5,16,512]{2,1,0:T(8,128)(2,1)S(1)}) custom-call(bf16[16,16,512]{2,1,0:T(8,128)(2,1)S(1)} %get-tuple-element.87.strips_ref.refs_0_.refs_10_, bf16[16,16,512]{2,1,0:T(8,128)(2,1)S(1)} %get-tuple-element.89.refs_1_, ...), custom_call_target="tpu_custom_call" | custom-call | tf_op jit(solution)/shard_map/border_512_0/pallas_call | solution.py:400
  60.5 3.0 %collective-permute-start.22 = (bf16[3,16,512]{2,1,0:T(8,128)(2,1)S(1)}, bf16[3,16,512]{2,1,0:T(8,128)(2,1)S(1)}, u32[]{:S(2)}, u32[]{:S(2)}) collective-permute-start(bf16[3,16,512]{2,1,0:T(8,128)(2,1)S(1)} %get-tuple-element.103), channel_id=1, source_target_pairs={{0,240},{8,248},{16,32},{24,40},{32,16},{40,24},{48,64},{56,72},{6... | collective-permute-start | bytes 147464 | tf_op jit(solution)/shard_map/ppermute | solution.py:440
  64.2 4.8 %last_inner.1.refs_13_ = bf16[4,14,16,128]{3,2,1,0:T(8,128)(2,1)S(1)} custom-call(bf16[4,14,16,512]{3,2,1,0:T(8,128)(2,1)S(1)} %get-tuple-element.104.field_ref, bf16[16,16,512]{2,1,0:T(8,128)(2,1)S(1)} %get-tuple-element.100.strips_ref.refs_0_, bf16[2304,256]{1,0:T(8,128)(2,1)S(1)} %get-tuple-element.105.weight_ref, ...), custom_call_target="tpu_custom_call" | custom-call | tf_op jit(solution)/shard_map/last_inner/pallas_call | solution.py:400
  70.5 3.3 %last_border.1 = bf16[4,16,16,128]{3,2,1,0:T(8,128)(2,1)} custom-call(bf16[16,16,512]{2,1,0:T(8,128)(2,1)S(1)} %get-tuple-element.100.strips_ref.refs_0_, bf16[16,16,512]{2,1,0:T(8,128)(2,1)S(1)} %get-tuple-element.101.refs_1_, bf16[3,16,512]{2,1,0:T(8,128)(2,1)S(1)} %collective-permute-done.21.refs_2_, ...), custom_call_target="tpu_custom_call" | custom-call | tf_op jit(solution)/shard_map/last_border/pallas_call | solution.py:400
  (41 shorter events, 10.8 us)
Async XLA Ops:
  1.7 15.5 %collective-permute-start = (bf16[3,16,128]{2,1,0:T(8,128)(2,1)S(1)}, bf16[3,16,128]{2,1,0:T(8,128)(2,1)S(1)}, u32[]{:S(2)}, u32[]{:S(2)}) collective-permute-start(bf16[3,16,128]{2,1,0:T(8,128)(2,1)S(1)} %get-tuple-element.58), channel_id=1, source_target_pairs={{0,16},{8,24},{16,0},{24,8},{32,48},{40,56},{48,32},{56,40},{64,80... | collective-permute-start | bytes 36872 | tf_op jit(solution)/shard_map/ppermute | solution.py:441
  4.3 13.0 %collective-permute-start.1 = (bf16[3,16,128]{2,1,0:T(8,128)(2,1)S(1)}, bf16[3,16,128]{2,1,0:T(8,128)(2,1)S(1)}, u32[]{:S(2)}, u32[]{:S(2)}) collective-permute-start(bf16[3,16,128]{2,1,0:T(8,128)(2,1)S(1)} %get-tuple-element.59), channel_id=1, source_target_pairs={{0,240},{8,248},{16,32},{24,40},{32,16},{40,24},{48,64},{56,72},{6... | collective-permute-start | bytes 36872 | tf_op jit(solution)/shard_map/ppermute | solution.py:440
  11.6 6.3 %collective-permute-start.2 = (bf16[5,16,128]{2,1,0:T(8,128)(2,1)S(1)}, bf16[5,16,128]{2,1,0:T(8,128)(2,1)S(1)}, u32[]{:S(2)}, u32[]{:S(2)}) collective-permute-start(bf16[5,16,128]{2,1,0:T(8,128)(2,1)S(1)} %get-tuple-element.72), channel_id=1, source_target_pairs={{0,8},{8,0},{16,24},{24,16},{32,40},{40,32},{48,56},{56,48},{64,72... | collective-permute-start | bytes 61448 | tf_op jit(solution)/shard_map/ppermute | solution.py:442
  17.4 1.3 %collective-permute-start.4 = (bf16[3,16,128]{2,1,0:T(8,128)(2,1)S(1)}, bf16[3,16,128]{2,1,0:T(8,128)(2,1)S(1)}, u32[]{:S(2)}, u32[]{:S(2)}) collective-permute-start(bf16[3,16,128]{2,1,0:T(8,128)(2,1)S(1)} %collective-permute-done.1.refs_3_), channel_id=1, source_target_pairs={{0,8},{8,0},{16,24},{24,16},{32,40},{40,32},{48,56},{56,48},{64,72... | collective-permute-start | bytes 36872 | tf_op jit(solution)/shard_map/ppermute | solution.py:449
  21.6 12.9 %collective-permute-start.5 = (bf16[4,14,16,128]{3,2,1,0:T(8,128)(2,1)S(1)}, bf16[4,14,16,128]{3,2,1,0:T(8,128)(2,1)S(1)}, u32[]{:S(2)}, u32[]{:S(2)}) collective-permute-start(bf16[4,14,16,128]{3,2,1,0:T(8,128)(2,1)S(1)} %inner_128_1.1.own_ref), channel_id=1, source_target_pairs={{0,6},{2,4},{4,2},{6,0},{1,7},{3,5},{5,3},{7,1},{8,14},{10,12},{12... | collective-permute-start | bytes 688136 | tf_op jit(solution)/shard_map/ppermute | solution.py:455
  24.1 3.1 %collective-permute-start.6 = (bf16[3,16,128]{2,1,0:T(8,128)(2,1)S(1)}, bf16[3,16,128]{2,1,0:T(8,128)(2,1)S(1)}, u32[]{:S(2)}, u32[]{:S(2)}) collective-permute-start(bf16[3,16,128]{2,1,0:T(8,128)(2,1)S(1)} %get-tuple-element.79), channel_id=1, source_target_pairs={{0,16},{8,24},{16,0},{24,8},{32,48},{40,56},{48,32},{56,40},{64,80... | collective-permute-start | bytes 36872 | tf_op jit(solution)/shard_map/ppermute | solution.py:441
  24.1 6.2 %collective-permute-start.7 = (bf16[3,16,128]{2,1,0:T(8,128)(2,1)S(1)}, bf16[3,16,128]{2,1,0:T(8,128)(2,1)S(1)}, u32[]{:S(2)}, u32[]{:S(2)}) collective-permute-start(bf16[3,16,128]{2,1,0:T(8,128)(2,1)S(1)} %get-tuple-element.80), channel_id=1, source_target_pairs={{0,240},{8,248},{16,32},{24,40},{32,16},{40,24},{48,64},{56,72},{6... | collective-permute-start | bytes 36872 | tf_op jit(solution)/shard_map/ppermute | solution.py:440
  26.5 5.6 %collective-permute-start.8 = (bf16[5,16,128]{2,1,0:T(8,128)(2,1)S(1)}, bf16[5,16,128]{2,1,0:T(8,128)(2,1)S(1)}, u32[]{:S(2)}, u32[]{:S(2)}) collective-permute-start(bf16[5,16,128]{2,1,0:T(8,128)(2,1)S(1)} %get-tuple-element.83), channel_id=1, source_target_pairs={{0,8},{8,0},{16,24},{24,16},{32,40},{40,32},{48,56},{56,48},{64,72... | collective-permute-start | bytes 61448 | tf_op jit(solution)/shard_map/ppermute | solution.py:442
  30.3 2.6 %collective-permute-start.9 = (bf16[3,16,128]{2,1,0:T(8,128)(2,1)S(1)}, bf16[3,16,128]{2,1,0:T(8,128)(2,1)S(1)}, u32[]{:S(2)}, u32[]{:S(2)}) collective-permute-start(bf16[3,16,128]{2,1,0:T(8,128)(2,1)S(1)} %collective-permute-done.6.refs_2_), channel_id=1, source_target_pairs={{0,8},{8,0},{16,24},{24,16},{32,40},{40,32},{48,56},{56,48},{64,72... | collective-permute-start | bytes 36872 | tf_op jit(solution)/shard_map/ppermute | solution.py:449
  32.1 19.5 %collective-permute-start.14 = (bf16[4,14,16,128]{3,2,1,0:T(8,128)(2,1)S(1)}, bf16[4,14,16,128]{3,2,1,0:T(8,128)(2,1)S(1)}, u32[]{:S(2)}, u32[]{:S(2)}) collective-permute-start(bf16[4,14,16,128]{3,2,1,0:T(8,128)(2,1)S(1)} %inner_128_1.1.own_ref), channel_id=1, source_target_pairs={{0,2},{2,0},{4,6},{6,4},{1,3},{3,1},{5,7},{7,5},{8,10},{10,8},{12,... | collective-permute-start | bytes 688136 | tf_op jit(solution)/shard_map/ppermute | solution.py:455
  34.5 17.1 %collective-permute-start.15 = (bf16[4,14,16,128]{3,2,1,0:T(8,128)(2,1)S(1)}, bf16[4,14,16,128]{3,2,1,0:T(8,128)(2,1)S(1)}, u32[]{:S(2)}, u32[]{:S(2)}) collective-permute-start(bf16[4,14,16,128]{3,2,1,0:T(8,128)(2,1)S(1)} %collective-permute-done.5.three_ref), channel_id=1, source_target_pairs={{0,2},{2,0},{4,6},{6,4},{1,3},{3,1},{5,7},{7,5},{8,10},{10,8},{12,... | collective-permute-start | bytes 688136 | tf_op jit(solution)/shard_map/ppermute | solution.py:455
  35.1 4.9 %collective-permute-start.13 = (bf16[16,16,128]{2,1,0:T(8,128)(2,1)S(1)}, bf16[16,16,128]{2,1,0:T(8,128)(2,1)S(1)}, u32[]{:S(2)}, u32[]{:S(2)}) collective-permute-start(bf16[16,16,128]{2,1,0:T(8,128)(2,1)S(1)} %border_128_1.1.refs_3_.own_ref), channel_id=1, source_target_pairs={{0,6},{2,4},{4,2},{6,0},{1,7},{3,5},{5,3},{7,1},{8,14},{10,12},{12... | collective-permute-start | bytes 196616 | tf_op jit(solution)/shard_map/ppermute | solution.py:455
  35.6 9.1 %collective-permute-start.12 = (bf16[16,16,128]{2,1,0:T(8,128)(2,1)S(1)}, bf16[16,16,128]{2,1,0:T(8,128)(2,1)S(1)}, u32[]{:S(2)}, u32[]{:S(2)}) collective-permute-start(bf16[16,16,128]{2,1,0:T(8,128)(2,1)S(1)} %border_128_1.1.refs_3_.own_ref), channel_id=1, source_target_pairs={{0,4},{2,6},{4,0},{6,2},{1,5},{3,7},{5,1},{7,3},{8,12},{10,14},{12... | collective-permute-start | bytes 196616 | tf_op jit(solution)/shard_map/ppermute | solution.py:455
  38.0 8.5 %collective-permute-start.11 = (bf16[16,16,128]{2,1,0:T(8,128)(2,1)S(1)}, bf16[16,16,128]{2,1,0:T(8,128)(2,1)S(1)}, u32[]{:S(2)}, u32[]{:S(2)}) collective-permute-start(bf16[16,16,128]{2,1,0:T(8,128)(2,1)S(1)} %border_128_1.1.refs_3_.own_ref), channel_id=1, source_target_pairs={{0,2},{2,0},{4,6},{6,4},{1,3},{3,1},{5,7},{7,5},{8,10},{10,8},{12,... | collective-permute-start | bytes 196616 | tf_op jit(solution)/shard_map/ppermute | solution.py:455
  47.7 9.1 %collective-permute-start.16 = (bf16[3,16,512]{2,1,0:T(8,128)(2,1)S(1)}, bf16[3,16,512]{2,1,0:T(8,128)(2,1)S(1)}, u32[]{:S(2)}, u32[]{:S(2)}) collective-permute-start(bf16[3,16,512]{2,1,0:T(8,128)(2,1)S(1)} %get-tuple-element.90), channel_id=1, source_target_pairs={{0,16},{8,24},{16,0},{24,8},{32,48},{40,56},{48,32},{56,40},{64,80... | collective-permute-start | bytes 147464 | tf_op jit(solution)/shard_map/ppermute | solution.py:441
  47.7 9.1 %collective-permute-start.17 = (bf16[3,16,512]{2,1,0:T(8,128)(2,1)S(1)}, bf16[3,16,512]{2,1,0:T(8,128)(2,1)S(1)}, u32[]{:S(2)}, u32[]{:S(2)}) collective-permute-start(bf16[3,16,512]{2,1,0:T(8,128)(2,1)S(1)} %get-tuple-element.91), channel_id=1, source_target_pairs={{0,240},{8,248},{16,32},{24,40},{32,16},{40,24},{48,64},{56,72},{6... | collective-permute-start | bytes 147464 | tf_op jit(solution)/shard_map/ppermute | solution.py:440
  50.0 7.5 %collective-permute-start.18 = (bf16[5,16,512]{2,1,0:T(8,128)(2,1)S(1)}, bf16[5,16,512]{2,1,0:T(8,128)(2,1)S(1)}, u32[]{:S(2)}, u32[]{:S(2)}) collective-permute-start(bf16[5,16,512]{2,1,0:T(8,128)(2,1)S(1)} %get-tuple-element.98), channel_id=1, source_target_pairs={{0,8},{8,0},{16,24},{24,16},{32,40},{40,32},{48,56},{56,48},{64,72... | collective-permute-start | bytes 245768 | tf_op jit(solution)/shard_map/ppermute | solution.py:442
  56.9 1.3 %collective-permute-start.19 = (bf16[3,16,512]{2,1,0:T(8,128)(2,1)S(1)}, bf16[3,16,512]{2,1,0:T(8,128)(2,1)S(1)}, u32[]{:S(2)}, u32[]{:S(2)}) collective-permute-start(bf16[3,16,512]{2,1,0:T(8,128)(2,1)S(1)} %collective-permute-done.16.refs_2_), channel_id=1, source_target_pairs={{0,8},{8,0},{16,24},{24,16},{32,40},{40,32},{48,56},{56,48},{64,72... | collective-permute-start | bytes 147464 | tf_op jit(solution)/shard_map/ppermute | solution.py:449
  57.0 1.4 %collective-permute-start.20 = (bf16[3,16,512]{2,1,0:T(8,128)(2,1)S(1)}, bf16[3,16,512]{2,1,0:T(8,128)(2,1)S(1)}, u32[]{:S(2)}, u32[]{:S(2)}) collective-permute-start(bf16[3,16,512]{2,1,0:T(8,128)(2,1)S(1)} %collective-permute-done.17.refs_3_), channel_id=1, source_target_pairs={{0,8},{8,0},{16,24},{24,16},{32,40},{40,32},{48,56},{56,48},{64,72... | collective-permute-start | bytes 147464 | tf_op jit(solution)/shard_map/ppermute | solution.py:449
  60.5 8.5 %collective-permute-start.21 = (bf16[3,16,512]{2,1,0:T(8,128)(2,1)S(1)}, bf16[3,16,512]{2,1,0:T(8,128)(2,1)S(1)}, u32[]{:S(2)}, u32[]{:S(2)}) collective-permute-start(bf16[3,16,512]{2,1,0:T(8,128)(2,1)S(1)} %get-tuple-element.102), channel_id=1, source_target_pairs={{0,16},{8,24},{16,0},{24,8},{32,48},{40,56},{48,32},{56,40},{64,80... | collective-permute-start | bytes 147464 | tf_op jit(solution)/shard_map/ppermute | solution.py:441
  60.5 8.5 %collective-permute-start.22 = (bf16[3,16,512]{2,1,0:T(8,128)(2,1)S(1)}, bf16[3,16,512]{2,1,0:T(8,128)(2,1)S(1)}, u32[]{:S(2)}, u32[]{:S(2)}) collective-permute-start(bf16[3,16,512]{2,1,0:T(8,128)(2,1)S(1)} %get-tuple-element.103), channel_id=1, source_target_pairs={{0,240},{8,248},{16,32},{24,40},{32,16},{40,24},{48,64},{56,72},{6... | collective-permute-start | bytes 147464 | tf_op jit(solution)/shard_map/ppermute | solution.py:440
  63.5 6.1 %collective-permute-start.23 = (bf16[5,16,512]{2,1,0:T(8,128)(2,1)S(1)}, bf16[5,16,512]{2,1,0:T(8,128)(2,1)S(1)}, u32[]{:S(2)}, u32[]{:S(2)}) collective-permute-start(bf16[5,16,512]{2,1,0:T(8,128)(2,1)S(1)} %get-tuple-element.108), channel_id=1, source_target_pairs={{0,8},{8,0},{16,24},{24,16},{32,40},{40,32},{48,56},{56,48},{64,72... | collective-permute-start | bytes 245768 | tf_op jit(solution)/shard_map/ppermute | solution.py:442
  69.0 1.3 %collective-permute-start.24 = (bf16[3,16,512]{2,1,0:T(8,128)(2,1)S(1)}, bf16[3,16,512]{2,1,0:T(8,128)(2,1)S(1)}, u32[]{:S(2)}, u32[]{:S(2)}) collective-permute-start(bf16[3,16,512]{2,1,0:T(8,128)(2,1)S(1)} %collective-permute-done.21.refs_2_), channel_id=1, source_target_pairs={{0,8},{8,0},{16,24},{24,16},{32,40},{40,32},{48,56},{56,48},{64,72... | collective-permute-start | bytes 147464 | tf_op jit(solution)/shard_map/ppermute | solution.py:449
  69.1 1.4 %collective-permute-start.25 = (bf16[3,16,512]{2,1,0:T(8,128)(2,1)S(1)}, bf16[3,16,512]{2,1,0:T(8,128)(2,1)S(1)}, u32[]{:S(2)}, u32[]{:S(2)}) collective-permute-start(bf16[3,16,512]{2,1,0:T(8,128)(2,1)S(1)} %collective-permute-done.22.refs_3_), channel_id=1, source_target_pairs={{0,8},{8,0},{16,24},{24,16},{32,40},{40,32},{48,56},{56,48},{64,72... | collective-permute-start | bytes 147464 | tf_op jit(solution)/shard_map/ppermute | solution.py:449
  (2 other events, 2.4 us)

commit v2 on v1

--- a/solution.py
+++ b/solution.py
@@ -100,7 +100,7 @@
 
 
 def gelu(z):
-    return 0.5 * z * (1.0 + jnp.tanh(0.7978845608028654 * (z + 0.044715 * (z * z * z))))
+    return z * (0.5 + 0.5 * jnp.tanh(z * (0.7978845608028654 + 0.035677408136300125 * (z * z))))
 
 
 def copies(sems, *pairs):
@@ -149,8 +149,8 @@
         taken = jnp.int32(0)
         for strip in range(STRIPS):
             wanted = edges[strip % 4, target * HERE + strip // 4]
-            fits = jnp.logical_and(wanted // STRIPS == own, taken < capacity)
-            send[jnp.where(fits, start + taken, 8)] = wanted % STRIPS
+            fits = jnp.logical_and(wanted >> 4 == own, taken < capacity)
+            send[jnp.where(fits, start + taken, 8)] = wanted & 15
             taken = taken + fits.astype(I32)
     for slot in range(8):
         table_ref[slot] = send[slot]
@@ -185,7 +185,7 @@
         table_ref[2 * STRIPS + slot] = send_ref[slot]
     for strip in range(STRIPS):
         wanted = edges[strip % 4, own * HERE + strip // 4]
-        holder, place = wanted // STRIPS, wanted % STRIPS
+        holder, place = wanted >> 4, wanted & 15
         by_pair, by_near, mine = holder == paired, holder == near, holder == own
         by_far = jnp.logical_not(mine | by_pair | by_near)
         table_ref[strip] = jnp.where(
@@ -207,7 +207,7 @@
     for corner in range(STRIPS):
         wanted = cornered[corner % 4, own * HERE + corner // 4]
         safe = jnp.maximum(wanted, 0)
-        holder, place = safe // STRIPS, safe % STRIPS
+        holder, place = safe >> 4, safe & 15
         source = jnp.where(
             holder == own,
             0,
@@ -501,25 +501,27 @@
             (field, strips, weight, tiled, other),
         )
 
+    received, table = receive(sent, table)
+    inner_edge, *messages = border(False, True, strips, state_inner, received, narrow1)
+
+    sent = send(*messages)
     inner, inner_ring = interior(False, 1, state, strips, narrow1, inner_places)
-    received, inner, inner_ring = receive(sent, inner, inner_ring)
-    inner_edge, *messages = border(False, True, strips, state_inner, received, narrow1)
-
-    sent = send(*messages)
     (field,) = interior(True, 0, inner, inner_edge, narrow2, state)
+    received, inner_ring, field = receive(sent, inner_ring, field)
+    *received, field = lax.optimization_barrier((*received, field))
     one, three = from_level(field, 1), from_level(field, 3)
-    received, _ = receive(sent, field)
     (edge,) = border(True, False, inner_edge, inner_ring, received, narrow2, (strips,))
 
+    parts = [from_level(edge, d) for d in (2, 1, 3)]
     narrow3, narrow4, wide1, wide2, mix_in, mix_out = call(
         weights_kernel, "weights", [H] * 3 + [V], [V] * 6,
         arrays((1152, 128), (1152, 128), (2304, 256), (2304, 256), mix_in.shape, mix_out.shape),
         [pltpu.VMEM(conv_weight.shape[1:], BF16), pltpu.SemaphoreType.DMA((3,))],
         (conv_weight, mix_in, mix_out, edge),
     )
-    three, edge = lax.optimization_barrier((three, edge))
+    *parts, mix_in, three = lax.optimization_barrier((*parts, mix_in, three))
+    edge_parts = [edge, parts[1], parts[0], parts[2]]
     fields = [field, one, from_level(three, 1), three]
-    edge_parts = [edge] + [from_level(edge, d) for d in (1, 2, 3)]
     strips, *messages = call(
         functools.partial(mix_strips_kernel, 0), "mix_strips",
         [V] * 6 + [S, V], [V] * 4,
@@ -532,17 +534,17 @@
         [V] * 7, [V] * 2, arrays((HERE, INNER, SIDE, wide), strip_shape(wide)), [],
         (*fields, mix_in, mix_out, inner_places),
     )
+    received, ring1 = receive(sent, ring1)
+    inner_edge, *messages = border(False, True, strips, ring1, received, narrow3)
+
+    sent = send(*messages)
     inner, inner_ring = interior(False, 0, field, strips, wide1, inner_places)
-    received, inner, inner_ring = receive(sent, inner, inner_ring)
-    inner_edge, *messages = border(False, True, strips, ring1, received, narrow3)
-
-    sent = send(*messages)
     tiles = call(
         functools.partial(last_inner_kernel, 1), "last_inner",
         [V] * 7, V, arrays((HERE, INNER, SIDE, thin))[0], tile_scratch(wide),
         (inner, inner_edge, wide2, tiled, field, mix_in, mix_out),
     )
-    received, tiles = receive(sent, tiles)
+    received, tiles, inner_ring = receive(sent, tiles, inner_ring)
     return call(
         functools.partial(last_border_kernel, 1), "last_border",
         [V] * 7 + [S] + [V] * 7, V, arrays((HERE, SIDE, SIDE, thin))[0], border_scratch(wide),

time: 73.9 us -> 70 us (0.947)
  waiting for transfers between devices: 13.4 us -> 7.06 us
  starting transfers between devices: 31.6 us -> 34.4 us
    ppermute x4, starting transfers between devices: 14.9 us -> 19.1 us  [send(): from_far = lax.ppermute(far, 'face', apart)]
    ppermute x6, waiting for transfers between devices: 6.48 us -> 3.37 us  [from_level(): lax.ppermute(shard, 'level', [(i, i ^ distance) for i in range(levels)])]
    ppermute x4, waiting for transfers between devices: 3.1 us -> 0.01 us  [send(): from_far = lax.ppermute(far, 'face', apart)]
  transfers between devices with their start and end apart: 26 -> 26, of which waited for: 11 -> 10; matrix products, arithmetic and copies ran while one was open for 0% -> 0% of each run, Pallas kernels for 25% -> 28%
where the time goes in v2:
time: 70 us; the launch traced here: 69.9 us
  starting transfers between devices  34.4 us (49%)
  Pallas kernels  28.2 us (40%)
  waiting for transfers between devices  7.06 us (10%)
    pallas_call x13, Pallas kernels, call(): pl.pallas_call(kernel, name=name, in_specs=in_specs, out_specs=out_specs,...  28.2 us
    ppermute x4, starting transfers between devices, send(): from_far = lax.ppermute(far, 'face', apart)  19.1 us
    ppermute x6, starting transfers between devices, from_level(): lax.ppermute(shard, 'level', [(i, i ^ distance) for i in range(levels)])  5.83 us
    ppermute x4, starting transfers between devices, send(): lax.ppermute(to_pair, 'face', [(i, i ^ 1) for i in range(faces)])  3.65 us
    ppermute x6, waiting for transfers between devices, from_level(): lax.ppermute(shard, 'level', [(i, i ^ distance) for i in range(levels)])  3.37 us
    ppermute x4, waiting for transfers between devices, receive(): lax.ppermute(near, 'face', pairs)  2.82 us
    ppermute x4, starting transfers between devices, send(): from_near = lax.ppermute(near, 'face', [(i, i ^ 2) for i in range(faces)])  2.57 us
    ppermute x4, starting transfers between devices, receive(): lax.ppermute(near, 'face', pairs)  1.8 us
  transfers between devices with their start and end apart: 26, of which 10 were waited for; matrix products, arithmetic and copies ran while one was open for 0% of the time, Pallas kernels for 28%

profile of v2, /device:TPU:1, one launch (start us, length us, event | category | flops | bytes accessed | tf_op | source)
XLA Modules:
  0.0 69.9 jit_solution(14561634410901766344)
XLA Ops:
  0.0 1.8 %first.1 = (bf16[16,16,128]{2,1,0:T(8,128)(2,1)S(1)}, bf16[3,16,128]{2,1,0:T(8,128)(2,1)S(1)}, bf16[3,16,128]{2,1,0:T(8,128)(2,1)S(1)}, bf16[5,16,128]{2,1,0:T(8...) custom-call(bf16[4,16,16,128]{3,2,1,0:T(8,128)(2,1)} %state_ref.1, ...), custom_call_target="tpu_custom_call" | custom-call | tf_op jit(solution)/shard_map/first/pallas_call | solution.py:400
  1.8 2.6 %collective-permute-start = (bf16[3,16,128]{2,1,0:T(8,128)(2,1)S(1)}, bf16[3,16,128]{2,1,0:T(8,128)(2,1)S(1)}, u32[]{:S(2)}, u32[]{:S(2)}) collective-permute-start(bf16[3,16,128]{2,1,0:T(8,128)(2,1)S(1)} %get-tuple-element.72), channel_id=1, source_target_pairs={{0,16},{8,24},{16,0},{24,8},{32,48},{40,56},{48,32},{56,40},{64,80... | collective-permute-start | bytes 36872 | tf_op jit(solution)/shard_map/ppermute | solution.py:441
  4.3 7.3 %collective-permute-start.1 = (bf16[3,16,128]{2,1,0:T(8,128)(2,1)S(1)}, bf16[3,16,128]{2,1,0:T(8,128)(2,1)S(1)}, u32[]{:S(2)}, u32[]{:S(2)}) collective-permute-start(bf16[3,16,128]{2,1,0:T(8,128)(2,1)S(1)} %get-tuple-element.73), channel_id=1, source_target_pairs={{0,240},{8,248},{16,32},{24,40},{32,16},{40,24},{48,64},{56,72},{6... | collective-permute-start | bytes 36872 | tf_op jit(solution)/shard_map/ppermute | solution.py:440
  11.6 1.2 %collective-permute-start.2 = (bf16[5,16,128]{2,1,0:T(8,128)(2,1)S(1)}, bf16[5,16,128]{2,1,0:T(8,128)(2,1)S(1)}, u32[]{:S(2)}, u32[]{:S(2)}) collective-permute-start(bf16[5,16,128]{2,1,0:T(8,128)(2,1)S(1)} %get-tuple-element.77), channel_id=1, source_target_pairs={{0,8},{8,0},{16,24},{24,16},{32,40},{40,32},{48,56},{56,48},{64,72... | collective-permute-start | bytes 61448 | tf_op jit(solution)/shard_map/ppermute | solution.py:442
  12.8 2.4 %side.1 = (s32[40]{0:T(128)S(1)}, bf16[1152,128]{1,0:T(8,128)(2,1)S(1)}, bf16[1152,128]{1,0:T(8,128)(2,1)S(1)}, bf16[576,208]{1,0:T(8,128)(2,1)S(1)}, bf16[2,384...) custom-call(s32[4,128]{1,0:T(4,128)} %bitcast.3, s32[4,128]{1,0:T(4,128)} %bitcast.4, ...), custom_call_target="tpu_custom_call" | custom-call | tf_op jit(solution)/shard_map/side/pallas_call | solution.py:400
  16.8 1.4 %border_128_0.1 = (bf16[16,16,128]{2,1,0:T(8,128)(2,1)S(1)}, bf16[3,16,128]{2,1,0:T(8,128)(2,1)S(1)}, bf16[3,16,128]{2,1,0:T(8,128)(2,1)S(1)}, bf16[5,16,128]{2,1,0:T(8,128)(2,1)S(1)}) custom-call(bf16[16,16,128]{2,1,0:T(8,128)(2,1)S(1)} %get-tuple-element.68.refs_0_.strips_ref.refs_11_, bf16[16,16,128]{2,1,0:T(8,128)(2,1)S(1)} %get-tuple-element.71.refs_1_, ...), custom_call_target="tpu_custom_call" | custom-call | tf_op jit(solution)/shard_map/border_128_0/pallas_call | solution.py:400
  18.1 4.4 %collective-permute-start.6 = (bf16[3,16,128]{2,1,0:T(8,128)(2,1)S(1)}, bf16[3,16,128]{2,1,0:T(8,128)(2,1)S(1)}, u32[]{:S(2)}, u32[]{:S(2)}) collective-permute-start(bf16[3,16,128]{2,1,0:T(8,128)(2,1)S(1)} %get-tuple-element.84), channel_id=1, source_target_pairs={{0,240},{8,248},{16,32},{24,40},{32,16},{40,24},{48,64},{56,72},{6... | collective-permute-start | bytes 36872 | tf_op jit(solution)/shard_map/ppermute | solution.py:440
  23.0 1.7 %inner_128_0.1 = (bf16[4,14,16,128]{3,2,1,0:T(8,128)(2,1)S(1)}, bf16[16,16,128]{2,1,0:T(8,128)(2,1)S(1)}) custom-call(bf16[4,16,16,128]{3,2,1,0:T(8,128)(2,1)S(1)} %get-tuple-element.70.refs_7_.field_ref.other_ref, bf16[16,16,128]{2,1,0:T(8,128)(2,1)S(1)} %get-tuple-element.68.refs_0_.strips_ref.refs_11_, ...), custom_call_target="tpu_custom_call" | custom-call | tf_op jit(solution)/shard_map/inner_128_0/pallas_call | solution.py:400
  24.6 1.5 %inner_128_1.1.own_ref = bf16[4,14,16,128]{3,2,1,0:T(8,128)(2,1)S(1)} custom-call(bf16[4,14,16,128]{3,2,1,0:T(8,128)(2,1)S(1)} %get-tuple-element.88.field_ref, bf16[16,16,128]{2,1,0:T(8,128)(2,1)S(1)} %get-tuple-element.82.strips_ref.refs_0_, bf16[1152,128]{1,0:T(8,128)(2,1)S(1)} %get-tuple-element.89.weight_ref.refs_8_, ...), custom_call_target="tpu_custom_call" | custom-call | tf_op jit(solution)/shard_map/inner_128_1/pallas_call | solution.py:400
  27.6 2.5 %collective-permute-start.13 = (bf16[4,14,16,128]{3,2,1,0:T(8,128)(2,1)S(1)}, bf16[4,14,16,128]{3,2,1,0:T(8,128)(2,1)S(1)}, u32[]{:S(2)}, u32[]{:S(2)}) collective-permute-start(bf16[4,14,16,128]{3,2,1,0:T(8,128)(2,1)S(1)} %inner_128_1.1.own_ref), channel_id=1, source_target_pairs={{0,6},{2,4},{4,2},{6,0},{1,7},{3,5},{5,3},{7,1},{8,14},{10,12},{12... | collective-permute-start | bytes 688136 | tf_op jit(solution)/shard_map/ppermute | solution.py:455
  30.1 1.2 %border_128_1.1.refs_3_.own_ref = bf16[16,16,128]{2,1,0:T(8,128)(2,1)S(1)} custom-call(bf16[16,16,128]{2,1,0:T(8,128)(2,1)S(1)} %get-tuple-element.82.strips_ref.refs_0_, bf16[16,16,128]{2,1,0:T(8,128)(2,1)S(1)} %get-tuple-element.90.refs_1_, bf16[3,16,128]{2,1,0:T(8,128)(2,1)S(1)} %collective-permute-done.5.refs_2_, ...), custom_call_target="tpu_custom_call" | custom-call | tf_op jit(solution)/shard_map/border_128_1/pallas_call | solution.py:400
  32.1 2.5 %collective-permute-start.12 = (bf16[16,16,128]{2,1,0:T(8,128)(2,1)S(1)}, bf16[16,16,128]{2,1,0:T(8,128)(2,1)S(1)}, u32[]{:S(2)}, u32[]{:S(2)}) collective-permute-start(bf16[16,16,128]{2,1,0:T(8,128)(2,1)S(1)} %border_128_1.1.refs_3_.own_ref), channel_id=1, source_target_pairs={{0,6},{2,4},{4,2},{6,0},{1,7},{3,5},{5,3},{7,1},{8,14},{10,12},{12... | collective-permute-start | bytes 196616 | tf_op jit(solution)/shard_map/ppermute | solution.py:455
  34.6 1.7 %weights.1 = (bf16[1152,128]{1,0:T(8,128)(2,1)S(1)}, bf16[1152,128]{1,0:T(8,128)(2,1)S(1)}, bf16[2304,256]{1,0:T(8,128)(2,1)S(1)}, bf16[2304,256]{1,0:T(8,128)(2...) custom-call(bf16[2,2,9,64,64]{4,3,2,1,0:T(8,128)(2,1)} %refs_0_.1, ...), custom_call_target="tpu_custom_call" | custom-call | tf_op jit(solution)/shard_map/weights/pallas_call | solution.py:400
  36.3 2.2 %collective-permute-done.12.three_ref = bf16[16,16,128]{2,1,0:T(8,128)(2,1)S(1)} collective-permute-done((bf16[16,16,128]{2,1,0:T(8,128)(2,1)S(1)}, bf16[16,16,128]{2,1,0:T(8,128)(2,1)S(1)}, u32[]{:S(2)}, u32[]{:S(2)}) %collective-permute-start.12) | collective-permute-done | bytes 65568 | tf_op jit(solution)/shard_map/ppermute | solution.py:455
  38.6 1.3 %mix_strips.1 = (bf16[16,16,512]{2,1,0:T(8,128)(2,1)S(1)}, bf16[3,16,512]{2,1,0:T(8,128)(2,1)S(1)}, bf16[3,16,512]{2,1,0:T(8,128)(2,1)S(1)}, bf16[5,16,512]{2,1,0:T(8,128)(2,1)S(1)}) custom-call(bf16[16,16,128]{2,1,0:T(8,128)(2,1)S(1)} %border_128_1.1.refs_3_.own_ref, bf16[16,16,128]{2,1,0:T(8,128)(2,1)S(1)} %collective-permute-done.11.one_ref, ...), custom_call_target="tpu_custom_call" | custom-call | tf_op jit(solution)/shard_map/mix_strips/pallas_call | solution.py:400
  39.8 3.8 %collective-permute-start.15 = (bf16[3,16,512]{2,1,0:T(8,128)(2,1)S(1)}, bf16[3,16,512]{2,1,0:T(8,128)(2,1)S(1)}, u32[]{:S(2)}, u32[]{:S(2)}) collective-permute-start(bf16[3,16,512]{2,1,0:T(8,128)(2,1)S(1)} %get-tuple-element.109), channel_id=1, source_target_pairs={{0,240},{8,248},{16,32},{24,40},{32,16},{40,24},{48,64},{56,72},{6... | collective-permute-start | bytes 147464 | tf_op jit(solution)/shard_map/ppermute | solution.py:440
  43.6 1.5 %collective-permute-start.18 = (bf16[5,16,512]{2,1,0:T(8,128)(2,1)S(1)}, bf16[5,16,512]{2,1,0:T(8,128)(2,1)S(1)}, u32[]{:S(2)}, u32[]{:S(2)}) collective-permute-start(bf16[5,16,512]{2,1,0:T(8,128)(2,1)S(1)} %get-tuple-element.115), channel_id=1, source_target_pairs={{0,8},{8,0},{16,24},{24,16},{32,40},{40,32},{48,56},{56,48},{64,72... | collective-permute-start | bytes 245768 | tf_op jit(solution)/shard_map/ppermute | solution.py:442
  46.2 1.8 %mix_tiles.1 = (bf16[4,14,16,512]{3,2,1,0:T(8,128)(2,1)S(1)}, bf16[16,16,512]{2,1,0:T(8,128)(2,1)S(1)}) custom-call(bf16[4,14,16,128]{3,2,1,0:T(8,128)(2,1)S(1)} %inner_128_1.1.own_ref, bf16[4,14,16,128]{3,2,1,0:T(8,128)(2,1)S(1)} %collective-permute-done.16.one_ref, bf16[4,14,16,128]{3,2,1,0:T(8,128)(2,1)S(1)} %collective-permute-done.17.two_ref, ...), custom_call_target="tpu_custom_call" | custom-call | tf_op jit(solution)/shard_map/mix_tiles/pallas_call | solution.py:400
  48.1 1.4 %collective-permute-start.19 = (bf16[3,16,512]{2,1,0:T(8,128)(2,1)S(1)}, bf16[3,16,512]{2,1,0:T(8,128)(2,1)S(1)}, u32[]{:S(2)}, u32[]{:S(2)}) collective-permute-start(bf16[3,16,512]{2,1,0:T(8,128)(2,1)S(1)} %collective-permute-done.14.refs_2_), channel_id=1, source_target_pairs={{0,8},{8,0},{16,24},{24,16},{32,40},{40,32},{48,56},{56,48},{64,72... | collective-permute-start | bytes 147464 | tf_op jit(solution)/shard_map/ppermute | solution.py:449
  50.7 2.1 %border_512_0.1 = (bf16[16,16,512]{2,1,0:T(8,128)(2,1)S(1)}, bf16[3,16,512]{2,1,0:T(8,128)(2,1)S(1)}, bf16[3,16,512]{2,1,0:T(8,128)(2,1)S(1)}, bf16[5,16,512]{2,1,0:T(8,128)(2,1)S(1)}) custom-call(bf16[16,16,512]{2,1,0:T(8,128)(2,1)S(1)} %get-tuple-element.107.refs_0_.strips_ref.refs_10_, bf16[16,16,512]{2,1,0:T(8,128)(2,1)S(1)} %get-tuple-element.112.refs_1_, ...), custom_call_target="tpu_custom_call" | custom-call | tf_op jit(solution)/shard_map/border_512_0/pallas_call | solution.py:400
  52.9 3.7 %collective-permute-start.22 = (bf16[3,16,512]{2,1,0:T(8,128)(2,1)S(1)}, bf16[3,16,512]{2,1,0:T(8,128)(2,1)S(1)}, u32[]{:S(2)}, u32[]{:S(2)}) collective-permute-start(bf16[3,16,512]{2,1,0:T(8,128)(2,1)S(1)} %get-tuple-element.119), channel_id=1, source_target_pairs={{0,240},{8,248},{16,32},{24,40},{32,16},{40,24},{48,64},{56,72},{6... | collective-permute-start | bytes 147464 | tf_op jit(solution)/shard_map/ppermute | solution.py:440
  57.0 3.4 %inner_512_0.1 = (bf16[4,14,16,512]{3,2,1,0:T(8,128)(2,1)S(1)}, bf16[16,16,512]{2,1,0:T(8,128)(2,1)S(1)}) custom-call(bf16[4,14,16,512]{3,2,1,0:T(8,128)(2,1)S(1)} %get-tuple-element.120.field_ref.state_ref, bf16[16,16,512]{2,1,0:T(8,128)(2,1)S(1)} %get-tuple-element.107.refs_0_.strips_ref.refs_10_, bf16[2304,256]{1,0:T(8,128)(2,1)S(1)} %get-tuple-element.121.weight_ref, ...), custom_call_target="tpu_custom_call" | custom-call | tf_op jit(solution)/shard_map/inner_512_0/pallas_call | solution.py:400
  60.4 4.7 %last_inner.1.refs_13_ = bf16[4,14,16,128]{3,2,1,0:T(8,128)(2,1)S(1)} custom-call(bf16[4,14,16,512]{3,2,1,0:T(8,128)(2,1)S(1)} %get-tuple-element.122.field_ref, bf16[16,16,512]{2,1,0:T(8,128)(2,1)S(1)} %get-tuple-element.117.strips_ref.refs_0_, bf16[2304,256]{1,0:T(8,128)(2,1)S(1)} %get-tuple-element.123.weight_ref, ...), custom_call_target="tpu_custom_call" | custom-call | tf_op jit(solution)/shard_map/last_inner/pallas_call | solution.py:400
  66.6 3.3 %last_border.1 = bf16[4,16,16,128]{3,2,1,0:T(8,128)(2,1)} custom-call(bf16[16,16,512]{2,1,0:T(8,128)(2,1)S(1)} %get-tuple-element.117.strips_ref.refs_0_, bf16[16,16,512]{2,1,0:T(8,128)(2,1)S(1)} %get-tuple-element.125.refs_1_, bf16[3,16,512]{2,1,0:T(8,128)(2,1)S(1)} %collective-permute-done.21.refs_2_, ...), custom_call_target="tpu_custom_call" | custom-call | tf_op jit(solution)/shard_map/last_border/pallas_call | solution.py:400
  (41 shorter events, 8.5 us)
Async XLA Ops:
  1.8 13.5 %collective-permute-start = (bf16[3,16,128]{2,1,0:T(8,128)(2,1)S(1)}, bf16[3,16,128]{2,1,0:T(8,128)(2,1)S(1)}, u32[]{:S(2)}, u32[]{:S(2)}) collective-permute-start(bf16[3,16,128]{2,1,0:T(8,128)(2,1)S(1)} %get-tuple-element.72), channel_id=1, source_target_pairs={{0,16},{8,24},{16,0},{24,8},{32,48},{40,56},{48,32},{56,40},{64,80... | collective-permute-start | bytes 36872 | tf_op jit(solution)/shard_map/ppermute | solution.py:441
  4.3 11.0 %collective-permute-start.1 = (bf16[3,16,128]{2,1,0:T(8,128)(2,1)S(1)}, bf16[3,16,128]{2,1,0:T(8,128)(2,1)S(1)}, u32[]{:S(2)}, u32[]{:S(2)}) collective-permute-start(bf16[3,16,128]{2,1,0:T(8,128)(2,1)S(1)} %get-tuple-element.73), channel_id=1, source_target_pairs={{0,240},{8,248},{16,32},{24,40},{32,16},{40,24},{48,64},{56,72},{6... | collective-permute-start | bytes 36872 | tf_op jit(solution)/shard_map/ppermute | solution.py:440
  11.6 4.3 %collective-permute-start.2 = (bf16[5,16,128]{2,1,0:T(8,128)(2,1)S(1)}, bf16[5,16,128]{2,1,0:T(8,128)(2,1)S(1)}, u32[]{:S(2)}, u32[]{:S(2)}) collective-permute-start(bf16[5,16,128]{2,1,0:T(8,128)(2,1)S(1)} %get-tuple-element.77), channel_id=1, source_target_pairs={{0,8},{8,0},{16,24},{24,16},{32,40},{40,32},{48,56},{56,48},{64,72... | collective-permute-start | bytes 61448 | tf_op jit(solution)/shard_map/ppermute | solution.py:442
  15.3 1.3 %collective-permute-start.3 = (bf16[3,16,128]{2,1,0:T(8,128)(2,1)S(1)}, bf16[3,16,128]{2,1,0:T(8,128)(2,1)S(1)}, u32[]{:S(2)}, u32[]{:S(2)}) collective-permute-start(bf16[3,16,128]{2,1,0:T(8,128)(2,1)S(1)} %collective-permute-done.refs_2_), channel_id=1, source_target_pairs={{0,8},{8,0},{16,24},{24,16},{32,40},{40,32},{48,56},{56,48},{64,72... | collective-permute-start | bytes 36872 | tf_op jit(solution)/shard_map/ppermute | solution.py:449
  15.4 1.3 %collective-permute-start.4 = (bf16[3,16,128]{2,1,0:T(8,128)(2,1)S(1)}, bf16[3,16,128]{2,1,0:T(8,128)(2,1)S(1)}, u32[]{:S(2)}, u32[]{:S(2)}) collective-permute-start(bf16[3,16,128]{2,1,0:T(8,128)(2,1)S(1)} %collective-permute-done.1.refs_3_), channel_id=1, source_target_pairs={{0,8},{8,0},{16,24},{24,16},{32,40},{40,32},{48,56},{56,48},{64,72... | collective-permute-start | bytes 36872 | tf_op jit(solution)/shard_map/ppermute | solution.py:449
  18.1 8.0 %collective-permute-start.5 = (bf16[3,16,128]{2,1,0:T(8,128)(2,1)S(1)}, bf16[3,16,128]{2,1,0:T(8,128)(2,1)S(1)}, u32[]{:S(2)}, u32[]{:S(2)}) collective-permute-start(bf16[3,16,128]{2,1,0:T(8,128)(2,1)S(1)} %get-tuple-element.83), channel_id=1, source_target_pairs={{0,16},{8,24},{16,0},{24,8},{32,48},{40,56},{48,32},{56,40},{64,80... | collective-permute-start | bytes 36872 | tf_op jit(solution)/shard_map/ppermute | solution.py:441
  18.1 8.0 %collective-permute-start.6 = (bf16[3,16,128]{2,1,0:T(8,128)(2,1)S(1)}, bf16[3,16,128]{2,1,0:T(8,128)(2,1)S(1)}, u32[]{:S(2)}, u32[]{:S(2)}) collective-permute-start(bf16[3,16,128]{2,1,0:T(8,128)(2,1)S(1)} %get-tuple-element.84), channel_id=1, source_target_pairs={{0,240},{8,248},{16,32},{24,40},{32,16},{40,24},{48,64},{56,72},{6... | collective-permute-start | bytes 36872 | tf_op jit(solution)/shard_map/ppermute | solution.py:440
  22.5 4.2 %collective-permute-start.7 = (bf16[5,16,128]{2,1,0:T(8,128)(2,1)S(1)}, bf16[5,16,128]{2,1,0:T(8,128)(2,1)S(1)}, u32[]{:S(2)}, u32[]{:S(2)}) collective-permute-start(bf16[5,16,128]{2,1,0:T(8,128)(2,1)S(1)} %get-tuple-element.93), channel_id=1, source_target_pairs={{0,8},{8,0},{16,24},{24,16},{32,40},{40,32},{48,56},{56,48},{64,72... | collective-permute-start | bytes 61448 | tf_op jit(solution)/shard_map/ppermute | solution.py:442
  26.3 1.3 %collective-permute-start.9 = (bf16[3,16,128]{2,1,0:T(8,128)(2,1)S(1)}, bf16[3,16,128]{2,1,0:T(8,128)(2,1)S(1)}, u32[]{:S(2)}, u32[]{:S(2)}) collective-permute-start(bf16[3,16,128]{2,1,0:T(8,128)(2,1)S(1)} %collective-permute-done.6.refs_3_), channel_id=1, source_target_pairs={{0,8},{8,0},{16,24},{24,16},{32,40},{40,32},{48,56},{56,48},{64,72... | collective-permute-start | bytes 36872 | tf_op jit(solution)/shard_map/ppermute | solution.py:449
  27.6 11.0 %collective-permute-start.13 = (bf16[4,14,16,128]{3,2,1,0:T(8,128)(2,1)S(1)}, bf16[4,14,16,128]{3,2,1,0:T(8,128)(2,1)S(1)}, u32[]{:S(2)}, u32[]{:S(2)}) collective-permute-start(bf16[4,14,16,128]{3,2,1,0:T(8,128)(2,1)S(1)} %inner_128_1.1.own_ref), channel_id=1, source_target_pairs={{0,6},{2,4},{4,2},{6,0},{1,7},{3,5},{5,3},{7,1},{8,14},{10,12},{12... | collective-permute-start | bytes 688136 | tf_op jit(solution)/shard_map/ppermute | solution.py:455
  31.3 5.0 %collective-permute-start.10 = (bf16[16,16,128]{2,1,0:T(8,128)(2,1)S(1)}, bf16[16,16,128]{2,1,0:T(8,128)(2,1)S(1)}, u32[]{:S(2)}, u32[]{:S(2)}) collective-permute-start(bf16[16,16,128]{2,1,0:T(8,128)(2,1)S(1)} %border_128_1.1.refs_3_.own_ref), channel_id=1, source_target_pairs={{0,4},{2,6},{4,0},{6,2},{1,5},{3,7},{5,1},{7,3},{8,12},{10,14},{12... | collective-permute-start | bytes 196616 | tf_op jit(solution)/shard_map/ppermute | solution.py:455
  31.9 4.4 %collective-permute-start.11 = (bf16[16,16,128]{2,1,0:T(8,128)(2,1)S(1)}, bf16[16,16,128]{2,1,0:T(8,128)(2,1)S(1)}, u32[]{:S(2)}, u32[]{:S(2)}) collective-permute-start(bf16[16,16,128]{2,1,0:T(8,128)(2,1)S(1)} %border_128_1.1.refs_3_.own_ref), channel_id=1, source_target_pairs={{0,2},{2,0},{4,6},{6,4},{1,3},{3,1},{5,7},{7,5},{8,10},{10,8},{12,... | collective-permute-start | bytes 196616 | tf_op jit(solution)/shard_map/ppermute | solution.py:455
  32.1 6.4 %collective-permute-start.12 = (bf16[16,16,128]{2,1,0:T(8,128)(2,1)S(1)}, bf16[16,16,128]{2,1,0:T(8,128)(2,1)S(1)}, u32[]{:S(2)}, u32[]{:S(2)}) collective-permute-start(bf16[16,16,128]{2,1,0:T(8,128)(2,1)S(1)} %border_128_1.1.refs_3_.own_ref), channel_id=1, source_target_pairs={{0,6},{2,4},{4,2},{6,0},{1,7},{3,5},{5,3},{7,1},{8,14},{10,12},{12... | collective-permute-start | bytes 196616 | tf_op jit(solution)/shard_map/ppermute | solution.py:455
  34.6 10.5 %collective-permute-start.16 = (bf16[4,14,16,128]{3,2,1,0:T(8,128)(2,1)S(1)}, bf16[4,14,16,128]{3,2,1,0:T(8,128)(2,1)S(1)}, u32[]{:S(2)}, u32[]{:S(2)}) collective-permute-start(bf16[4,14,16,128]{3,2,1,0:T(8,128)(2,1)S(1)} %inner_128_1.1.own_ref), channel_id=1, source_target_pairs={{0,2},{2,0},{4,6},{6,4},{1,3},{3,1},{5,7},{7,5},{8,10},{10,8},{12,... | collective-permute-start | bytes 688136 | tf_op jit(solution)/shard_map/ppermute | solution.py:455
  38.5 7.7 %collective-permute-start.17 = (bf16[4,14,16,128]{3,2,1,0:T(8,128)(2,1)S(1)}, bf16[4,14,16,128]{3,2,1,0:T(8,128)(2,1)S(1)}, u32[]{:S(2)}, u32[]{:S(2)}) collective-permute-start(bf16[4,14,16,128]{3,2,1,0:T(8,128)(2,1)S(1)} %collective-permute-done.13.three_ref), channel_id=1, source_target_pairs={{0,2},{2,0},{4,6},{6,4},{1,3},{3,1},{5,7},{7,5},{8,10},{10,8},{12,... | collective-permute-start | bytes 688136 | tf_op jit(solution)/shard_map/ppermute | solution.py:455
  39.8 8.3 %collective-permute-start.14 = (bf16[3,16,512]{2,1,0:T(8,128)(2,1)S(1)}, bf16[3,16,512]{2,1,0:T(8,128)(2,1)S(1)}, u32[]{:S(2)}, u32[]{:S(2)}) collective-permute-start(bf16[3,16,512]{2,1,0:T(8,128)(2,1)S(1)} %get-tuple-element.108), channel_id=1, source_target_pairs={{0,16},{8,24},{16,0},{24,8},{32,48},{40,56},{48,32},{56,40},{64,80... | collective-permute-start | bytes 147464 | tf_op jit(solution)/shard_map/ppermute | solution.py:441
  39.8 8.3 %collective-permute-start.15 = (bf16[3,16,512]{2,1,0:T(8,128)(2,1)S(1)}, bf16[3,16,512]{2,1,0:T(8,128)(2,1)S(1)}, u32[]{:S(2)}, u32[]{:S(2)}) collective-permute-start(bf16[3,16,512]{2,1,0:T(8,128)(2,1)S(1)} %get-tuple-element.109), channel_id=1, source_target_pairs={{0,240},{8,248},{16,32},{24,40},{32,16},{40,24},{48,64},{56,72},{6... | collective-permute-start | bytes 147464 | tf_op jit(solution)/shard_map/ppermute | solution.py:440
  43.6 6.0 %collective-permute-start.18 = (bf16[5,16,512]{2,1,0:T(8,128)(2,1)S(1)}, bf16[5,16,512]{2,1,0:T(8,128)(2,1)S(1)}, u32[]{:S(2)}, u32[]{:S(2)}) collective-permute-start(bf16[5,16,512]{2,1,0:T(8,128)(2,1)S(1)} %get-tuple-element.115), channel_id=1, source_target_pairs={{0,8},{8,0},{16,24},{24,16},{32,40},{40,32},{48,56},{56,48},{64,72... | collective-permute-start | bytes 245768 | tf_op jit(solution)/shard_map/ppermute | solution.py:442
  48.1 2.3 %collective-permute-start.19 = (bf16[3,16,512]{2,1,0:T(8,128)(2,1)S(1)}, bf16[3,16,512]{2,1,0:T(8,128)(2,1)S(1)}, u32[]{:S(2)}, u32[]{:S(2)}) collective-permute-start(bf16[3,16,512]{2,1,0:T(8,128)(2,1)S(1)} %collective-permute-done.14.refs_2_), channel_id=1, source_target_pairs={{0,8},{8,0},{16,24},{24,16},{32,40},{40,32},{48,56},{56,48},{64,72... | collective-permute-start | bytes 147464 | tf_op jit(solution)/shard_map/ppermute | solution.py:449
  52.9 12.3 %collective-permute-start.21 = (bf16[3,16,512]{2,1,0:T(8,128)(2,1)S(1)}, bf16[3,16,512]{2,1,0:T(8,128)(2,1)S(1)}, u32[]{:S(2)}, u32[]{:S(2)}) collective-permute-start(bf16[3,16,512]{2,1,0:T(8,128)(2,1)S(1)} %get-tuple-element.118), channel_id=1, source_target_pairs={{0,16},{8,24},{16,0},{24,8},{32,48},{40,56},{48,32},{56,40},{64,80... | collective-permute-start | bytes 147464 | tf_op jit(solution)/shard_map/ppermute | solution.py:441
  52.9 12.3 %collective-permute-start.22 = (bf16[3,16,512]{2,1,0:T(8,128)(2,1)S(1)}, bf16[3,16,512]{2,1,0:T(8,128)(2,1)S(1)}, u32[]{:S(2)}, u32[]{:S(2)}) collective-permute-start(bf16[3,16,512]{2,1,0:T(8,128)(2,1)S(1)} %get-tuple-element.119), channel_id=1, source_target_pairs={{0,240},{8,248},{16,32},{24,40},{32,16},{40,24},{48,64},{56,72},{6... | collective-permute-start | bytes 147464 | tf_op jit(solution)/shard_map/ppermute | solution.py:440
  56.6 9.2 %collective-permute-start.23 = (bf16[5,16,512]{2,1,0:T(8,128)(2,1)S(1)}, bf16[5,16,512]{2,1,0:T(8,128)(2,1)S(1)}, u32[]{:S(2)}, u32[]{:S(2)}) collective-permute-start(bf16[5,16,512]{2,1,0:T(8,128)(2,1)S(1)} %get-tuple-element.128), channel_id=1, source_target_pairs={{0,8},{8,0},{16,24},{24,16},{32,40},{40,32},{48,56},{56,48},{64,72... | collective-permute-start | bytes 245768 | tf_op jit(solution)/shard_map/ppermute | solution.py:442
  65.2 1.3 %collective-permute-start.24 = (bf16[3,16,512]{2,1,0:T(8,128)(2,1)S(1)}, bf16[3,16,512]{2,1,0:T(8,128)(2,1)S(1)}, u32[]{:S(2)}, u32[]{:S(2)}) collective-permute-start(bf16[3,16,512]{2,1,0:T(8,128)(2,1)S(1)} %collective-permute-done.21.refs_2_), channel_id=1, source_target_pairs={{0,8},{8,0},{16,24},{24,16},{32,40},{40,32},{48,56},{56,48},{64,72... | collective-permute-start | bytes 147464 | tf_op jit(solution)/shard_map/ppermute | solution.py:449
  65.3 1.3 %collective-permute-start.25 = (bf16[3,16,512]{2,1,0:T(8,128)(2,1)S(1)}, bf16[3,16,512]{2,1,0:T(8,128)(2,1)S(1)}, u32[]{:S(2)}, u32[]{:S(2)}) collective-permute-start(bf16[3,16,512]{2,1,0:T(8,128)(2,1)S(1)} %collective-permute-done.22.refs_3_), channel_id=1, source_target_pairs={{0,8},{8,0},{16,24},{24,16},{32,40},{40,32},{48,56},{56,48},{64,72... | collective-permute-start | bytes 147464 | tf_op jit(solution)/shard_map/ppermute | solution.py:449
  (2 other events, 2.5 us)

commit v3 on v2

--- a/solution.py
+++ b/solution.py
@@ -67,22 +67,42 @@
     return one_hot(columns, 3 * BORDER + SIDE)
 
 
-def tile_table():
-    outer, half = ring(0), INNER // 2
+STARTS = 0, 3, 7, 10
+
+
+def known_rows(group, paired):
+    outer, places = ring(0), {}
+    for tile in range(2):
+        for (i, j), place in outer.items():
+            places[tile, i, j] = 2 * BORDER + BORDER * tile + place
+        for row in range(4):
+            for j in range(1, SIDE - 1):
+                i = STARTS[group] + row + 1
+                if 1 <= i < SIDE - 1:
+                    apart = BORDER * (j % 2) + SIDE * row + 8 * tile + j // 2
+                    places[tile, i, j] = apart if paired else BORDER * tile + SIDE * row + j
+    return places
+
+
+def tile_table(paired):
     groups = []
-    for group in range(2):
-        columns = []
-        for b in range(3):
-            for i in range(SIDE // 2 * group, SIDE // 2 * (group + 1)):
-                for j in range(SIDE):
-                    column = j + b - 1
-                    if column < 0 or column >= SIDE:
-                        columns.append(None)
-                    elif (i, column) in outer:
-                        columns.append(half * SIDE + outer[i, column])
-                    else:
-                        columns.append((i - 1 - half * group) * SIDE + column)
-        groups.append(one_hot(columns, half * SIDE + BORDER))
+    for group in range(4):
+        places, columns = known_rows(group, paired), []
+        for shift in range(4):
+            for i in range(4 * group, 4 * group + 4):
+                for tile in range(2):
+                    columns += [places.get((tile, i, 2 * n + shift - 1)) for n in range(8)]
+        groups.append(one_hot(columns, 4 * BORDER))
+    return np.stack(groups)
+
+
+def merge_table():
+    groups = []
+    for group in range(4):
+        places = known_rows(group, True)
+        rows = range(4 * group, 4 * group + 4)
+        columns = [places[tile, i, j] for tile in range(2) for i in rows for j in range(SIDE)]
+        groups.append(one_hot(columns, 4 * BORDER))
     return np.stack(groups)
 
 
@@ -93,6 +113,17 @@
             i, j = strip_pixel(side, k, 1)
             columns.append((i - 1) * SIDE + j if 1 <= k < SIDE - 1 else None)
     return one_hot(columns, INNER * SIDE)
+
+
+def paired_inner_table():
+    columns = []
+    for tile in range(2):
+        for side in range(4):
+            for k in range(SIDE):
+                i, j = strip_pixel(side, k, 1)
+                place = INNER * SIDE * (j % 2) + SIDE * (i - 1) + 8 * tile + j // 2
+                columns.append(place if 1 <= k < SIDE - 1 else None)
+    return one_hot(columns, 2 * INNER * SIDE)
 
 
 def dot(a, b):
@@ -163,20 +194,22 @@
 
 
 def side_kernel(faces, *refs):
-    edge_ref, corner_ref, conv_ref, border_ref, tile_ref, inner_ref, send_ref, state_ref = refs[:8]
-    table_ref, narrow1_ref, narrow2_ref, border_held, tile_held, inner_held, strips_ref = refs[8:15]
-    edges, cornered, conv, sems = refs[15:]
+    edge_ref, corner_ref, conv_ref, border_ref, plain_ref, tile_ref, inner_ref, ring_ref, send_ref, state_ref = refs[:10]
+    table_ref, narrow1_ref, narrow2_ref, wide1_ref, wide2_ref, border_held, plain_held, tile_held, inner_held, strips_ref = refs[10:20]
+    edges, cornered, conv, ring_held, sems = refs[20:]
     started = copies(
         sems,
         (edge_ref, edges),
         (corner_ref, cornered),
         (conv_ref.at[0], conv),
+        (ring_ref, ring_held),
+        (border_ref, border_held),
+        (plain_ref, plain_held),
+        (tile_ref, tile_held),
         (inner_ref, inner_held),
-        (border_ref, border_held),
-        (tile_ref, tile_held),
-    )
-    for narrow in (narrow1_ref, narrow2_ref):
-        narrow[...] = jnp.zeros_like(narrow)
+    )
+    for weight in (narrow1_ref, narrow2_ref, wide1_ref, wide2_ref):
+        weight[...] = jnp.zeros_like(weight)
     own, paired, near, far = neighbours(faces)
     from_pair, from_near, from_far = jnp.int32(0), jnp.int32(0), jnp.int32(0)
     for copy in started[:4]:
@@ -218,18 +251,25 @@
             ),
         )
         table_ref[STRIPS + corner] = jnp.where(wanted < 0, ZERO_ROW, source * STRIPS + place)
-    for layer, narrow in enumerate((narrow1_ref, narrow2_ref)):
-        spread(conv, layer, narrow)
-    inner_strips(state_ref, 1, inner_held, strips_ref)
+    for layer, (narrow, wide) in enumerate(((narrow1_ref, wide1_ref), (narrow2_ref, wide2_ref))):
+        spread(conv, layer, narrow, wide)
+    features = state_ref.shape[-1]
+    for tile in range(HERE):
+        rows = state_ref[tile, 1 : 1 + INNER].reshape(INNER * SIDE, features)
+        strips_ref[4 * tile : 4 * tile + 4] = dot(ring_held[...], rows).astype(BF16).reshape(4, SIDE, features)
     for copy in started[4:]:
         copy.wait()
 
 
-def spread(conv, layer, weight):
-    width = weight.shape[-1]
-    for tap in range(9):
-        for level in range(width // 64):
-            weight[pl.ds(width * tap + 64 * level, 64), pl.ds(64 * level, 64)] = conv[layer, tap]
+def spread(conv, layer, narrow, wide):
+    for a in range(3):
+        for b in range(3):
+            tap = conv[layer, 3 * a + b]
+            for level in range(2):
+                lanes = 64 * level
+                narrow[pl.ds(128 * (3 * a + b) + lanes, 64), pl.ds(lanes, 64)] = tap
+                for parity in range(2):
+                    wide[pl.ds(128 * (4 * a + b + parity) + lanes, 64), pl.ds(128 * parity + lanes, 64)] = tap
 
 
 def weights_kernel(*refs):
@@ -238,19 +278,17 @@
     for weight in (narrow1_ref, narrow2_ref, wide1_ref, wide2_ref):
         weight[...] = jnp.zeros_like(weight)
     started[0].wait()
-    for layer, weights in enumerate(((narrow1_ref, wide1_ref), (narrow2_ref, wide2_ref))):
-        for weight in weights:
-            spread(conv, layer, weight)
+    for layer, (narrow, wide) in enumerate(((narrow1_ref, wide1_ref), (narrow2_ref, wide2_ref))):
+        spread(conv, layer, narrow, wide)
     for copy in started[1:]:
         copy.wait()
 
 
-def inner_strips(field_ref, top, inner_ref, strips_ref):
+def inner_strips(field_ref, inner_ref, strips_ref):
     features = field_ref.shape[-1]
-    for tile in range(HERE):
-        rows = field_ref[tile, top : top + INNER].reshape(INNER * SIDE, features)
-        strips = dot(inner_ref[...], rows).astype(BF16)
-        strips_ref[4 * tile : 4 * tile + 4] = strips.reshape(4, SIDE, features)
+    for pair in range(HERE // 2):
+        strips = dot(inner_ref[...], field_ref[pair].reshape(2 * INNER * SIDE, features)).astype(BF16)
+        strips_ref[8 * pair : 8 * pair + 8] = strips.reshape(8, SIDE, features)
 
 
 def gather_rims(received, strips_ref, inner_ref, table_ref, held, corners, row, known):
@@ -308,31 +346,47 @@
         address(out_ref, table_ref.at[pl.ds(2 * STRIPS, 8)], *messages, corners_ref)
 
 
-def tile_conv(field_ref, top, strips_ref, weight_ref, tile_ref, shifted, tile):
-    features, width = field_ref.shape[-1], weight_ref.shape[-1]
-    strips = strips_ref[4 * tile : 4 * tile + 4].reshape(BORDER, features)
-    half, rows = SIDE // 2, INNER // 2
-    for group in range(2):
-        inner = field_ref[tile, top + rows * group : top + rows * (group + 1)].reshape(rows * SIDE, features)
-        moved = dot(tile_ref[group], jnp.concatenate([inner, strips], 0)).astype(BF16)
-        shifted[:, half * group : half * (group + 1)] = moved.reshape(3, half, SIDE, features)
-    for group in range(features // width):
-        lanes = slice(width * group, width * (group + 1))
-        windows = [shifted[b, a : a + INNER, :, lanes].reshape(INNER * SIDE, width) for a in range(3) for b in range(3)]
+def tile_conv(field_ref, strips_ref, weight_ref, tile_ref, shifted, pair):
+    features = strips_ref.shape[-1]
+    strips = strips_ref[8 * pair : 8 * pair + 8].reshape(2 * BORDER, features)
+    for group, start in enumerate(STARTS):
+        if field_ref.shape[0] == HERE:
+            rows = [field_ref[2 * pair + tile, start + 1 : start + 5] for tile in range(2)]
+        else:
+            rows = [field_ref[pair, parity, start : start + 4] for parity in range(2)]
+        known = jnp.concatenate([part.reshape(BORDER, features) for part in rows] + [strips], 0)
+        moved = dot(tile_ref[group], known).astype(BF16)
+        shifted[:, 4 * group : 4 * group + 4] = moved.reshape(4, 4, SIDE, features)
+    for group in range(features // 128):
+        lanes = slice(128 * group, 128 * (group + 1))
+        windows = [shifted[c, a : a + INNER, :, lanes].reshape(INNER * SIDE, 128) for a in range(3) for c in range(4)]
         yield lanes, dot(jnp.concatenate(windows, 1), weight_ref[...])
 
 
-def inner_kernel(last, top, field_ref, strips_ref, weight_ref, tile_ref, other_ref, out_ref, *rest):
-    shifted = rest[-1]
-    for tile in range(HERE):
-        for lanes, total in tile_conv(field_ref, top, strips_ref, weight_ref, tile_ref, shifted.at[tile], tile):
-            if last:
-                total = total + other_ref[tile, 1 : 1 + INNER, :, lanes].reshape(total.shape).astype(F32)
-            else:
-                total = gelu(total)
-            out_ref[tile, :, :, lanes] = total.astype(BF16).reshape(INNER, SIDE, -1)
-    if not last:
-        inner_strips(out_ref, 0, other_ref, rest[0])
+def columns_of(total, parity):
+    return total[:, 128 * parity : 128 * (parity + 1)]
+
+
+def inner_kernel(field_ref, strips_ref, weight_ref, tile_ref, inner_ref, out_ref, ring_ref, *rest):
+    *kept, shifted = rest
+    for pair in range(HERE // 2):
+        window = shifted.at[pair]
+        for lanes, total in tile_conv(field_ref, strips_ref, weight_ref, tile_ref, window, pair):
+            total = gelu(total).astype(BF16)
+            for parity in range(2):
+                out_ref[pair, parity, :, :, lanes] = columns_of(total, parity).reshape(INNER, SIDE, 128)
+        for ref in kept:
+            ref[pair] = window[1:3, 1 : 1 + INNER]
+    inner_strips(out_ref, inner_ref, ring_ref)
+
+
+def second_inner_kernel(field_ref, strips_ref, weight_ref, tile_ref, state_ref, out_ref, shifted):
+    for pair in range(HERE // 2):
+        for lanes, total in tile_conv(field_ref, strips_ref, weight_ref, tile_ref, shifted.at[pair], pair):
+            for parity in range(2):
+                before = state_ref[pair, parity, :, :, lanes].reshape(INNER * SIDE, 128)
+                after = (columns_of(total, parity) + before.astype(F32)).astype(BF16)
+                out_ref[pair, parity, :, :, lanes] = after.reshape(INNER, SIDE, 128)
 
 
 def mixer(block, level, mix_in_ref, mix_out_ref, outs):
@@ -356,39 +410,44 @@
     address(strips_ref, table_ref.at[pl.ds(2 * STRIPS, 8)], near_ref, far_ref, pair_ref, corners_ref)
 
 
-def mix_tiles_kernel(block, own_ref, one_ref, two_ref, three_ref, mix_in_ref, mix_out_ref, inner_ref, out_ref, strips_ref):
+def mix_tiles_kernel(block, own_ref, one_ref, two_ref, three_ref, mix_in_ref, mix_out_ref, inner_ref, out_ref, ring_ref):
     mix = mixer(block, lax.axis_index("level"), mix_in_ref, mix_out_ref, 4)
-    for tile in range(HERE):
-        column = jnp.concatenate([ref[tile].reshape(INNER * SIDE, 128) for ref in (own_ref, one_ref, two_ref, three_ref)], 1)
-        out_ref[tile] = mix(column).reshape(INNER, SIDE, 512)
-    inner_strips(out_ref, 0, inner_ref, strips_ref)
+    for pair in range(HERE // 2):
+        for parity in range(2):
+            parts = [ref[pair, parity].reshape(INNER * SIDE, 128) for ref in (own_ref, one_ref, two_ref, three_ref)]
+            out_ref[pair, parity] = mix(jnp.concatenate(parts, 1)).reshape(INNER, SIDE, 512)
+    inner_strips(out_ref, inner_ref, ring_ref)
 
 
 def last_inner_kernel(block, field_ref, strips_ref, weight_ref, tile_ref, state_ref, mix_in_ref, mix_out_ref, out_ref, shifted):
     mix = mixer(block, lax.axis_index("level"), mix_in_ref, mix_out_ref, 1)
-    for tile in range(HERE):
-        columns = []
-        for lanes, total in tile_conv(field_ref, 0, strips_ref, weight_ref, tile_ref, shifted.at[tile], tile):
-            columns.append((total + state_ref[tile, :, :, lanes].reshape(total.shape).astype(F32)).astype(BF16))
-        out_ref[tile] = mix(jnp.concatenate(columns, 1)).reshape(INNER, SIDE, 128)
+    for pair in range(HERE // 2):
+        columns = [], []
+        for lanes, total in tile_conv(field_ref, strips_ref, weight_ref, tile_ref, shifted.at[pair], pair):
+            for parity in range(2):
+                before = state_ref[pair, parity, :, :, lanes].reshape(INNER * SIDE, 128)
+                columns[parity].append((columns_of(total, parity) + before.astype(F32)).astype(BF16))
+        for parity in range(2):
+            mixed = mix(jnp.concatenate(columns[parity], 1))
+            out_ref[pair, parity] = mixed.reshape(INNER, SIDE, 128)
 
 
 def last_border_kernel(block, *refs):
     strips_ref, inner_ref, *received = refs[:7]
-    table_ref, weight_ref, border_ref, state_ref, mix_in_ref, mix_out_ref, tiles_ref, tile_ref, out_ref = refs[7:16]
+    table_ref, weight_ref, border_ref, state_ref, mix_in_ref, mix_out_ref, tiles_ref, merge_ref, out_ref = refs[7:16]
     mix = mixer(block, lax.axis_index("level"), mix_in_ref, mix_out_ref, 1)
     columns = []
     for lanes, total in border_conv(received, strips_ref, inner_ref, table_ref, weight_ref, border_ref, refs[16:]):
         columns.append((total + state_ref[:, :, lanes].reshape(total.shape).astype(F32)).astype(BF16))
     mixed = mix(jnp.concatenate(columns, 1))
-    half, rows = SIDE // 2, INNER // 2
-    for tile in range(HERE):
-        strips = mixed[BORDER * tile : BORDER * (tile + 1)]
-        for group in range(2):
-            inner = tiles_ref[tile, rows * group : rows * (group + 1)].reshape(rows * SIDE, 128)
-            place = tile_ref[group, half * SIDE : 2 * half * SIDE]
-            merged = dot(place, jnp.concatenate([inner, strips], 0)).astype(BF16)
-            out_ref[tile, half * group : half * (group + 1)] = merged.reshape(half, SIDE, 128)
+    for pair in range(HERE // 2):
+        strips = mixed[2 * BORDER * pair : 2 * BORDER * (pair + 1)]
+        for group, start in enumerate(STARTS):
+            rows = [tiles_ref[pair, parity, start : start + 4].reshape(BORDER, 128) for parity in range(2)]
+            merged = dot(merge_ref[group], jnp.concatenate(rows + [strips], 0)).astype(BF16)
+            merged = merged.reshape(2, 4, SIDE, 128)
+            for tile in range(2):
+                out_ref[2 * pair + tile, 4 * group : 4 * group + 4] = merged[tile]
 
 
 V = pl.BlockSpec(memory_space=pltpu.VMEM)
@@ -416,6 +475,10 @@
     return STRIPS, SIDE, features
 
 
+def tiles_shape(features):
+    return HERE // 2, 2, INNER, SIDE, features
+
+
 def message_shapes(features):
     return (3, SIDE, features), (3, SIDE, features), (5, SIDE, features)
 
@@ -431,7 +494,7 @@
 
 
 def tile_scratch(features):
-    return [pltpu.VMEM((HERE, 3, SIDE, SIDE, features), BF16)]
+    return [pltpu.VMEM((HERE // 2, 4, SIDE, SIDE, features), BF16)]
 
 
 def send(near, far, to_pair):
@@ -442,12 +505,12 @@
     return from_near, from_far, lax.ppermute(to_pair, "face", [(i, i ^ 1) for i in range(faces)])
 
 
-def receive(sent, *beside):
-    near, far, paired = sent
-    near, far, *beside = lax.optimization_barrier((near, far, *beside))
+def receive(sent, beside_near, beside_far):
+    near, *beside_near = lax.optimization_barrier((sent[0], *beside_near))
+    far, *beside_far = lax.optimization_barrier((sent[1], *beside_far))
     pairs = [(i, i ^ 1) for i in range(lax.axis_size("face"))]
-    arrived = near, far, paired, lax.ppermute(near, "face", pairs), lax.ppermute(far, "face", pairs)
-    return arrived, *beside
+    arrived = near, far, sent[2], lax.ppermute(near, "face", pairs), lax.ppermute(far, "face", pairs)
+    return arrived, *beside_near, *beside_far
 
 
 def from_level(shard, distance):
@@ -459,7 +522,8 @@
     faces = lax.axis_size("face")
     thin = state.shape[-1]
     wide = 4 * thin
-    border_hbm, tile_hbm, inner_hbm = (jnp.asarray(t) for t in (border_table(), tile_table(), inner_table()))
+    tables = border_table(), tile_table(False), tile_table(True), paired_inner_table(), inner_table()
+    border_hbm, plain_hbm, tile_hbm, inner_hbm, ring_hbm = (jnp.asarray(t) for t in tables)
     edges, cornered = edge_source.T, corner_source.T
     edge_scratch = pltpu.SMEM(edges.shape, I32)
 
@@ -473,13 +537,20 @@
         (state, edges),
     )
     sent = send(*messages)
-    table, narrow1, narrow2, borders, tiled, inner_places, state_inner = call(
+    shape_w = (1152, 128), (1152, 128), (1536, 256), (1536, 256)
+    table, narrow1, narrow2, wide1, wide2, borders, plain, tiled, inner_places, state_inner = call(
         functools.partial(side_kernel, faces), "side",
-        [H] * 6 + [S, V], [S] + [V] * 6,
+        [H] * 8 + [S, V], [S] + [V] * 9,
         [jax.ShapeDtypeStruct((2 * STRIPS + 8,), I32)]
-        + arrays((1152, 128), (1152, 128), border_hbm.shape, tile_hbm.shape, inner_hbm.shape, strip_shape(thin)),
-        [edge_scratch, edge_scratch, pltpu.VMEM(conv_weight.shape[1:], BF16), pltpu.SemaphoreType.DMA((6,))],
-        (edges, cornered, conv_weight, border_hbm, tile_hbm, inner_hbm, sends, state),
+        + arrays(*shape_w, border_hbm.shape, plain_hbm.shape, tile_hbm.shape, inner_hbm.shape, strip_shape(thin)),
+        [
+            edge_scratch,
+            edge_scratch,
+            pltpu.VMEM(conv_weight.shape[1:], BF16),
+            pltpu.VMEM(ring_hbm.shape, BF16),
+            pltpu.SemaphoreType.DMA((8,)),
+        ],
+        (edges, cornered, conv_weight, border_hbm, plain_hbm, tile_hbm, inner_hbm, ring_hbm, sends, state),
     )
 
     def border(last, sending, strips, inner_strips, received, weight, residual=()):
@@ -492,22 +563,25 @@
             (strips, inner_strips, *received, table, weight, borders, corners, *residual),
         )
 
-    def interior(last, top, field, strips, weight, other):
+    def interior(field, strips, weight, table, keep=False):
         size = field.shape[-1]
-        shapes = [(HERE, INNER, SIDE, size)] + ([] if last else [strip_shape(size)])
+        shapes = [tiles_shape(size), strip_shape(size)] + ([tiles_shape(size)] if keep else [])
         return call(
-            functools.partial(inner_kernel, last, top), f"inner_{size}_{int(last)}",
+            inner_kernel, f"inner_{size}",
             [V] * 5, [V] * len(shapes), arrays(*shapes), tile_scratch(size),
-            (field, strips, weight, tiled, other),
+            (field, strips, weight, table, inner_places),
         )
 
-    received, table = receive(sent, table)
+    received, table = receive(sent, (), (table,))
     inner_edge, *messages = border(False, True, strips, state_inner, received, narrow1)
 
     sent = send(*messages)
-    inner, inner_ring = interior(False, 1, state, strips, narrow1, inner_places)
-    (field,) = interior(True, 0, inner, inner_edge, narrow2, state)
-    received, inner_ring, field = receive(sent, inner_ring, field)
+    inner, inner_ring, before = interior(state, strips, wide1, plain, True)
+    (field,) = call(
+        second_inner_kernel, "inner_second", [V] * 5, [V], arrays(tiles_shape(thin)), tile_scratch(thin),
+        (inner, inner_edge, wide2, tiled, before),
+    )
+    received, inner_ring, field = receive(sent, (inner_ring,), (field,))
     *received, field = lax.optimization_barrier((*received, field))
     one, three = from_level(field, 1), from_level(field, 3)
     (edge,) = border(True, False, inner_edge, inner_ring, received, narrow2, (strips,))
@@ -515,7 +589,7 @@
     parts = [from_level(edge, d) for d in (2, 1, 3)]
     narrow3, narrow4, wide1, wide2, mix_in, mix_out = call(
         weights_kernel, "weights", [H] * 3 + [V], [V] * 6,
-        arrays((1152, 128), (1152, 128), (2304, 256), (2304, 256), mix_in.shape, mix_out.shape),
+        arrays(*shape_w, mix_in.shape, mix_out.shape),
         [pltpu.VMEM(conv_weight.shape[1:], BF16), pltpu.SemaphoreType.DMA((3,))],
         (conv_weight, mix_in, mix_out, edge),
     )
@@ -531,24 +605,24 @@
     sent = send(*messages)
     field, ring1 = call(
         functools.partial(mix_tiles_kernel, 0), "mix_tiles",
-        [V] * 7, [V] * 2, arrays((HERE, INNER, SIDE, wide), strip_shape(wide)), [],
+        [V] * 7, [V] * 2, arrays(tiles_shape(wide), strip_shape(wide)), [],
         (*fields, mix_in, mix_out, inner_places),
     )
-    received, ring1 = receive(sent, ring1)
+    received, ring1 = receive(sent, (), (ring1,))
     inner_edge, *messages = border(False, True, strips, ring1, received, narrow3)
 
     sent = send(*messages)
-    inner, inner_ring = interior(False, 0, field, strips, wide1, inner_places)
+    inner, inner_ring = interior(field, strips, wide1, tiled)
     tiles = call(
         functools.partial(last_inner_kernel, 1), "last_inner",
-        [V] * 7, V, arrays((HERE, INNER, SIDE, thin))[0], tile_scratch(wide),
+        [V] * 7, V, arrays(tiles_shape(thin))[0], tile_scratch(wide),
         (inner, inner_edge, wide2, tiled, field, mix_in, mix_out),
     )
-    received, tiles, inner_ring = receive(sent, tiles, inner_ring)
+    received, inner_ring, tiles = receive(sent, (inner_ring,), (tiles,))
     return call(
         functools.partial(last_border_kernel, 1), "last_border",
         [V] * 7 + [S] + [V] * 7, V, arrays((HERE, SIDE, SIDE, thin))[0], border_scratch(wide),
-        (inner_edge, inner_ring, *received, table, narrow4, borders, strips, mix_in, mix_out, tiles, tiled),
+        (inner_edge, inner_ring, *received, table, narrow4, borders, strips, mix_in, mix_out, tiles, jnp.asarray(merge_table())),
     )
 
 

time: 70 us -> 67 us (0.957)
  Pallas kernels: 28.2 us -> 25.3 us
  starting transfers between devices: 34.4 us -> 32.5 us
  waiting for transfers between devices: 7.06 us -> 8.79 us
    ppermute x4, starting transfers between devices: 19.1 us -> 15.8 us  [send(): from_far = lax.ppermute(far, 'face', apart)]
    pallas_call x13, Pallas kernels: 28.2 us -> 25.3 us  [call(): pl.pallas_call(kernel, name=name, in_specs=in_specs, out_specs=out_specs,...]
    ppermute x4, starting transfers between devices: 1.8 us -> 4.63 us  [receive(): lax.ppermute(near, 'face', pairs)]
    ppermute x4, starting transfers between devices: 2.57 us -> 0.98 us  [send(): from_near = lax.ppermute(near, 'face', [(i, i ^ 2) for i in range(faces)])]
    ppermute x4, waiting for transfers between devices: 0.01 us -> 1.24 us  [send(): from_far = lax.ppermute(far, 'face', apart)]
    ppermute x4, waiting for transfers between devices: 0.84 us -> 1.72 us  [receive(): lax.ppermute(far, 'face', pairs)]
  transfers between devices with their start and end apart: 26 -> 26, of which waited for: 10 -> 10; matrix products, arithmetic and copies ran while one was open for 0% -> 0% of each run, Pallas kernels for 28% -> 25%
where the time goes in v3:
time: 67 us; the launch traced here: 66.8 us
  starting transfers between devices  32.5 us (49%)
  Pallas kernels  25.3 us (38%)
  waiting for transfers between devices  8.79 us (13%)
    pallas_call x13, Pallas kernels, call(): pl.pallas_call(kernel, name=name, in_specs=in_specs, out_specs=out_specs,...  25.3 us
    ppermute x4, starting transfers between devices, send(): from_far = lax.ppermute(far, 'face', apart)  15.8 us
    ppermute x6, starting transfers between devices, from_level(): lax.ppermute(shard, 'level', [(i, i ^ distance) for i in range(levels)])  5.82 us
    ppermute x4, starting transfers between devices, receive(): lax.ppermute(near, 'face', pairs)  4.63 us
    ppermute x4, starting transfers between devices, send(): lax.ppermute(to_pair, 'face', [(i, i ^ 1) for i in range(faces)])  3.55 us
    ppermute x6, waiting for transfers between devices, from_level(): lax.ppermute(shard, 'level', [(i, i ^ distance) for i in range(levels)])  3.44 us
    ppermute x4, waiting for transfers between devices, receive(): lax.ppermute(near, 'face', pairs)  2.37 us
    ppermute x4, starting transfers between devices, receive(): lax.ppermute(far, 'face', pairs)  1.79 us
  transfers between devices with their start and end apart: 26, of which 10 were waited for; matrix products, arithmetic and copies ran while one was open for 0% of the time, Pallas kernels for 25%

profile of v3, /device:TPU:1, one launch (start us, length us, event | category | flops | bytes accessed | tf_op | source)
XLA Modules:
  0.0 66.8 jit_solution(4030283952148803971)
XLA Ops:
  0.0 1.8 %first.1 = (bf16[16,16,128]{2,1,0:T(8,128)(2,1)S(1)}, bf16[3,16,128]{2,1,0:T(8,128)(2,1)S(1)}, bf16[3,16,128]{2,1,0:T(8,128)(2,1)S(1)}, bf16[5,16,128]{2,1,0:T(8...) custom-call(bf16[4,16,16,128]{3,2,1,0:T(8,128)(2,1)} %state_ref.1, ...), custom_call_target="tpu_custom_call" | custom-call | tf_op jit(solution)/shard_map/first/pallas_call | solution.py:459
  1.8 9.1 %collective-permute-start.1 = (bf16[3,16,128]{2,1,0:T(8,128)(2,1)S(1)}, bf16[3,16,128]{2,1,0:T(8,128)(2,1)S(1)}, u32[]{:S(2)}, u32[]{:S(2)}) collective-permute-start(bf16[3,16,128]{2,1,0:T(8,128)(2,1)S(1)} %get-tuple-element.75), channel_id=1, source_target_pairs={{0,240},{8,248},{16,32},{24,40},{32,16},{40,24},{48,64},{56,72},{6... | collective-permute-start | bytes 36872 | tf_op jit(solution)/shard_map/ppermute | solution.py:503
  11.8 2.6 %side.1 = (s32[40]{0:T(128)S(1)}, bf16[1152,128]{1,0:T(8,128)(2,1)S(1)}, bf16[1152,128]{1,0:T(8,128)(2,1)S(1)}, bf16[1536,256]{1,0:T(8,128)(2,1)S(1)}, bf16[1536...) custom-call(s32[4,128]{1,0:T(4,128)} %bitcast.3, ...), custom_call_target="tpu_custom_call" | custom-call | tf_op jit(solution)/shard_map/side/pallas_call | solution.py:459
  16.7 1.4 %border_128_0.1 = (bf16[16,16,128]{2,1,0:T(8,128)(2,1)S(1)}, bf16[3,16,128]{2,1,0:T(8,128)(2,1)S(1)}, bf16[3,16,128]{2,1,0:T(8,128)(2,1)S(1)}, bf16[5,16,128]{2,1,0:T(8,128)(2,1)S(1)}) custom-call(bf16[16,16,128]{2,1,0:T(8,128)(2,1)S(1)} %get-tuple-element.70.refs_0_.strips_ref.refs_11_, bf16[16,16,128]{2,1,0:T(8,128)(2,1)S(1)} %get-tuple-element.73.refs_1_, ...), custom_call_target="tpu_custom_call" | custom-call | tf_op jit(solution)/shard_map/border_128_0/pallas_call | solution.py:459
  19.0 2.5 %collective-permute-start.6 = (bf16[3,16,128]{2,1,0:T(8,128)(2,1)S(1)}, bf16[3,16,128]{2,1,0:T(8,128)(2,1)S(1)}, u32[]{:S(2)}, u32[]{:S(2)}) collective-permute-start(bf16[3,16,128]{2,1,0:T(8,128)(2,1)S(1)} %get-tuple-element.91), channel_id=1, source_target_pairs={{0,240},{8,248},{16,32},{24,40},{32,16},{40,24},{48,64},{56,72},{6... | collective-permute-start | bytes 36872 | tf_op jit(solution)/shard_map/ppermute | solution.py:503
  22.0 1.2 %inner_128.1 = (bf16[2,2,14,16,128]{4,3,2,1,0:T(8,128)(2,1)S(1)}, bf16[16,16,128]{2,1,0:T(8,128)(2,1)S(1)}, bf16[2,2,14,16,128]{4,3,2,1,0:T(8,128)(2,1)S(1)}) custom-call(bf16[4,16,16,128]{3,2,1,0:T(8,128)(2,1)S(1)} %get-tuple-element.72.refs_9_.field_ref, bf16[16,16,128]{2,1,0:T(8,128)(2,1)S(1)} %get-tuple-element.70.refs_0_.strips_ref.refs_11_, ...), custom_call_target="tpu_custom_call" | custom-call | tf_op jit(solution)/shard_map/inner_128/pallas_call | solution.py:459
  24.0 1.2 %collective-permute-done.6.refs_3_ = bf16[3,16,128]{2,1,0:T(8,128)(2,1)S(1)} collective-permute-done((bf16[3,16,128]{2,1,0:T(8,128)(2,1)S(1)}, bf16[3,16,128]{2,1,0:T(8,128)(2,1)S(1)}, u32[]{:S(2)}, u32[]{:S(2)}) %collective-permute-start.6) | collective-permute-done | bytes 12320 | tf_op jit(solution)/shard_map/ppermute | solution.py:503
  25.2 1.8 %collective-permute-start.8 = (bf16[3,16,128]{2,1,0:T(8,128)(2,1)S(1)}, bf16[3,16,128]{2,1,0:T(8,128)(2,1)S(1)}, u32[]{:S(2)}, u32[]{:S(2)}) collective-permute-start(bf16[3,16,128]{2,1,0:T(8,128)(2,1)S(1)} %collective-permute-done.5.refs_2_), channel_id=1, source_target_pairs={{0,8},{8,0},{16,24},{24,16},{32,40},{40,32},{48,56},{56,48},{64,72... | collective-permute-start | bytes 36872 | tf_op jit(solution)/shard_map/ppermute | solution.py:512
  28.2 2.5 %collective-permute-start.13 = (bf16[2,2,14,16,128]{4,3,2,1,0:T(8,128)(2,1)S(1)}, bf16[2,2,14,16,128]{4,3,2,1,0:T(8,128)(2,1)S(1)}, u32[]{:S(2)}, u32[]{:S(2)}) collective-permute-start(bf16[2,2,14,16,128]{4,3,2,1,0:T(8,128)(2,1)S(1)} %inner_second.1.own_ref), channel_id=1, source_target_pairs={{0,6},{2,4},{4,2},{6,0},{1,7},{3,5},{5,3},{7,1},{8,14},{10,12},{12... | collective-permute-start | bytes 688136 | tf_op jit(solution)/shard_map/ppermute | solution.py:518
  30.6 1.2 %border_128_1.1.refs_3_.own_ref = bf16[16,16,128]{2,1,0:T(8,128)(2,1)S(1)} custom-call(bf16[16,16,128]{2,1,0:T(8,128)(2,1)S(1)} %get-tuple-element.83.strips_ref.refs_0_, bf16[16,16,128]{2,1,0:T(8,128)(2,1)S(1)} %get-tuple-element.89.refs_1_, bf16[3,16,128]{2,1,0:T(8,128)(2,1)S(1)} %collective-permute-done.5.refs_2_, ...), custom_call_target="tpu_custom_call" | custom-call | tf_op jit(solution)/shard_map/border_128_1/pallas_call | solution.py:459
  32.7 2.5 %collective-permute-start.12 = (bf16[16,16,128]{2,1,0:T(8,128)(2,1)S(1)}, bf16[16,16,128]{2,1,0:T(8,128)(2,1)S(1)}, u32[]{:S(2)}, u32[]{:S(2)}) collective-permute-start(bf16[16,16,128]{2,1,0:T(8,128)(2,1)S(1)} %border_128_1.1.refs_3_.own_ref), channel_id=1, source_target_pairs={{0,6},{2,4},{4,2},{6,0},{1,7},{3,5},{5,3},{7,1},{8,14},{10,12},{12... | collective-permute-start | bytes 196616 | tf_op jit(solution)/shard_map/ppermute | solution.py:518
  35.2 1.7 %weights.1 = (bf16[1152,128]{1,0:T(8,128)(2,1)S(1)}, bf16[1152,128]{1,0:T(8,128)(2,1)S(1)}, bf16[1536,256]{1,0:T(8,128)(2,1)S(1)}, bf16[1536,256]{1,0:T(8,128)(2...) custom-call(bf16[2,2,9,64,64]{4,3,2,1,0:T(8,128)(2,1)} %refs_0_.1, ...), custom_call_target="tpu_custom_call" | custom-call | tf_op jit(solution)/shard_map/weights/pallas_call | solution.py:459
  36.9 2.3 %collective-permute-done.12.three_ref = bf16[16,16,128]{2,1,0:T(8,128)(2,1)S(1)} collective-permute-done((bf16[16,16,128]{2,1,0:T(8,128)(2,1)S(1)}, bf16[16,16,128]{2,1,0:T(8,128)(2,1)S(1)}, u32[]{:S(2)}, u32[]{:S(2)}) %collective-permute-start.12) | collective-permute-done | bytes 65568 | tf_op jit(solution)/shard_map/ppermute | solution.py:518
  39.2 1.3 %mix_strips.1 = (bf16[16,16,512]{2,1,0:T(8,128)(2,1)S(1)}, bf16[3,16,512]{2,1,0:T(8,128)(2,1)S(1)}, bf16[3,16,512]{2,1,0:T(8,128)(2,1)S(1)}, bf16[5,16,512]{2,1,0:T(8,128)(2,1)S(1)}) custom-call(bf16[16,16,128]{2,1,0:T(8,128)(2,1)S(1)} %border_128_1.1.refs_3_.own_ref, bf16[16,16,128]{2,1,0:T(8,128)(2,1)S(1)} %collective-permute-done.11.one_ref, ...), custom_call_target="tpu_custom_call" | custom-call | tf_op jit(solution)/shard_map/mix_strips/pallas_call | solution.py:459
  40.5 2.1 %collective-permute-start.14 = (bf16[3,16,512]{2,1,0:T(8,128)(2,1)S(1)}, bf16[3,16,512]{2,1,0:T(8,128)(2,1)S(1)}, u32[]{:S(2)}, u32[]{:S(2)}) collective-permute-start(bf16[3,16,512]{2,1,0:T(8,128)(2,1)S(1)} %get-tuple-element.113), channel_id=1, source_target_pairs={{0,240},{8,248},{16,32},{24,40},{32,16},{40,24},{48,64},{56,72},{6... | collective-permute-start | bytes 147464 | tf_op jit(solution)/shard_map/ppermute | solution.py:503
  42.6 1.5 %collective-permute-start.18 = (bf16[5,16,512]{2,1,0:T(8,128)(2,1)S(1)}, bf16[5,16,512]{2,1,0:T(8,128)(2,1)S(1)}, u32[]{:S(2)}, u32[]{:S(2)}) collective-permute-start(bf16[5,16,512]{2,1,0:T(8,128)(2,1)S(1)} %get-tuple-element.119), channel_id=1, source_target_pairs={{0,8},{8,0},{16,24},{24,16},{32,40},{40,32},{48,56},{56,48},{64,72... | collective-permute-start | bytes 245768 | tf_op jit(solution)/shard_map/ppermute | solution.py:505
  44.1 1.7 %collective-permute-start.19 = (bf16[3,16,512]{2,1,0:T(8,128)(2,1)S(1)}, bf16[3,16,512]{2,1,0:T(8,128)(2,1)S(1)}, u32[]{:S(2)}, u32[]{:S(2)}) collective-permute-start(bf16[3,16,512]{2,1,0:T(8,128)(2,1)S(1)} %collective-permute-done.17.refs_2_), channel_id=1, source_target_pairs={{0,8},{8,0},{16,24},{24,16},{32,40},{40,32},{48,56},{56,48},{64,72... | collective-permute-start | bytes 147464 | tf_op jit(solution)/shard_map/ppermute | solution.py:512
  46.9 1.8 %mix_tiles.1 = (bf16[2,2,14,16,512]{4,3,2,1,0:T(8,128)(2,1)S(1)}, bf16[16,16,512]{2,1,0:T(8,128)(2,1)S(1)}) custom-call(bf16[2,2,14,16,128]{4,3,2,1,0:T(8,128)(2,1)S(1)} %inner_second.1.own_ref, bf16[2,2,14,16,128]{4,3,2,1,0:T(8,128)(2,1)S(1)} %collective-permute-done.15.one_ref, bf16[2,2,14,16,128]{4,3,2,1,0:T(8,128)(2,1)S(1)} %collective-permute-done.16.two_ref, ...), custom_call_target="tpu_custom_call" | custom-call | tf_op jit(solution)/shard_map/mix_tiles/pallas_call | solution.py:459
  48.8 1.3 %collective-permute-start.20 = (bf16[3,16,512]{2,1,0:T(8,128)(2,1)S(1)}, bf16[3,16,512]{2,1,0:T(8,128)(2,1)S(1)}, u32[]{:S(2)}, u32[]{:S(2)}) collective-permute-start(bf16[3,16,512]{2,1,0:T(8,128)(2,1)S(1)} %collective-permute-done.14.refs_3_), channel_id=1, source_target_pairs={{0,8},{8,0},{16,24},{24,16},{32,40},{40,32},{48,56},{56,48},{64,72... | collective-permute-start | bytes 147464 | tf_op jit(solution)/shard_map/ppermute | solution.py:512
  50.9 2.2 %border_512_0.1 = (bf16[16,16,512]{2,1,0:T(8,128)(2,1)S(1)}, bf16[3,16,512]{2,1,0:T(8,128)(2,1)S(1)}, bf16[3,16,512]{2,1,0:T(8,128)(2,1)S(1)}, bf16[5,16,512]{2,1,0:T(8,128)(2,1)S(1)}) custom-call(bf16[16,16,512]{2,1,0:T(8,128)(2,1)S(1)} %get-tuple-element.112.refs_0_.strips_ref.refs_10_, bf16[16,16,512]{2,1,0:T(8,128)(2,1)S(1)} %get-tuple-element.116.refs_1_, ...), custom_call_target="tpu_custom_call" | custom-call | tf_op jit(solution)/shard_map/border_512_0/pallas_call | solution.py:459
  53.1 2.1 %collective-permute-start.22 = (bf16[3,16,512]{2,1,0:T(8,128)(2,1)S(1)}, bf16[3,16,512]{2,1,0:T(8,128)(2,1)S(1)}, u32[]{:S(2)}, u32[]{:S(2)}) collective-permute-start(bf16[3,16,512]{2,1,0:T(8,128)(2,1)S(1)} %get-tuple-element.128), channel_id=1, source_target_pairs={{0,240},{8,248},{16,32},{24,40},{32,16},{40,24},{48,64},{56,72},{6... | collective-permute-start | bytes 147464 | tf_op jit(solution)/shard_map/ppermute | solution.py:503
  55.8 2.6 %inner_512.1 = (bf16[2,2,14,16,512]{4,3,2,1,0:T(8,128)(2,1)S(1)}, bf16[16,16,512]{2,1,0:T(8,128)(2,1)S(1)}) custom-call(bf16[2,2,14,16,512]{4,3,2,1,0:T(8,128)(2,1)S(1)} %get-tuple-element.123.field_ref.state_ref, bf16[16,16,512]{2,1,0:T(8,128)(2,1)S(1)} %get-tuple-element.112.refs_0_.strips_ref.refs_10_, ...), custom_call_target="tpu_custom_call" | custom-call | tf_op jit(solution)/shard_map/inner_512/pallas_call | solution.py:459
  58.5 3.5 %last_inner.1.refs_13_ = bf16[2,2,14,16,128]{4,3,2,1,0:T(8,128)(2,1)S(1)} custom-call(bf16[2,2,14,16,512]{4,3,2,1,0:T(8,128)(2,1)S(1)} %get-tuple-element.129.field_ref, bf16[16,16,512]{2,1,0:T(8,128)(2,1)S(1)} %get-tuple-element.121.strips_ref.refs_0_, bf16[1536,256]{1,0:T(8,128)(2,1)S(1)} %get-tuple-element.130.weight_ref, ...), custom_call_target="tpu_custom_call" | custom-call | tf_op jit(solution)/shard_map/last_inner/pallas_call | solution.py:459
  63.5 3.3 %last_border.1 = bf16[4,16,16,128]{3,2,1,0:T(8,128)(2,1)} custom-call(bf16[16,16,512]{2,1,0:T(8,128)(2,1)S(1)} %get-tuple-element.121.strips_ref.refs_0_, bf16[16,16,512]{2,1,0:T(8,128)(2,1)S(1)} %get-tuple-element.126.refs_1_, bf16[3,16,512]{2,1,0:T(8,128)(2,1)S(1)} %collective-permute-done.21.refs_2_, ...), custom_call_target="tpu_custom_call" | custom-call | tf_op jit(solution)/shard_map/last_border/pallas_call | solution.py:459
  (43 shorter events, 11.6 us)
Async XLA Ops:
  1.8 12.7 %collective-permute-start.1 = (bf16[3,16,128]{2,1,0:T(8,128)(2,1)S(1)}, bf16[3,16,128]{2,1,0:T(8,128)(2,1)S(1)}, u32[]{:S(2)}, u32[]{:S(2)}) collective-permute-start(bf16[3,16,128]{2,1,0:T(8,128)(2,1)S(1)} %get-tuple-element.75), channel_id=1, source_target_pairs={{0,240},{8,248},{16,32},{24,40},{32,16},{40,24},{48,64},{56,72},{6... | collective-permute-start | bytes 36872 | tf_op jit(solution)/shard_map/ppermute | solution.py:503
  10.9 3.6 %collective-permute-start = (bf16[3,16,128]{2,1,0:T(8,128)(2,1)S(1)}, bf16[3,16,128]{2,1,0:T(8,128)(2,1)S(1)}, u32[]{:S(2)}, u32[]{:S(2)}) collective-permute-start(bf16[3,16,128]{2,1,0:T(8,128)(2,1)S(1)} %get-tuple-element.74), channel_id=1, source_target_pairs={{0,16},{8,24},{16,0},{24,8},{32,48},{40,56},{48,32},{56,40},{64,80... | collective-permute-start | bytes 36872 | tf_op jit(solution)/shard_map/ppermute | solution.py:504
  10.9 4.7 %collective-permute-start.2 = (bf16[5,16,128]{2,1,0:T(8,128)(2,1)S(1)}, bf16[5,16,128]{2,1,0:T(8,128)(2,1)S(1)}, u32[]{:S(2)}, u32[]{:S(2)}) collective-permute-start(bf16[5,16,128]{2,1,0:T(8,128)(2,1)S(1)} %get-tuple-element.78), channel_id=1, source_target_pairs={{0,8},{8,0},{16,24},{24,16},{32,40},{40,32},{48,56},{56,48},{64,72... | collective-permute-start | bytes 61448 | tf_op jit(solution)/shard_map/ppermute | solution.py:505
  14.5 1.9 %collective-permute-start.3 = (bf16[3,16,128]{2,1,0:T(8,128)(2,1)S(1)}, bf16[3,16,128]{2,1,0:T(8,128)(2,1)S(1)}, u32[]{:S(2)}, u32[]{:S(2)}) collective-permute-start(bf16[3,16,128]{2,1,0:T(8,128)(2,1)S(1)} %collective-permute-done.refs_2_), channel_id=1, source_target_pairs={{0,8},{8,0},{16,24},{24,16},{32,40},{40,32},{48,56},{56,48},{64,72... | collective-permute-start | bytes 36872 | tf_op jit(solution)/shard_map/ppermute | solution.py:512
  18.1 5.9 %collective-permute-start.5 = (bf16[3,16,128]{2,1,0:T(8,128)(2,1)S(1)}, bf16[3,16,128]{2,1,0:T(8,128)(2,1)S(1)}, u32[]{:S(2)}, u32[]{:S(2)}) collective-permute-start(bf16[3,16,128]{2,1,0:T(8,128)(2,1)S(1)} %get-tuple-element.84), channel_id=1, source_target_pairs={{0,16},{8,24},{16,0},{24,8},{32,48},{40,56},{48,32},{56,40},{64,80... | collective-permute-start | bytes 36872 | tf_op jit(solution)/shard_map/ppermute | solution.py:504
  19.0 6.2 %collective-permute-start.6 = (bf16[3,16,128]{2,1,0:T(8,128)(2,1)S(1)}, bf16[3,16,128]{2,1,0:T(8,128)(2,1)S(1)}, u32[]{:S(2)}, u32[]{:S(2)}) collective-permute-start(bf16[3,16,128]{2,1,0:T(8,128)(2,1)S(1)} %get-tuple-element.91), channel_id=1, source_target_pairs={{0,240},{8,248},{16,32},{24,40},{32,16},{40,24},{48,64},{56,72},{6... | collective-permute-start | bytes 36872 | tf_op jit(solution)/shard_map/ppermute | solution.py:503
  21.5 5.5 %collective-permute-start.7 = (bf16[5,16,128]{2,1,0:T(8,128)(2,1)S(1)}, bf16[5,16,128]{2,1,0:T(8,128)(2,1)S(1)}, u32[]{:S(2)}, u32[]{:S(2)}) collective-permute-start(bf16[5,16,128]{2,1,0:T(8,128)(2,1)S(1)} %get-tuple-element.97), channel_id=1, source_target_pairs={{0,8},{8,0},{16,24},{24,16},{32,40},{40,32},{48,56},{56,48},{64,72... | collective-permute-start | bytes 61448 | tf_op jit(solution)/shard_map/ppermute | solution.py:505
  25.2 2.6 %collective-permute-start.8 = (bf16[3,16,128]{2,1,0:T(8,128)(2,1)S(1)}, bf16[3,16,128]{2,1,0:T(8,128)(2,1)S(1)}, u32[]{:S(2)}, u32[]{:S(2)}) collective-permute-start(bf16[3,16,128]{2,1,0:T(8,128)(2,1)S(1)} %collective-permute-done.5.refs_2_), channel_id=1, source_target_pairs={{0,8},{8,0},{16,24},{24,16},{32,40},{40,32},{48,56},{56,48},{64,72... | collective-permute-start | bytes 36872 | tf_op jit(solution)/shard_map/ppermute | solution.py:512
  28.2 11.1 %collective-permute-start.13 = (bf16[2,2,14,16,128]{4,3,2,1,0:T(8,128)(2,1)S(1)}, bf16[2,2,14,16,128]{4,3,2,1,0:T(8,128)(2,1)S(1)}, u32[]{:S(2)}, u32[]{:S(2)}) collective-permute-start(bf16[2,2,14,16,128]{4,3,2,1,0:T(8,128)(2,1)S(1)} %inner_second.1.own_ref), channel_id=1, source_target_pairs={{0,6},{2,4},{4,2},{6,0},{1,7},{3,5},{5,3},{7,1},{8,14},{10,12},{12... | collective-permute-start | bytes 688136 | tf_op jit(solution)/shard_map/ppermute | solution.py:518
  31.9 5.0 %collective-permute-start.10 = (bf16[16,16,128]{2,1,0:T(8,128)(2,1)S(1)}, bf16[16,16,128]{2,1,0:T(8,128)(2,1)S(1)}, u32[]{:S(2)}, u32[]{:S(2)}) collective-permute-start(bf16[16,16,128]{2,1,0:T(8,128)(2,1)S(1)} %border_128_1.1.refs_3_.own_ref), channel_id=1, source_target_pairs={{0,4},{2,6},{4,0},{6,2},{1,5},{3,7},{5,1},{7,3},{8,12},{10,14},{12... | collective-permute-start | bytes 196616 | tf_op jit(solution)/shard_map/ppermute | solution.py:518
  32.5 4.4 %collective-permute-start.11 = (bf16[16,16,128]{2,1,0:T(8,128)(2,1)S(1)}, bf16[16,16,128]{2,1,0:T(8,128)(2,1)S(1)}, u32[]{:S(2)}, u32[]{:S(2)}) collective-permute-start(bf16[16,16,128]{2,1,0:T(8,128)(2,1)S(1)} %border_128_1.1.refs_3_.own_ref), channel_id=1, source_target_pairs={{0,2},{2,0},{4,6},{6,4},{1,3},{3,1},{5,7},{7,5},{8,10},{10,8},{12,... | collective-permute-start | bytes 196616 | tf_op jit(solution)/shard_map/ppermute | solution.py:518
  32.7 6.5 %collective-permute-start.12 = (bf16[16,16,128]{2,1,0:T(8,128)(2,1)S(1)}, bf16[16,16,128]{2,1,0:T(8,128)(2,1)S(1)}, u32[]{:S(2)}, u32[]{:S(2)}) collective-permute-start(bf16[16,16,128]{2,1,0:T(8,128)(2,1)S(1)} %border_128_1.1.refs_3_.own_ref), channel_id=1, source_target_pairs={{0,6},{2,4},{4,2},{6,0},{1,7},{3,5},{5,3},{7,1},{8,14},{10,12},{12... | collective-permute-start | bytes 196616 | tf_op jit(solution)/shard_map/ppermute | solution.py:518
  35.2 10.6 %collective-permute-start.15 = (bf16[2,2,14,16,128]{4,3,2,1,0:T(8,128)(2,1)S(1)}, bf16[2,2,14,16,128]{4,3,2,1,0:T(8,128)(2,1)S(1)}, u32[]{:S(2)}, u32[]{:S(2)}) collective-permute-start(bf16[2,2,14,16,128]{4,3,2,1,0:T(8,128)(2,1)S(1)} %inner_second.1.own_ref), channel_id=1, source_target_pairs={{0,2},{2,0},{4,6},{6,4},{1,3},{3,1},{5,7},{7,5},{8,10},{10,8},{12,... | collective-permute-start | bytes 688136 | tf_op jit(solution)/shard_map/ppermute | solution.py:518
  39.2 7.7 %collective-permute-start.16 = (bf16[2,2,14,16,128]{4,3,2,1,0:T(8,128)(2,1)S(1)}, bf16[2,2,14,16,128]{4,3,2,1,0:T(8,128)(2,1)S(1)}, u32[]{:S(2)}, u32[]{:S(2)}) collective-permute-start(bf16[2,2,14,16,128]{4,3,2,1,0:T(8,128)(2,1)S(1)} %collective-permute-done.13.three_ref), channel_id=1, source_target_pairs={{0,2},{2,0},{4,6},{6,4},{1,3},{3,1},{5,7},{7,5},{8,10},{10,8},{12,... | collective-permute-start | bytes 688136 | tf_op jit(solution)/shard_map/ppermute | solution.py:518
  40.5 3.6 %collective-permute-start.17 = (bf16[3,16,512]{2,1,0:T(8,128)(2,1)S(1)}, bf16[3,16,512]{2,1,0:T(8,128)(2,1)S(1)}, u32[]{:S(2)}, u32[]{:S(2)}) collective-permute-start(bf16[3,16,512]{2,1,0:T(8,128)(2,1)S(1)} %get-tuple-element.117), channel_id=1, source_target_pairs={{0,16},{8,24},{16,0},{24,8},{32,48},{40,56},{48,32},{56,40},{64,80... | collective-permute-start | bytes 147464 | tf_op jit(solution)/shard_map/ppermute | solution.py:504
  40.5 8.3 %collective-permute-start.14 = (bf16[3,16,512]{2,1,0:T(8,128)(2,1)S(1)}, bf16[3,16,512]{2,1,0:T(8,128)(2,1)S(1)}, u32[]{:S(2)}, u32[]{:S(2)}) collective-permute-start(bf16[3,16,512]{2,1,0:T(8,128)(2,1)S(1)} %get-tuple-element.113), channel_id=1, source_target_pairs={{0,240},{8,248},{16,32},{24,40},{32,16},{40,24},{48,64},{56,72},{6... | collective-permute-start | bytes 147464 | tf_op jit(solution)/shard_map/ppermute | solution.py:503
  42.6 7.5 %collective-permute-start.18 = (bf16[5,16,512]{2,1,0:T(8,128)(2,1)S(1)}, bf16[5,16,512]{2,1,0:T(8,128)(2,1)S(1)}, u32[]{:S(2)}, u32[]{:S(2)}) collective-permute-start(bf16[5,16,512]{2,1,0:T(8,128)(2,1)S(1)} %get-tuple-element.119), channel_id=1, source_target_pairs={{0,8},{8,0},{16,24},{24,16},{32,40},{40,32},{48,56},{56,48},{64,72... | collective-permute-start | bytes 245768 | tf_op jit(solution)/shard_map/ppermute | solution.py:505
  44.1 6.0 %collective-permute-start.19 = (bf16[3,16,512]{2,1,0:T(8,128)(2,1)S(1)}, bf16[3,16,512]{2,1,0:T(8,128)(2,1)S(1)}, u32[]{:S(2)}, u32[]{:S(2)}) collective-permute-start(bf16[3,16,512]{2,1,0:T(8,128)(2,1)S(1)} %collective-permute-done.17.refs_2_), channel_id=1, source_target_pairs={{0,8},{8,0},{16,24},{24,16},{32,40},{40,32},{48,56},{56,48},{64,72... | collective-permute-start | bytes 147464 | tf_op jit(solution)/shard_map/ppermute | solution.py:512
  48.8 2.2 %collective-permute-start.20 = (bf16[3,16,512]{2,1,0:T(8,128)(2,1)S(1)}, bf16[3,16,512]{2,1,0:T(8,128)(2,1)S(1)}, u32[]{:S(2)}, u32[]{:S(2)}) collective-permute-start(bf16[3,16,512]{2,1,0:T(8,128)(2,1)S(1)} %collective-permute-done.14.refs_3_), channel_id=1, source_target_pairs={{0,8},{8,0},{16,24},{24,16},{32,40},{40,32},{48,56},{56,48},{64,72... | collective-permute-start | bytes 147464 | tf_op jit(solution)/shard_map/ppermute | solution.py:512
  53.1 8.9 %collective-permute-start.21 = (bf16[3,16,512]{2,1,0:T(8,128)(2,1)S(1)}, bf16[3,16,512]{2,1,0:T(8,128)(2,1)S(1)}, u32[]{:S(2)}, u32[]{:S(2)}) collective-permute-start(bf16[3,16,512]{2,1,0:T(8,128)(2,1)S(1)} %get-tuple-element.122), channel_id=1, source_target_pairs={{0,16},{8,24},{16,0},{24,8},{32,48},{40,56},{48,32},{56,40},{64,80... | collective-permute-start | bytes 147464 | tf_op jit(solution)/shard_map/ppermute | solution.py:504
  53.1 8.9 %collective-permute-start.22 = (bf16[3,16,512]{2,1,0:T(8,128)(2,1)S(1)}, bf16[3,16,512]{2,1,0:T(8,128)(2,1)S(1)}, u32[]{:S(2)}, u32[]{:S(2)}) collective-permute-start(bf16[3,16,512]{2,1,0:T(8,128)(2,1)S(1)} %get-tuple-element.128), channel_id=1, source_target_pairs={{0,240},{8,248},{16,32},{24,40},{32,16},{40,24},{48,64},{56,72},{6... | collective-permute-start | bytes 147464 | tf_op jit(solution)/shard_map/ppermute | solution.py:503
  55.2 7.5 %collective-permute-start.23 = (bf16[5,16,512]{2,1,0:T(8,128)(2,1)S(1)}, bf16[5,16,512]{2,1,0:T(8,128)(2,1)S(1)}, u32[]{:S(2)}, u32[]{:S(2)}) collective-permute-start(bf16[5,16,512]{2,1,0:T(8,128)(2,1)S(1)} %get-tuple-element.132), channel_id=1, source_target_pairs={{0,8},{8,0},{16,24},{24,16},{32,40},{40,32},{48,56},{56,48},{64,72... | collective-permute-start | bytes 245768 | tf_op jit(solution)/shard_map/ppermute | solution.py:505
  62.1 1.3 %collective-permute-start.24 = (bf16[3,16,512]{2,1,0:T(8,128)(2,1)S(1)}, bf16[3,16,512]{2,1,0:T(8,128)(2,1)S(1)}, u32[]{:S(2)}, u32[]{:S(2)}) collective-permute-start(bf16[3,16,512]{2,1,0:T(8,128)(2,1)S(1)} %collective-permute-done.21.refs_2_), channel_id=1, source_target_pairs={{0,8},{8,0},{16,24},{24,16},{32,40},{40,32},{48,56},{56,48},{64,72... | collective-permute-start | bytes 147464 | tf_op jit(solution)/shard_map/ppermute | solution.py:512
  62.2 1.4 %collective-permute-start.25 = (bf16[3,16,512]{2,1,0:T(8,128)(2,1)S(1)}, bf16[3,16,512]{2,1,0:T(8,128)(2,1)S(1)}, u32[]{:S(2)}, u32[]{:S(2)}) collective-permute-start(bf16[3,16,512]{2,1,0:T(8,128)(2,1)S(1)} %collective-permute-done.22.refs_3_), channel_id=1, source_target_pairs={{0,8},{8,0},{16,24},{24,16},{32,40},{40,32},{48,56},{56,48},{64,72... | collective-permute-start | bytes 147464 | tf_op jit(solution)/shard_map/ppermute | solution.py:512
  (3 other events, 7.4 us)

commit v4 on v3

--- a/solution.py
+++ b/solution.py
@@ -15,7 +15,8 @@
 HERE = 4
 STRIPS = 4 * HERE
 BORDER = 4 * SIDE
-ZERO_ROW = 6 * STRIPS
+ARRIVED = 16 * STRIPS
+CANDIDATES = ARRIVED + (5 + 3 + 3 + 1 + 1) * SIDE
 VMEM_LIMIT = 16 * 1024 * 1024
 
 
@@ -141,17 +142,19 @@
     return started
 
 
-def address(strips_ref, send_ref, near_ref, far_ref, pair_ref, corners_ref):
+def address(strips_ref, sender_ref, near_ref, far_ref, pair_ref):
     features = strips_ref.shape[-1]
-    corners = dot(corners_ref[...], strips_ref[...].reshape(STRIPS * SIDE, features)).astype(BF16)
-    for slot in range(4):
-        pair_ref[slot] = strips_ref[send_ref[slot]]
-    for slot in range(2):
-        near_ref[slot] = strips_ref[send_ref[4 + slot]]
-        far_ref[slot] = strips_ref[send_ref[6 + slot]]
-    pair_ref[4] = corners
-    near_ref[2] = corners
-    far_ref[2] = corners
+    wanted = dot(sender_ref[...], strips_ref[...].reshape(STRIPS * SIDE, features)).astype(BF16)
+    wanted = wanted.reshape(11, SIDE, features)
+    near_ref[...] = wanted[0:3]
+    far_ref[...] = wanted[3:6]
+    pair_ref[...] = wanted[6:11]
+
+
+def run_of_rows(start, width):
+    row = lax.broadcasted_iota(I32, (SIDE, width), 0)
+    column = lax.broadcasted_iota(I32, (SIDE, width), 1)
+    return (column == row + start).astype(F32).astype(BF16)
 
 
 def neighbours(faces):
@@ -160,7 +163,7 @@
     return own, own ^ 1, own ^ 2, jnp.where(own & 2 == 0, behind, ahead)
 
 
-def first_kernel(faces, state_ref, edge_ref, strips_ref, near_ref, far_ref, pair_ref, table_ref, held_ref, corners_ref, edges, send, sems):
+def first_kernel(faces, state_ref, edge_ref, strips_ref, near_ref, far_ref, pair_ref, held_ref, sender_ref, edges, send, sems):
     edge_copy, state_copy = copies(sems, (edge_ref, edges), (state_ref, held_ref))
     row = lax.broadcasted_iota(I32, (BORDER, PIXELS), 0)
     column = lax.broadcasted_iota(I32, (BORDER, PIXELS), 1)
@@ -173,30 +176,32 @@
     picks = (place == column).astype(F32).astype(BF16)
     row = lax.broadcasted_iota(I32, (STRIPS, STRIPS * SIDE), 0)
     column = lax.broadcasted_iota(I32, (STRIPS, STRIPS * SIDE), 1)
-    corners_ref[...] = (row * SIDE == column).astype(F32).astype(BF16)
+    corners = (row * SIDE == column).astype(F32).astype(BF16)
     own, paired, near, far = neighbours(faces)
     edge_copy.wait()
-    for target, start, capacity in ((paired, 0, 4), (near, 4, 2), (far, 6, 2)):
+    for target, start, capacity in ((near, 0, 2), (far, 2, 2), (paired, 4, 4)):
         taken = jnp.int32(0)
         for strip in range(STRIPS):
             wanted = edges[strip % 4, target * HERE + strip // 4]
             fits = jnp.logical_and(wanted >> 4 == own, taken < capacity)
             send[jnp.where(fits, start + taken, 8)] = wanted & 15
             taken = taken + fits.astype(I32)
-    for slot in range(8):
-        table_ref[slot] = send[slot]
+    for block in range(11):
+        slot = block - block // 3 if block < 6 else block - 2
+        rows = corners if block in (2, 5, 10) else run_of_rows(SIDE * send[slot], STRIPS * SIDE)
+        sender_ref[SIDE * block : SIDE * (block + 1)] = rows
     state_copy.wait()
     features = state_ref.shape[-1]
     for tile in range(HERE):
         strips = dot(picks, held_ref[tile].reshape(PIXELS, features)).astype(BF16)
         strips_ref[4 * tile : 4 * tile + 4] = strips.reshape(4, SIDE, features)
-    address(strips_ref, send, near_ref, far_ref, pair_ref, corners_ref)
+    address(strips_ref, sender_ref, near_ref, far_ref, pair_ref)
 
 
 def side_kernel(faces, *refs):
-    edge_ref, corner_ref, conv_ref, border_ref, plain_ref, tile_ref, inner_ref, ring_ref, send_ref, state_ref = refs[:10]
-    table_ref, narrow1_ref, narrow2_ref, wide1_ref, wide2_ref, border_held, plain_held, tile_held, inner_held, strips_ref = refs[10:20]
-    edges, cornered, conv, ring_held, sems = refs[20:]
+    edge_ref, corner_ref, conv_ref, border_ref, plain_ref, tile_ref, inner_ref, ring_ref, state_ref = refs[:9]
+    gather_ref, narrow1_ref, narrow2_ref, wide1_ref, wide2_ref, border_held, plain_held, tile_held, inner_held, strips_ref = refs[9:19]
+    edges, cornered, conv, ring_held, sems = refs[19:]
     started = copies(
         sems,
         (edge_ref, edges),
@@ -214,43 +219,50 @@
     from_pair, from_near, from_far = jnp.int32(0), jnp.int32(0), jnp.int32(0)
     for copy in started[:4]:
         copy.wait()
-    for slot in range(8):
-        table_ref[2 * STRIPS + slot] = send_ref[slot]
-    for strip in range(STRIPS):
-        wanted = edges[strip % 4, own * HERE + strip // 4]
-        holder, place = wanted >> 4, wanted & 15
-        by_pair, by_near, mine = holder == paired, holder == near, holder == own
-        by_far = jnp.logical_not(mine | by_pair | by_near)
-        table_ref[strip] = jnp.where(
-            mine,
-            place,
-            jnp.where(
+    near_start, far_start, late_start = ARRIVED + 5 * SIDE, ARRIVED + 8 * SIDE, ARRIVED + 11 * SIDE
+    row = lax.broadcasted_iota(I32, (SIDE, CANDIDATES), 0)
+    column = lax.broadcasted_iota(I32, (SIDE, CANDIDATES), 1)
+    for tile in range(HERE):
+        corners = row < 0
+        for side in range(4):
+            wanted = edges[side, own * HERE + tile]
+            holder, place = wanted >> 4, wanted & 15
+            by_pair, by_near, mine = holder == paired, holder == near, holder == own
+            by_far = jnp.logical_not(mine | by_pair | by_near)
+            arrived = jnp.where(
                 by_pair,
-                STRIPS + jnp.minimum(from_pair, 3),
+                ARRIVED + SIDE * jnp.minimum(from_pair, 3),
                 jnp.where(
                     by_near,
-                    STRIPS + 4 + jnp.minimum(from_near, 1),
-                    STRIPS + 6 + jnp.minimum(from_far, 1),
+                    near_start + SIDE * jnp.minimum(from_near, 1),
+                    far_start + SIDE * jnp.minimum(from_far, 1),
                 ),
-            ),
-        )
-        from_pair = from_pair + by_pair.astype(I32)
-        from_near = from_near + by_near.astype(I32)
-        from_far = from_far + by_far.astype(I32)
-    for corner in range(STRIPS):
-        wanted = cornered[corner % 4, own * HERE + corner // 4]
-        safe = jnp.maximum(wanted, 0)
-        holder, place = safe >> 4, safe & 15
-        source = jnp.where(
-            holder == own,
-            0,
-            jnp.where(
+            )
+            start = jnp.where(mine, SIDE * place, arrived)
+            gather_ref[tile, SIDE * side : SIDE * (side + 1)] = run_of_rows(start, CANDIDATES)
+            from_pair = from_pair + by_pair.astype(I32)
+            from_near = from_near + by_near.astype(I32)
+            from_far = from_far + by_far.astype(I32)
+            wanted = cornered[side, own * HERE + tile]
+            safe = jnp.maximum(wanted, 0)
+            holder, place = safe >> 4, safe & 15
+            start = jnp.where(
                 holder == paired,
-                1,
-                jnp.where(holder == near, 2, jnp.where(holder == (near ^ 1), 3, jnp.where(holder == far, 4, 5))),
-            ),
-        )
-        table_ref[STRIPS + corner] = jnp.where(wanted < 0, ZERO_ROW, source * STRIPS + place)
+                ARRIVED + 4 * SIDE,
+                jnp.where(
+                    holder == near,
+                    near_start + 2 * SIDE,
+                    jnp.where(
+                        holder == far,
+                        far_start + 2 * SIDE,
+                        jnp.where(holder == (near ^ 1), late_start, late_start + SIDE),
+                    ),
+                ),
+            )
+            start = jnp.where(holder == own, SIDE * place, start + place)
+            start = jnp.where(wanted < 0, CANDIDATES, start)
+            corners = jnp.logical_or(corners, jnp.logical_and(row == side, column == start))
+        gather_ref[tile, BORDER:] = corners.astype(F32).astype(BF16)
     for layer, (narrow, wide) in enumerate(((narrow1_ref, wide1_ref), (narrow2_ref, wide2_ref))):
         spread(conv, layer, narrow, wide)
     features = state_ref.shape[-1]
@@ -291,59 +303,39 @@
         strips_ref[8 * pair : 8 * pair + 8] = strips.reshape(8, SIDE, features)
 
 
-def gather_rims(received, strips_ref, inner_ref, table_ref, held, corners, row, known):
+def border_conv(received, strips_ref, inner_ref, gather_ref, weight_ref, border_ref, patches):
     near_ref, far_ref, pair_ref, near2_ref, far2_ref = received
     features = strips_ref.shape[-1]
-    for strip in range(STRIPS):
-        held[strip] = strips_ref[strip]
-        corners[strip : strip + 1] = strips_ref[strip, 0:1].astype(F32)
-    for slot in range(4):
-        held[STRIPS + slot] = pair_ref[slot]
-    for slot in range(2):
-        held[STRIPS + 4 + slot] = near_ref[slot]
-        held[STRIPS + 6 + slot] = far_ref[slot]
-    for source, ref in enumerate((pair_ref.at[4], near_ref.at[2], near2_ref.at[2], far_ref.at[2], far2_ref.at[2])):
-        corners[(source + 1) * STRIPS : (source + 2) * STRIPS] = ref[...].astype(F32)
-    corners[ZERO_ROW : ZERO_ROW + 8] = jnp.zeros((8, features), F32)
-    row[...] = jnp.zeros_like(row)
+    strips = strips_ref[...].reshape(STRIPS * SIDE, features)
+    inner = inner_ref[...].reshape(STRIPS * SIDE, features)
+    arrived = [ref[...].reshape(-1, features) for ref in (pair_ref, near_ref, far_ref)] + [near2_ref[2], far2_ref[2]]
+    around = dot(gather_ref[...].reshape(HERE * 80, CANDIDATES), jnp.concatenate([strips] + arrived, 0)).astype(BF16)
     for tile in range(HERE):
-        for side in range(4):
-            strip = 4 * tile + side
-            known[tile, SIDE * side : SIDE * (side + 1)] = strips_ref[strip]
-            known[tile, BORDER + SIDE * side : BORDER + SIDE * (side + 1)] = inner_ref[strip]
-            known[tile, 2 * BORDER + SIDE * side : 2 * BORDER + SIDE * (side + 1)] = held[table_ref[strip]]
-            row[tile, side : side + 1] = corners[pl.ds(table_ref[STRIPS + strip], 1)]
-        known[tile, 3 * BORDER :] = row[tile].astype(BF16)
-
-
-def border_conv(received, strips_ref, inner_ref, table_ref, weight_ref, border_ref, scratch):
-    held, corners, row, known, patches = scratch
-    gather_rims(received, strips_ref, inner_ref, table_ref, held, corners, row, known)
-    features, width = strips_ref.shape[-1], weight_ref.shape[-1]
-    for tile in range(HERE):
-        moved = dot(border_ref[...], known[tile]).astype(BF16)
+        rows = slice(BORDER * tile, BORDER * (tile + 1))
+        known = jnp.concatenate([strips[rows], inner[rows], around[80 * tile : 80 * (tile + 1)]], 0)
+        moved = dot(border_ref[...], known).astype(BF16)
         for tap in range(9):
-            patches[tap, BORDER * tile : BORDER * (tile + 1)] = moved[BORDER * tap : BORDER * (tap + 1)]
-    for group in range(features // width):
-        lanes = slice(width * group, width * (group + 1))
+            patches[tap, rows] = moved[BORDER * tap : BORDER * (tap + 1)]
+    for group in range(features // 128):
+        lanes = slice(128 * group, 128 * (group + 1))
         yield lanes, dot(jnp.concatenate([patches[tap, :, lanes] for tap in range(9)], 1), weight_ref[...])
 
 
 def border_kernel(last, sends, *refs):
     strips_ref, inner_ref, *received = refs[:7]
-    table_ref, weight_ref, border_ref, corners_ref = refs[7:11]
+    gather_ref, weight_ref, border_ref, sender_ref = refs[7:11]
     rest = list(refs[11:])
     state_ref = rest.pop(0) if last else None
     out_ref = rest.pop(0)
     messages = [rest.pop(0) for _ in range(3 if sends else 0)]
-    for lanes, total in border_conv(received, strips_ref, inner_ref, table_ref, weight_ref, border_ref, rest):
+    for lanes, total in border_conv(received, strips_ref, inner_ref, gather_ref, weight_ref, border_ref, *rest):
         if last:
             total = total + state_ref[:, :, lanes].reshape(total.shape).astype(F32)
         else:
             total = gelu(total)
         out_ref[:, :, lanes] = total.astype(BF16).reshape(STRIPS, SIDE, -1)
     if sends:
-        address(out_ref, table_ref.at[pl.ds(2 * STRIPS, 8)], *messages, corners_ref)
+        address(out_ref, sender_ref, *messages)
 
 
 def tile_conv(field_ref, strips_ref, weight_ref, tile_ref, shifted, pair):
@@ -403,11 +395,11 @@
     return mix
 
 
-def mix_strips_kernel(block, own_ref, one_ref, two_ref, three_ref, mix_in_ref, mix_out_ref, table_ref, corners_ref, strips_ref, near_ref, far_ref, pair_ref):
+def mix_strips_kernel(block, own_ref, one_ref, two_ref, three_ref, mix_in_ref, mix_out_ref, sender_ref, strips_ref, near_ref, far_ref, pair_ref):
     mix = mixer(block, lax.axis_index("level"), mix_in_ref, mix_out_ref, 4)
     column = jnp.concatenate([ref[...].reshape(STRIPS * SIDE, 128) for ref in (own_ref, one_ref, two_ref, three_ref)], 1)
     strips_ref[...] = mix(column).reshape(STRIPS, SIDE, 512)
-    address(strips_ref, table_ref.at[pl.ds(2 * STRIPS, 8)], near_ref, far_ref, pair_ref, corners_ref)
+    address(strips_ref, sender_ref, near_ref, far_ref, pair_ref)
 
 
 def mix_tiles_kernel(block, own_ref, one_ref, two_ref, three_ref, mix_in_ref, mix_out_ref, inner_ref, out_ref, ring_ref):
@@ -434,10 +426,10 @@
 
 def last_border_kernel(block, *refs):
     strips_ref, inner_ref, *received = refs[:7]
-    table_ref, weight_ref, border_ref, state_ref, mix_in_ref, mix_out_ref, tiles_ref, merge_ref, out_ref = refs[7:16]
+    gather_ref, weight_ref, border_ref, state_ref, mix_in_ref, mix_out_ref, tiles_ref, merge_ref, out_ref = refs[7:16]
     mix = mixer(block, lax.axis_index("level"), mix_in_ref, mix_out_ref, 1)
     columns = []
-    for lanes, total in border_conv(received, strips_ref, inner_ref, table_ref, weight_ref, border_ref, refs[16:]):
+    for lanes, total in border_conv(received, strips_ref, inner_ref, gather_ref, weight_ref, border_ref, *refs[16:]):
         columns.append((total + state_ref[:, :, lanes].reshape(total.shape).astype(F32)).astype(BF16))
     mixed = mix(jnp.concatenate(columns, 1))
     for pair in range(HERE // 2):
@@ -451,7 +443,6 @@
 
 
 V = pl.BlockSpec(memory_space=pltpu.VMEM)
-S = pl.BlockSpec(memory_space=pltpu.SMEM)
 H = pl.BlockSpec(memory_space=pltpu.HBM)
 
 
@@ -484,13 +475,7 @@
 
 
 def border_scratch(features):
-    return [
-        pltpu.VMEM((STRIPS + 8, SIDE, features), BF16),
-        pltpu.VMEM((ZERO_ROW + 8, features), F32),
-        pltpu.VMEM((HERE, SIDE, features), F32),
-        pltpu.VMEM((HERE, 3 * BORDER + SIDE, features), BF16),
-        pltpu.VMEM((9, STRIPS * SIDE, features), BF16),
-    ]
+    return [pltpu.VMEM((9, STRIPS * SIDE, features), BF16)]
 
 
 def tile_scratch(features):
@@ -527,22 +512,20 @@
     edges, cornered = edge_source.T, corner_source.T
     edge_scratch = pltpu.SMEM(edges.shape, I32)
 
-    strips, *messages, sends, state, corners = call(
+    strips, *messages, state, sender = call(
         functools.partial(first_kernel, faces), "first",
-        [H, H], [V, V, V, V, S, V, V],
+        [H, H], [V] * 6,
         arrays(strip_shape(thin), *message_shapes(thin))
-        + [jax.ShapeDtypeStruct((8,), I32)]
-        + arrays(state.shape, (STRIPS, STRIPS * SIDE)),
+        + arrays(state.shape, (11 * SIDE, STRIPS * SIDE)),
         [edge_scratch, pltpu.SMEM((16,), I32), pltpu.SemaphoreType.DMA((2,))],
         (state, edges),
     )
     sent = send(*messages)
     shape_w = (1152, 128), (1152, 128), (1536, 256), (1536, 256)
-    table, narrow1, narrow2, wide1, wide2, borders, plain, tiled, inner_places, state_inner = call(
+    gatherer, narrow1, narrow2, wide1, wide2, borders, plain, tiled, inner_places, state_inner = call(
         functools.partial(side_kernel, faces), "side",
-        [H] * 8 + [S, V], [S] + [V] * 9,
-        [jax.ShapeDtypeStruct((2 * STRIPS + 8,), I32)]
-        + arrays(*shape_w, border_hbm.shape, plain_hbm.shape, tile_hbm.shape, inner_hbm.shape, strip_shape(thin)),
+        [H] * 8 + [V], [V] * 10,
+        arrays((HERE, 80, CANDIDATES), *shape_w, border_hbm.shape, plain_hbm.shape, tile_hbm.shape, inner_hbm.shape, strip_shape(thin)),
         [
             edge_scratch,
             edge_scratch,
@@ -550,7 +533,7 @@
             pltpu.VMEM(ring_hbm.shape, BF16),
             pltpu.SemaphoreType.DMA((8,)),
         ],
-        (edges, cornered, conv_weight, border_hbm, plain_hbm, tile_hbm, inner_hbm, ring_hbm, sends, state),
+        (edges, cornered, conv_weight, border_hbm, plain_hbm, tile_hbm, inner_hbm, ring_hbm, state),
     )
 
     def border(last, sending, strips, inner_strips, received, weight, residual=()):
@@ -558,9 +541,9 @@
         shapes = [strip_shape(size), *(message_shapes(size) if sending else ())]
         return call(
             functools.partial(border_kernel, last, sending), f"border_{size}_{int(last)}",
-            [V] * 7 + [S] + [V] * 3 + [V] * len(residual), [V] * len(shapes),
+            [V] * (11 + len(residual)), [V] * len(shapes),
             arrays(*shapes), border_scratch(size),
-            (strips, inner_strips, *received, table, weight, borders, corners, *residual),
+            (strips, inner_strips, *received, gatherer, weight, borders, sender, *residual),
         )
 
     def interior(field, strips, weight, table, keep=False):
@@ -572,7 +555,7 @@
             (field, strips, weight, table, inner_places),
         )
 
-    received, table = receive(sent, (), (table,))
+    received, gatherer = receive(sent, (), (gatherer,))
     inner_edge, *messages = border(False, True, strips, state_inner, received, narrow1)
 
     sent = send(*messages)
@@ -598,9 +581,9 @@
     fields = [field, one, from_level(three, 1), three]
     strips, *messages = call(
         functools.partial(mix_strips_kernel, 0), "mix_strips",
-        [V] * 6 + [S, V], [V] * 4,
+        [V] * 7, [V] * 4,
         arrays(strip_shape(wide), *message_shapes(wide)), [],
-        (*edge_parts, mix_in, mix_out, table, corners),
+        (*edge_parts, mix_in, mix_out, sender),
     )
     sent = send(*messages)
     field, ring1 = call(
@@ -621,8 +604,8 @@
     received, inner_ring, tiles = receive(sent, (inner_ring,), (tiles,))
     return call(
         functools.partial(last_border_kernel, 1), "last_border",
-        [V] * 7 + [S] + [V] * 7, V, arrays((HERE, SIDE, SIDE, thin))[0], border_scratch(wide),
-        (inner_edge, inner_ring, *received, table, narrow4, borders, strips, mix_in, mix_out, tiles, jnp.asarray(merge_table())),
+        [V] * 15, V, arrays((HERE, SIDE, SIDE, thin))[0], border_scratch(wide),
+        (inner_edge, inner_ring, *received, gatherer, narrow4, borders, strips, mix_in, mix_out, tiles, jnp.asarray(merge_table())),
     )
 
 

time: 67 us -> 65.7 us (0.981)
  Pallas kernels: 25.3 us -> 22.3 us
  starting transfers between devices: 32.5 us -> 34.7 us
    ppermute x4, starting transfers between devices: 15.8 us -> 18.8 us  [send(): from_far = lax.ppermute(far, 'face', apart)]
    pallas_call x13, Pallas kernels: 25.3 us -> 22.3 us  [call(): pl.pallas_call(kernel, name=name, in_specs=in_specs, out_specs=out_specs,...]
    ppermute x4, waiting for transfers between devices: 1.24 us -> 0.37 us  [send(): from_far = lax.ppermute(far, 'face', apart)]
    ppermute x4, starting transfers between devices: 0.98 us -> 0.28 us  [send(): from_near = lax.ppermute(near, 'face', [(i, i ^ 2) for i in range(faces)])]
  transfers between devices with their start and end apart: 26 -> 26, of which waited for: 10 -> 10; matrix products, arithmetic and copies ran while one was open for 0% -> 0% of each run, Pallas kernels for 25% -> 23%
where the time goes in v4:
time: 65.7 us; the launch traced here: 65.5 us
  starting transfers between devices  34.7 us (53%)
  Pallas kernels  22.3 us (34%)
  waiting for transfers between devices  8.34 us (13%)
    pallas_call x13, Pallas kernels, call(): pl.pallas_call(kernel, name=name, in_specs=in_specs, out_specs=out_specs,...  22.3 us
    ppermute x4, starting transfers between devices, send(): from_far = lax.ppermute(far, 'face', apart)  18.8 us
    ppermute x6, starting transfers between devices, from_level(): lax.ppermute(shard, 'level', [(i, i ^ distance) for i in range(levels)])  5.83 us
    ppermute x4, starting transfers between devices, receive(): lax.ppermute(near, 'face', pairs)  4.41 us
    ppermute x6, waiting for transfers between devices, from_level(): lax.ppermute(shard, 'level', [(i, i ^ distance) for i in range(levels)])  3.85 us
    ppermute x4, starting transfers between devices, send(): lax.ppermute(to_pair, 'face', [(i, i ^ 1) for i in range(faces)])  3.54 us
    ppermute x4, waiting for transfers between devices, receive(): lax.ppermute(near, 'face', pairs)  2.37 us
    ppermute x4, starting transfers between devices, receive(): lax.ppermute(far, 'face', pairs)  1.79 us
  transfers between devices with their start and end apart: 26, of which 10 were waited for; matrix products, arithmetic and copies ran while one was open for 0% of the time, Pallas kernels for 23%

profile of v4, /device:TPU:1, one launch (start us, length us, event | category | flops | bytes accessed | tf_op | source)
XLA Modules:
  0.0 65.5 jit_solution(11385811819515099985)
XLA Ops:
  0.0 1.3 %first.1 = (bf16[16,16,128]{2,1,0:T(8,128)(2,1)S(1)}, bf16[3,16,128]{2,1,0:T(8,128)(2,1)S(1)}, bf16[3,16,128]{2,1,0:T(8,128)(2,1)S(1)}, bf16[5,16,128]{2,1,0:T(8...) custom-call(bf16[4,16,16,128]{3,2,1,0:T(8,128)(2,1)} %state_ref.1, s32[4,128]{1,0:T(4,128)} %bitcast.2), custom_call_target="tpu_custom_call" | custom-call | tf_op jit(solution)/shard_map/first/pallas_call | solution.py:450
  1.3 9.1 %collective-permute-start.1 = (bf16[3,16,128]{2,1,0:T(8,128)(2,1)S(1)}, bf16[3,16,128]{2,1,0:T(8,128)(2,1)S(1)}, u32[]{:S(2)}, u32[]{:S(2)}) collective-permute-start(bf16[3,16,128]{2,1,0:T(8,128)(2,1)S(1)} %get-tuple-element.73), channel_id=1, source_target_pairs={{0,240},{8,248},{16,32},{24,40},{32,16},{40,24},{48,64},{56,72},{6... | collective-permute-start | bytes 36872 | tf_op jit(solution)/shard_map/ppermute | solution.py:488
  10.5 1.0 %collective-permute-start.2 = (bf16[5,16,128]{2,1,0:T(8,128)(2,1)S(1)}, bf16[5,16,128]{2,1,0:T(8,128)(2,1)S(1)}, u32[]{:S(2)}, u32[]{:S(2)}) collective-permute-start(bf16[5,16,128]{2,1,0:T(8,128)(2,1)S(1)} %get-tuple-element.76), channel_id=1, source_target_pairs={{0,8},{8,0},{16,24},{24,16},{32,40},{40,32},{48,56},{56,48},{64,72... | collective-permute-start | bytes 61448 | tf_op jit(solution)/shard_map/ppermute | solution.py:490
  11.4 1.6 %side.1 = (bf16[4,80,464]{2,1,0:T(8,128)(2,1)S(1)}, bf16[1152,128]{1,0:T(8,128)(2,1)S(1)}, bf16[1152,128]{1,0:T(8,128)(2,1)S(1)}, bf16[1536,256]{1,0:T(8,128)(2,...) custom-call(s32[4,128]{1,0:T(4,128)} %bitcast.3, ...), custom_call_target="tpu_custom_call" | custom-call | tf_op jit(solution)/shard_map/side/pallas_call | solution.py:450
  13.0 2.1 %collective-permute-start.3 = (bf16[3,16,128]{2,1,0:T(8,128)(2,1)S(1)}, bf16[3,16,128]{2,1,0:T(8,128)(2,1)S(1)}, u32[]{:S(2)}, u32[]{:S(2)}) collective-permute-start(bf16[3,16,128]{2,1,0:T(8,128)(2,1)S(1)} %collective-permute-done.refs_2_), channel_id=1, source_target_pairs={{0,8},{8,0},{16,24},{24,16},{32,40},{40,32},{48,56},{56,48},{64,72... | collective-permute-start | bytes 36872 | tf_op jit(solution)/shard_map/ppermute | solution.py:497
  16.3 1.2 %border_128_0.1 = (bf16[16,16,128]{2,1,0:T(8,128)(2,1)S(1)}, bf16[3,16,128]{2,1,0:T(8,128)(2,1)S(1)}, bf16[3,16,128]{2,1,0:T(8,128)(2,1)S(1)}, bf16[5,16,128]{2,1,0:T(8,128)(2,1)S(1)}) custom-call(bf16[16,16,128]{2,1,0:T(8,128)(2,1)S(1)} %get-tuple-element.69.refs_0_.strips_ref.refs_11_, bf16[16,16,128]{2,1,0:T(8,128)(2,1)S(1)} %get-tuple-element.71.refs_1_, ...), custom_call_target="tpu_custom_call" | custom-call | tf_op jit(solution)/shard_map/border_128_0/pallas_call | solution.py:450
  17.6 3.4 %collective-permute-start.6 = (bf16[3,16,128]{2,1,0:T(8,128)(2,1)S(1)}, bf16[3,16,128]{2,1,0:T(8,128)(2,1)S(1)}, u32[]{:S(2)}, u32[]{:S(2)}) collective-permute-start(bf16[3,16,128]{2,1,0:T(8,128)(2,1)S(1)} %get-tuple-element.89), channel_id=1, source_target_pairs={{0,240},{8,248},{16,32},{24,40},{32,16},{40,24},{48,64},{56,72},{6... | collective-permute-start | bytes 36872 | tf_op jit(solution)/shard_map/ppermute | solution.py:488
  21.5 1.2 %inner_128.1 = (bf16[2,2,14,16,128]{4,3,2,1,0:T(8,128)(2,1)S(1)}, bf16[16,16,128]{2,1,0:T(8,128)(2,1)S(1)}, bf16[2,2,14,16,128]{4,3,2,1,0:T(8,128)(2,1)S(1)}) custom-call(bf16[4,16,16,128]{3,2,1,0:T(8,128)(2,1)S(1)} %get-tuple-element.70.refs_8_.field_ref, bf16[16,16,128]{2,1,0:T(8,128)(2,1)S(1)} %get-tuple-element.69.refs_0_.strips_ref.refs_11_, ...), custom_call_target="tpu_custom_call" | custom-call | tf_op jit(solution)/shard_map/inner_128/pallas_call | solution.py:450
  23.8 1.6 %collective-permute-start.8 = (bf16[3,16,128]{2,1,0:T(8,128)(2,1)S(1)}, bf16[3,16,128]{2,1,0:T(8,128)(2,1)S(1)}, u32[]{:S(2)}, u32[]{:S(2)}) collective-permute-start(bf16[3,16,128]{2,1,0:T(8,128)(2,1)S(1)} %collective-permute-done.5.refs_2_), channel_id=1, source_target_pairs={{0,8},{8,0},{16,24},{24,16},{32,40},{40,32},{48,56},{56,48},{64,72... | collective-permute-start | bytes 36872 | tf_op jit(solution)/shard_map/ppermute | solution.py:497
  26.6 2.5 %collective-permute-start.13 = (bf16[2,2,14,16,128]{4,3,2,1,0:T(8,128)(2,1)S(1)}, bf16[2,2,14,16,128]{4,3,2,1,0:T(8,128)(2,1)S(1)}, u32[]{:S(2)}, u32[]{:S(2)}) collective-permute-start(bf16[2,2,14,16,128]{4,3,2,1,0:T(8,128)(2,1)S(1)} %inner_second.1.own_ref), channel_id=1, source_target_pairs={{0,6},{2,4},{4,2},{6,0},{1,7},{3,5},{5,3},{7,1},{8,14},{10,12},{12... | collective-permute-start | bytes 688136 | tf_op jit(solution)/shard_map/ppermute | solution.py:503
  29.1 1.0 %border_128_1.1.refs_3_.own_ref = bf16[16,16,128]{2,1,0:T(8,128)(2,1)S(1)} custom-call(bf16[16,16,128]{2,1,0:T(8,128)(2,1)S(1)} %get-tuple-element.81.strips_ref.refs_0_, bf16[16,16,128]{2,1,0:T(8,128)(2,1)S(1)} %get-tuple-element.87.refs_1_, bf16[3,16,128]{2,1,0:T(8,128)(2,1)S(1)} %collective-permute-done.5.refs_2_, ...), custom_call_target="tpu_custom_call" | custom-call | tf_op jit(solution)/shard_map/border_128_1/pallas_call | solution.py:450
  31.0 2.5 %collective-permute-start.12 = (bf16[16,16,128]{2,1,0:T(8,128)(2,1)S(1)}, bf16[16,16,128]{2,1,0:T(8,128)(2,1)S(1)}, u32[]{:S(2)}, u32[]{:S(2)}) collective-permute-start(bf16[16,16,128]{2,1,0:T(8,128)(2,1)S(1)} %border_128_1.1.refs_3_.own_ref), channel_id=1, source_target_pairs={{0,6},{2,4},{4,2},{6,0},{1,7},{3,5},{5,3},{7,1},{8,14},{10,12},{12... | collective-permute-start | bytes 196616 | tf_op jit(solution)/shard_map/ppermute | solution.py:503
  33.5 1.7 %weights.1 = (bf16[1152,128]{1,0:T(8,128)(2,1)S(1)}, bf16[1152,128]{1,0:T(8,128)(2,1)S(1)}, bf16[1536,256]{1,0:T(8,128)(2,1)S(1)}, bf16[1536,256]{1,0:T(8,128)(2...) custom-call(bf16[2,2,9,64,64]{4,3,2,1,0:T(8,128)(2,1)} %refs_0_.1, ...), custom_call_target="tpu_custom_call" | custom-call | tf_op jit(solution)/shard_map/weights/pallas_call | solution.py:450
  35.2 2.5 %collective-permute-done.12.three_ref = bf16[16,16,128]{2,1,0:T(8,128)(2,1)S(1)} collective-permute-done((bf16[16,16,128]{2,1,0:T(8,128)(2,1)S(1)}, bf16[16,16,128]{2,1,0:T(8,128)(2,1)S(1)}, u32[]{:S(2)}, u32[]{:S(2)}) %collective-permute-start.12) | collective-permute-done | bytes 65568 | tf_op jit(solution)/shard_map/ppermute | solution.py:503
  38.6 3.1 %collective-permute-start.14 = (bf16[3,16,512]{2,1,0:T(8,128)(2,1)S(1)}, bf16[3,16,512]{2,1,0:T(8,128)(2,1)S(1)}, u32[]{:S(2)}, u32[]{:S(2)}) collective-permute-start(bf16[3,16,512]{2,1,0:T(8,128)(2,1)S(1)} %get-tuple-element.111), channel_id=1, source_target_pairs={{0,240},{8,248},{16,32},{24,40},{32,16},{40,24},{48,64},{56,72},{6... | collective-permute-start | bytes 147464 | tf_op jit(solution)/shard_map/ppermute | solution.py:488
  41.7 1.5 %collective-permute-start.18 = (bf16[5,16,512]{2,1,0:T(8,128)(2,1)S(1)}, bf16[5,16,512]{2,1,0:T(8,128)(2,1)S(1)}, u32[]{:S(2)}, u32[]{:S(2)}) collective-permute-start(bf16[5,16,512]{2,1,0:T(8,128)(2,1)S(1)} %get-tuple-element.117), channel_id=1, source_target_pairs={{0,8},{8,0},{16,24},{24,16},{32,40},{40,32},{48,56},{56,48},{64,72... | collective-permute-start | bytes 245768 | tf_op jit(solution)/shard_map/ppermute | solution.py:490
  43.9 1.3 %collective-permute-done.16.two_ref = bf16[2,2,14,16,128]{4,3,2,1,0:T(8,128)(2,1)S(1)} collective-permute-done((bf16[2,2,14,16,128]{4,3,2,1,0:T(8,128)(2,1)S(1)}, bf16[2,2,14,16,128]{4,3,2,1,0:T(8,128)(2,1)S(1)}, u32[]{:S(2)}, u32[]{:S(2)}) %collective-permute-start.16) | collective-permute-done | bytes 229408 | tf_op jit(solution)/shard_map/ppermute | solution.py:503
  45.2 1.8 %mix_tiles.1 = (bf16[2,2,14,16,512]{4,3,2,1,0:T(8,128)(2,1)S(1)}, bf16[16,16,512]{2,1,0:T(8,128)(2,1)S(1)}) custom-call(bf16[2,2,14,16,128]{4,3,2,1,0:T(8,128)(2,1)S(1)} %inner_second.1.own_ref, bf16[2,2,14,16,128]{4,3,2,1,0:T(8,128)(2,1)S(1)} %collective-permute-done.15.one_ref, bf16[2,2,14,16,128]{4,3,2,1,0:T(8,128)(2,1)S(1)} %collective-permute-done.16.two_ref, ...), custom_call_target="tpu_custom_call" | custom-call | tf_op jit(solution)/shard_map/mix_tiles/pallas_call | solution.py:450
  47.0 1.3 %collective-permute-start.20 = (bf16[3,16,512]{2,1,0:T(8,128)(2,1)S(1)}, bf16[3,16,512]{2,1,0:T(8,128)(2,1)S(1)}, u32[]{:S(2)}, u32[]{:S(2)}) collective-permute-start(bf16[3,16,512]{2,1,0:T(8,128)(2,1)S(1)} %collective-permute-done.14.refs_3_), channel_id=1, source_target_pairs={{0,8},{8,0},{16,24},{24,16},{32,40},{40,32},{48,56},{56,48},{64,72... | collective-permute-start | bytes 147464 | tf_op jit(solution)/shard_map/ppermute | solution.py:497
  49.2 1.8 %border_512_0.1 = (bf16[16,16,512]{2,1,0:T(8,128)(2,1)S(1)}, bf16[3,16,512]{2,1,0:T(8,128)(2,1)S(1)}, bf16[3,16,512]{2,1,0:T(8,128)(2,1)S(1)}, bf16[5,16,512]{2,1,0:T(8,128)(2,1)S(1)}) custom-call(bf16[16,16,512]{2,1,0:T(8,128)(2,1)S(1)} %get-tuple-element.110.refs_0_.strips_ref.refs_10_, bf16[16,16,512]{2,1,0:T(8,128)(2,1)S(1)} %get-tuple-element.114.refs_1_, ...), custom_call_target="tpu_custom_call" | custom-call | tf_op jit(solution)/shard_map/border_512_0/pallas_call | solution.py:450
  51.1 3.1 %collective-permute-start.22 = (bf16[3,16,512]{2,1,0:T(8,128)(2,1)S(1)}, bf16[3,16,512]{2,1,0:T(8,128)(2,1)S(1)}, u32[]{:S(2)}, u32[]{:S(2)}) collective-permute-start(bf16[3,16,512]{2,1,0:T(8,128)(2,1)S(1)} %get-tuple-element.126), channel_id=1, source_target_pairs={{0,240},{8,248},{16,32},{24,40},{32,16},{40,24},{48,64},{56,72},{6... | collective-permute-start | bytes 147464 | tf_op jit(solution)/shard_map/ppermute | solution.py:488
  54.9 2.6 %inner_512.1 = (bf16[2,2,14,16,512]{4,3,2,1,0:T(8,128)(2,1)S(1)}, bf16[16,16,512]{2,1,0:T(8,128)(2,1)S(1)}) custom-call(bf16[2,2,14,16,512]{4,3,2,1,0:T(8,128)(2,1)S(1)} %get-tuple-element.121.field_ref.state_ref, bf16[16,16,512]{2,1,0:T(8,128)(2,1)S(1)} %get-tuple-element.110.refs_0_.strips_ref.refs_10_, ...), custom_call_target="tpu_custom_call" | custom-call | tf_op jit(solution)/shard_map/inner_512/pallas_call | solution.py:450
  57.6 3.5 %last_inner.1.refs_13_ = bf16[2,2,14,16,128]{4,3,2,1,0:T(8,128)(2,1)S(1)} custom-call(bf16[2,2,14,16,512]{4,3,2,1,0:T(8,128)(2,1)S(1)} %get-tuple-element.127.field_ref, bf16[16,16,512]{2,1,0:T(8,128)(2,1)S(1)} %get-tuple-element.119.strips_ref.refs_0_, bf16[1536,256]{1,0:T(8,128)(2,1)S(1)} %get-tuple-element.128.weight_ref, ...), custom_call_target="tpu_custom_call" | custom-call | tf_op jit(solution)/shard_map/last_inner/pallas_call | solution.py:450
  62.6 2.9 %last_border.1 = bf16[4,16,16,128]{3,2,1,0:T(8,128)(2,1)} custom-call(bf16[16,16,512]{2,1,0:T(8,128)(2,1)S(1)} %get-tuple-element.119.strips_ref.refs_0_, bf16[16,16,512]{2,1,0:T(8,128)(2,1)S(1)} %get-tuple-element.124.refs_1_, bf16[3,16,512]{2,1,0:T(8,128)(2,1)S(1)} %collective-permute-done.21.refs_2_, ...), custom_call_target="tpu_custom_call" | custom-call | tf_op jit(solution)/shard_map/last_border/pallas_call | solution.py:450
  (43 shorter events, 9.6 us)
Async XLA Ops:
  1.3 11.7 %collective-permute-start.1 = (bf16[3,16,128]{2,1,0:T(8,128)(2,1)S(1)}, bf16[3,16,128]{2,1,0:T(8,128)(2,1)S(1)}, u32[]{:S(2)}, u32[]{:S(2)}) collective-permute-start(bf16[3,16,128]{2,1,0:T(8,128)(2,1)S(1)} %get-tuple-element.73), channel_id=1, source_target_pairs={{0,240},{8,248},{16,32},{24,40},{32,16},{40,24},{48,64},{56,72},{6... | collective-permute-start | bytes 36872 | tf_op jit(solution)/shard_map/ppermute | solution.py:488
  10.4 2.6 %collective-permute-start = (bf16[3,16,128]{2,1,0:T(8,128)(2,1)S(1)}, bf16[3,16,128]{2,1,0:T(8,128)(2,1)S(1)}, u32[]{:S(2)}, u32[]{:S(2)}) collective-permute-start(bf16[3,16,128]{2,1,0:T(8,128)(2,1)S(1)} %get-tuple-element.72), channel_id=1, source_target_pairs={{0,16},{8,24},{16,0},{24,8},{32,48},{40,56},{48,32},{56,40},{64,80... | collective-permute-start | bytes 36872 | tf_op jit(solution)/shard_map/ppermute | solution.py:489
  10.5 4.7 %collective-permute-start.2 = (bf16[5,16,128]{2,1,0:T(8,128)(2,1)S(1)}, bf16[5,16,128]{2,1,0:T(8,128)(2,1)S(1)}, u32[]{:S(2)}, u32[]{:S(2)}) collective-permute-start(bf16[5,16,128]{2,1,0:T(8,128)(2,1)S(1)} %get-tuple-element.76), channel_id=1, source_target_pairs={{0,8},{8,0},{16,24},{24,16},{32,40},{40,32},{48,56},{56,48},{64,72... | collective-permute-start | bytes 61448 | tf_op jit(solution)/shard_map/ppermute | solution.py:490
  13.0 2.9 %collective-permute-start.3 = (bf16[3,16,128]{2,1,0:T(8,128)(2,1)S(1)}, bf16[3,16,128]{2,1,0:T(8,128)(2,1)S(1)}, u32[]{:S(2)}, u32[]{:S(2)}) collective-permute-start(bf16[3,16,128]{2,1,0:T(8,128)(2,1)S(1)} %collective-permute-done.refs_2_), channel_id=1, source_target_pairs={{0,8},{8,0},{16,24},{24,16},{32,40},{40,32},{48,56},{56,48},{64,72... | collective-permute-start | bytes 36872 | tf_op jit(solution)/shard_map/ppermute | solution.py:497
  17.5 6.0 %collective-permute-start.5 = (bf16[3,16,128]{2,1,0:T(8,128)(2,1)S(1)}, bf16[3,16,128]{2,1,0:T(8,128)(2,1)S(1)}, u32[]{:S(2)}, u32[]{:S(2)}) collective-permute-start(bf16[3,16,128]{2,1,0:T(8,128)(2,1)S(1)} %get-tuple-element.82), channel_id=1, source_target_pairs={{0,16},{8,24},{16,0},{24,8},{32,48},{40,56},{48,32},{56,40},{64,80... | collective-permute-start | bytes 36872 | tf_op jit(solution)/shard_map/ppermute | solution.py:489
  17.6 6.2 %collective-permute-start.6 = (bf16[3,16,128]{2,1,0:T(8,128)(2,1)S(1)}, bf16[3,16,128]{2,1,0:T(8,128)(2,1)S(1)}, u32[]{:S(2)}, u32[]{:S(2)}) collective-permute-start(bf16[3,16,128]{2,1,0:T(8,128)(2,1)S(1)} %get-tuple-element.89), channel_id=1, source_target_pairs={{0,240},{8,248},{16,32},{24,40},{32,16},{40,24},{48,64},{56,72},{6... | collective-permute-start | bytes 36872 | tf_op jit(solution)/shard_map/ppermute | solution.py:488
  21.0 4.4 %collective-permute-start.7 = (bf16[5,16,128]{2,1,0:T(8,128)(2,1)S(1)}, bf16[5,16,128]{2,1,0:T(8,128)(2,1)S(1)}, u32[]{:S(2)}, u32[]{:S(2)}) collective-permute-start(bf16[5,16,128]{2,1,0:T(8,128)(2,1)S(1)} %get-tuple-element.95), channel_id=1, source_target_pairs={{0,8},{8,0},{16,24},{24,16},{32,40},{40,32},{48,56},{56,48},{64,72... | collective-permute-start | bytes 61448 | tf_op jit(solution)/shard_map/ppermute | solution.py:490
  23.8 2.4 %collective-permute-start.8 = (bf16[3,16,128]{2,1,0:T(8,128)(2,1)S(1)}, bf16[3,16,128]{2,1,0:T(8,128)(2,1)S(1)}, u32[]{:S(2)}, u32[]{:S(2)}) collective-permute-start(bf16[3,16,128]{2,1,0:T(8,128)(2,1)S(1)} %collective-permute-done.5.refs_2_), channel_id=1, source_target_pairs={{0,8},{8,0},{16,24},{24,16},{32,40},{40,32},{48,56},{56,48},{64,72... | collective-permute-start | bytes 36872 | tf_op jit(solution)/shard_map/ppermute | solution.py:497
  26.6 11.1 %collective-permute-start.13 = (bf16[2,2,14,16,128]{4,3,2,1,0:T(8,128)(2,1)S(1)}, bf16[2,2,14,16,128]{4,3,2,1,0:T(8,128)(2,1)S(1)}, u32[]{:S(2)}, u32[]{:S(2)}) collective-permute-start(bf16[2,2,14,16,128]{4,3,2,1,0:T(8,128)(2,1)S(1)} %inner_second.1.own_ref), channel_id=1, source_target_pairs={{0,6},{2,4},{4,2},{6,0},{1,7},{3,5},{5,3},{7,1},{8,14},{10,12},{12... | collective-permute-start | bytes 688136 | tf_op jit(solution)/shard_map/ppermute | solution.py:503
  30.1 5.0 %collective-permute-start.10 = (bf16[16,16,128]{2,1,0:T(8,128)(2,1)S(1)}, bf16[16,16,128]{2,1,0:T(8,128)(2,1)S(1)}, u32[]{:S(2)}, u32[]{:S(2)}) collective-permute-start(bf16[16,16,128]{2,1,0:T(8,128)(2,1)S(1)} %border_128_1.1.refs_3_.own_ref), channel_id=1, source_target_pairs={{0,4},{2,6},{4,0},{6,2},{1,5},{3,7},{5,1},{7,3},{8,12},{10,14},{12... | collective-permute-start | bytes 196616 | tf_op jit(solution)/shard_map/ppermute | solution.py:503
  30.7 4.4 %collective-permute-start.11 = (bf16[16,16,128]{2,1,0:T(8,128)(2,1)S(1)}, bf16[16,16,128]{2,1,0:T(8,128)(2,1)S(1)}, u32[]{:S(2)}, u32[]{:S(2)}) collective-permute-start(bf16[16,16,128]{2,1,0:T(8,128)(2,1)S(1)} %border_128_1.1.refs_3_.own_ref), channel_id=1, source_target_pairs={{0,2},{2,0},{4,6},{6,4},{1,3},{3,1},{5,7},{7,5},{8,10},{10,8},{12,... | collective-permute-start | bytes 196616 | tf_op jit(solution)/shard_map/ppermute | solution.py:503
  31.0 6.7 %collective-permute-start.12 = (bf16[16,16,128]{2,1,0:T(8,128)(2,1)S(1)}, bf16[16,16,128]{2,1,0:T(8,128)(2,1)S(1)}, u32[]{:S(2)}, u32[]{:S(2)}) collective-permute-start(bf16[16,16,128]{2,1,0:T(8,128)(2,1)S(1)} %border_128_1.1.refs_3_.own_ref), channel_id=1, source_target_pairs={{0,6},{2,4},{4,2},{6,0},{1,7},{3,5},{5,3},{7,1},{8,14},{10,12},{12... | collective-permute-start | bytes 196616 | tf_op jit(solution)/shard_map/ppermute | solution.py:503
  33.5 10.4 %collective-permute-start.15 = (bf16[2,2,14,16,128]{4,3,2,1,0:T(8,128)(2,1)S(1)}, bf16[2,2,14,16,128]{4,3,2,1,0:T(8,128)(2,1)S(1)}, u32[]{:S(2)}, u32[]{:S(2)}) collective-permute-start(bf16[2,2,14,16,128]{4,3,2,1,0:T(8,128)(2,1)S(1)} %inner_second.1.own_ref), channel_id=1, source_target_pairs={{0,2},{2,0},{4,6},{6,4},{1,3},{3,1},{5,7},{7,5},{8,10},{10,8},{12,... | collective-permute-start | bytes 688136 | tf_op jit(solution)/shard_map/ppermute | solution.py:503
  37.7 7.5 %collective-permute-start.16 = (bf16[2,2,14,16,128]{4,3,2,1,0:T(8,128)(2,1)S(1)}, bf16[2,2,14,16,128]{4,3,2,1,0:T(8,128)(2,1)S(1)}, u32[]{:S(2)}, u32[]{:S(2)}) collective-permute-start(bf16[2,2,14,16,128]{4,3,2,1,0:T(8,128)(2,1)S(1)} %collective-permute-done.13.three_ref), channel_id=1, source_target_pairs={{0,2},{2,0},{4,6},{6,4},{1,3},{3,1},{5,7},{7,5},{8,10},{10,8},{12,... | collective-permute-start | bytes 688136 | tf_op jit(solution)/shard_map/ppermute | solution.py:503
  38.5 4.8 %collective-permute-start.17 = (bf16[3,16,512]{2,1,0:T(8,128)(2,1)S(1)}, bf16[3,16,512]{2,1,0:T(8,128)(2,1)S(1)}, u32[]{:S(2)}, u32[]{:S(2)}) collective-permute-start(bf16[3,16,512]{2,1,0:T(8,128)(2,1)S(1)} %get-tuple-element.115), channel_id=1, source_target_pairs={{0,16},{8,24},{16,0},{24,8},{32,48},{40,56},{48,32},{56,40},{64,80... | collective-permute-start | bytes 147464 | tf_op jit(solution)/shard_map/ppermute | solution.py:489
  38.6 8.5 %collective-permute-start.14 = (bf16[3,16,512]{2,1,0:T(8,128)(2,1)S(1)}, bf16[3,16,512]{2,1,0:T(8,128)(2,1)S(1)}, u32[]{:S(2)}, u32[]{:S(2)}) collective-permute-start(bf16[3,16,512]{2,1,0:T(8,128)(2,1)S(1)} %get-tuple-element.111), channel_id=1, source_target_pairs={{0,240},{8,248},{16,32},{24,40},{32,16},{40,24},{48,64},{56,72},{6... | collective-permute-start | bytes 147464 | tf_op jit(solution)/shard_map/ppermute | solution.py:488
  41.7 6.6 %collective-permute-start.18 = (bf16[5,16,512]{2,1,0:T(8,128)(2,1)S(1)}, bf16[5,16,512]{2,1,0:T(8,128)(2,1)S(1)}, u32[]{:S(2)}, u32[]{:S(2)}) collective-permute-start(bf16[5,16,512]{2,1,0:T(8,128)(2,1)S(1)} %get-tuple-element.117), channel_id=1, source_target_pairs={{0,8},{8,0},{16,24},{24,16},{32,40},{40,32},{48,56},{56,48},{64,72... | collective-permute-start | bytes 245768 | tf_op jit(solution)/shard_map/ppermute | solution.py:490
  43.2 5.1 %collective-permute-start.19 = (bf16[3,16,512]{2,1,0:T(8,128)(2,1)S(1)}, bf16[3,16,512]{2,1,0:T(8,128)(2,1)S(1)}, u32[]{:S(2)}, u32[]{:S(2)}) collective-permute-start(bf16[3,16,512]{2,1,0:T(8,128)(2,1)S(1)} %collective-permute-done.17.refs_2_), channel_id=1, source_target_pairs={{0,8},{8,0},{16,24},{24,16},{32,40},{40,32},{48,56},{56,48},{64,72... | collective-permute-start | bytes 147464 | tf_op jit(solution)/shard_map/ppermute | solution.py:497
  47.0 2.2 %collective-permute-start.20 = (bf16[3,16,512]{2,1,0:T(8,128)(2,1)S(1)}, bf16[3,16,512]{2,1,0:T(8,128)(2,1)S(1)}, u32[]{:S(2)}, u32[]{:S(2)}) collective-permute-start(bf16[3,16,512]{2,1,0:T(8,128)(2,1)S(1)} %collective-permute-done.14.refs_3_), channel_id=1, source_target_pairs={{0,8},{8,0},{16,24},{24,16},{32,40},{40,32},{48,56},{56,48},{64,72... | collective-permute-start | bytes 147464 | tf_op jit(solution)/shard_map/ppermute | solution.py:497
  51.0 10.1 %collective-permute-start.21 = (bf16[3,16,512]{2,1,0:T(8,128)(2,1)S(1)}, bf16[3,16,512]{2,1,0:T(8,128)(2,1)S(1)}, u32[]{:S(2)}, u32[]{:S(2)}) collective-permute-start(bf16[3,16,512]{2,1,0:T(8,128)(2,1)S(1)} %get-tuple-element.120), channel_id=1, source_target_pairs={{0,16},{8,24},{16,0},{24,8},{32,48},{40,56},{48,32},{56,40},{64,80... | collective-permute-start | bytes 147464 | tf_op jit(solution)/shard_map/ppermute | solution.py:489
  51.1 10.0 %collective-permute-start.22 = (bf16[3,16,512]{2,1,0:T(8,128)(2,1)S(1)}, bf16[3,16,512]{2,1,0:T(8,128)(2,1)S(1)}, u32[]{:S(2)}, u32[]{:S(2)}) collective-permute-start(bf16[3,16,512]{2,1,0:T(8,128)(2,1)S(1)} %get-tuple-element.126), channel_id=1, source_target_pairs={{0,240},{8,248},{16,32},{24,40},{32,16},{40,24},{48,64},{56,72},{6... | collective-permute-start | bytes 147464 | tf_op jit(solution)/shard_map/ppermute | solution.py:488
  54.3 7.5 %collective-permute-start.23 = (bf16[5,16,512]{2,1,0:T(8,128)(2,1)S(1)}, bf16[5,16,512]{2,1,0:T(8,128)(2,1)S(1)}, u32[]{:S(2)}, u32[]{:S(2)}) collective-permute-start(bf16[5,16,512]{2,1,0:T(8,128)(2,1)S(1)} %get-tuple-element.130), channel_id=1, source_target_pairs={{0,8},{8,0},{16,24},{24,16},{32,40},{40,32},{48,56},{56,48},{64,72... | collective-permute-start | bytes 245768 | tf_op jit(solution)/shard_map/ppermute | solution.py:490
  61.1 1.3 %collective-permute-start.24 = (bf16[3,16,512]{2,1,0:T(8,128)(2,1)S(1)}, bf16[3,16,512]{2,1,0:T(8,128)(2,1)S(1)}, u32[]{:S(2)}, u32[]{:S(2)}) collective-permute-start(bf16[3,16,512]{2,1,0:T(8,128)(2,1)S(1)} %collective-permute-done.21.refs_2_), channel_id=1, source_target_pairs={{0,8},{8,0},{16,24},{24,16},{32,40},{40,32},{48,56},{56,48},{64,72... | collective-permute-start | bytes 147464 | tf_op jit(solution)/shard_map/ppermute | solution.py:497
  61.2 1.4 %collective-permute-start.25 = (bf16[3,16,512]{2,1,0:T(8,128)(2,1)S(1)}, bf16[3,16,512]{2,1,0:T(8,128)(2,1)S(1)}, u32[]{:S(2)}, u32[]{:S(2)}) collective-permute-start(bf16[3,16,512]{2,1,0:T(8,128)(2,1)S(1)} %collective-permute-done.22.refs_3_), channel_id=1, source_target_pairs={{0,8},{8,0},{16,24},{24,16},{32,40},{40,32},{48,56},{56,48},{64,72... | collective-permute-start | bytes 147464 | tf_op jit(solution)/shard_map/ppermute | solution.py:497
  (3 other events, 7.4 us)

commit v5 on v4

--- a/solution.py
+++ b/solution.py
@@ -429,8 +429,10 @@
     gather_ref, weight_ref, border_ref, state_ref, mix_in_ref, mix_out_ref, tiles_ref, merge_ref, out_ref = refs[7:16]
     mix = mixer(block, lax.axis_index("level"), mix_in_ref, mix_out_ref, 1)
     columns = []
-    for lanes, total in border_conv(received, strips_ref, inner_ref, gather_ref, weight_ref, border_ref, *refs[16:]):
+    for lanes, total in border_conv(received, strips_ref, inner_ref, gather_ref, weight_ref, border_ref, refs[16]):
         columns.append((total + state_ref[:, :, lanes].reshape(total.shape).astype(F32)).astype(BF16))
+    held, sems = refs[17:]
+    leaving = []
     mixed = mix(jnp.concatenate(columns, 1))
     for pair in range(HERE // 2):
         strips = mixed[2 * BORDER * pair : 2 * BORDER * (pair + 1)]
@@ -439,7 +441,11 @@
             merged = dot(merge_ref[group], jnp.concatenate(rows + [strips], 0)).astype(BF16)
             merged = merged.reshape(2, 4, SIDE, 128)
             for tile in range(2):
-                out_ref[2 * pair + tile, 4 * group : 4 * group + 4] = merged[tile]
+                held[2 * pair + tile, 4 * group : 4 * group + 4] = merged[tile]
+        done = held.at[pl.ds(2 * pair, 2)], out_ref.at[pl.ds(2 * pair, 2)]
+        leaving += copies(sems.at[pl.ds(pair, 1)], done)
+    for copy in leaving:
+        copy.wait()
 
 
 V = pl.BlockSpec(memory_space=pltpu.VMEM)
@@ -604,7 +610,8 @@
     received, inner_ring, tiles = receive(sent, (inner_ring,), (tiles,))
     return call(
         functools.partial(last_border_kernel, 1), "last_border",
-        [V] * 15, V, arrays((HERE, SIDE, SIDE, thin))[0], border_scratch(wide),
+        [V] * 15, H, arrays((HERE, SIDE, SIDE, thin))[0],
+        border_scratch(wide) + [pltpu.VMEM((HERE, SIDE, SIDE, thin), BF16), pltpu.SemaphoreType.DMA((2,))],
         (inner_edge, inner_ring, *received, gatherer, narrow4, borders, strips, mix_in, mix_out, tiles, jnp.asarray(merge_table())),
     )
 

time: 65.7 us -> 65.8 us (level)
  no operation moved by 1% of the time
where the time goes in v5:
time: 65.8 us; the launch traced here: 65.7 us
  starting transfers between devices  34.7 us (53%)
  Pallas kernels  22.3 us (34%)
  waiting for transfers between devices  8.34 us (13%)
    pallas_call x13, Pallas kernels, call(): pl.pallas_call(kernel, name=name, in_specs=in_specs, out_specs=out_specs,...  22.3 us
    ppermute x4, starting transfers between devices, send(): from_far = lax.ppermute(far, 'face', apart)  18.8 us
    ppermute x6, starting transfers between devices, from_level(): lax.ppermute(shard, 'level', [(i, i ^ distance) for i in range(levels)])  5.83 us
    ppermute x4, starting transfers between devices, receive(): lax.ppermute(near, 'face', pairs)  4.41 us
    ppermute x6, waiting for transfers between devices, from_level(): lax.ppermute(shard, 'level', [(i, i ^ distance) for i in range(levels)])  3.85 us
    ppermute x4, starting transfers between devices, send(): lax.ppermute(to_pair, 'face', [(i, i ^ 1) for i in range(faces)])  3.54 us
    ppermute x4, waiting for transfers between devices, receive(): lax.ppermute(near, 'face', pairs)  2.37 us
    ppermute x4, starting transfers between devices, receive(): lax.ppermute(far, 'face', pairs)  1.79 us
  transfers between devices with their start and end apart: 26, of which 10 were waited for; matrix products, arithmetic and copies ran while one was open for 0% of the time, Pallas kernels for 23%

profile of v5, /device:TPU:1, one launch (start us, length us, event | category | flops | bytes accessed | tf_op | source)
XLA Modules:
  0.0 65.7 jit_solution(142292118283697257)
XLA Ops:
  0.0 1.3 %first.1 = (bf16[16,16,128]{2,1,0:T(8,128)(2,1)S(1)}, bf16[3,16,128]{2,1,0:T(8,128)(2,1)S(1)}, bf16[3,16,128]{2,1,0:T(8,128)(2,1)S(1)}, bf16[5,16,128]{2,1,0:T(8...) custom-call(bf16[4,16,16,128]{3,2,1,0:T(8,128)(2,1)} %state_ref.1, s32[4,128]{1,0:T(4,128)} %bitcast.2), custom_call_target="tpu_custom_call" | custom-call | tf_op jit(solution)/shard_map/first/pallas_call | solution.py:456
  1.3 9.1 %collective-permute-start.1 = (bf16[3,16,128]{2,1,0:T(8,128)(2,1)S(1)}, bf16[3,16,128]{2,1,0:T(8,128)(2,1)S(1)}, u32[]{:S(2)}, u32[]{:S(2)}) collective-permute-start(bf16[3,16,128]{2,1,0:T(8,128)(2,1)S(1)} %get-tuple-element.73), channel_id=1, source_target_pairs={{0,240},{8,248},{16,32},{24,40},{32,16},{40,24},{48,64},{56,72},{6... | collective-permute-start | bytes 36872 | tf_op jit(solution)/shard_map/ppermute | solution.py:494
  10.5 1.0 %collective-permute-start.2 = (bf16[5,16,128]{2,1,0:T(8,128)(2,1)S(1)}, bf16[5,16,128]{2,1,0:T(8,128)(2,1)S(1)}, u32[]{:S(2)}, u32[]{:S(2)}) collective-permute-start(bf16[5,16,128]{2,1,0:T(8,128)(2,1)S(1)} %get-tuple-element.76), channel_id=1, source_target_pairs={{0,8},{8,0},{16,24},{24,16},{32,40},{40,32},{48,56},{56,48},{64,72... | collective-permute-start | bytes 61448 | tf_op jit(solution)/shard_map/ppermute | solution.py:496
  11.4 1.6 %side.1 = (bf16[4,80,464]{2,1,0:T(8,128)(2,1)S(1)}, bf16[1152,128]{1,0:T(8,128)(2,1)S(1)}, bf16[1152,128]{1,0:T(8,128)(2,1)S(1)}, bf16[1536,256]{1,0:T(8,128)(2,...) custom-call(s32[4,128]{1,0:T(4,128)} %bitcast.3, ...), custom_call_target="tpu_custom_call" | custom-call | tf_op jit(solution)/shard_map/side/pallas_call | solution.py:456
  13.0 2.1 %collective-permute-start.3 = (bf16[3,16,128]{2,1,0:T(8,128)(2,1)S(1)}, bf16[3,16,128]{2,1,0:T(8,128)(2,1)S(1)}, u32[]{:S(2)}, u32[]{:S(2)}) collective-permute-start(bf16[3,16,128]{2,1,0:T(8,128)(2,1)S(1)} %collective-permute-done.refs_2_), channel_id=1, source_target_pairs={{0,8},{8,0},{16,24},{24,16},{32,40},{40,32},{48,56},{56,48},{64,72... | collective-permute-start | bytes 36872 | tf_op jit(solution)/shard_map/ppermute | solution.py:503
  16.3 1.2 %border_128_0.1 = (bf16[16,16,128]{2,1,0:T(8,128)(2,1)S(1)}, bf16[3,16,128]{2,1,0:T(8,128)(2,1)S(1)}, bf16[3,16,128]{2,1,0:T(8,128)(2,1)S(1)}, bf16[5,16,128]{2,1,0:T(8,128)(2,1)S(1)}) custom-call(bf16[16,16,128]{2,1,0:T(8,128)(2,1)S(1)} %get-tuple-element.69.refs_0_.strips_ref.refs_11_, bf16[16,16,128]{2,1,0:T(8,128)(2,1)S(1)} %get-tuple-element.71.refs_1_, ...), custom_call_target="tpu_custom_call" | custom-call | tf_op jit(solution)/shard_map/border_128_0/pallas_call | solution.py:456
  17.6 3.4 %collective-permute-start.6 = (bf16[3,16,128]{2,1,0:T(8,128)(2,1)S(1)}, bf16[3,16,128]{2,1,0:T(8,128)(2,1)S(1)}, u32[]{:S(2)}, u32[]{:S(2)}) collective-permute-start(bf16[3,16,128]{2,1,0:T(8,128)(2,1)S(1)} %get-tuple-element.89), channel_id=1, source_target_pairs={{0,240},{8,248},{16,32},{24,40},{32,16},{40,24},{48,64},{56,72},{6... | collective-permute-start | bytes 36872 | tf_op jit(solution)/shard_map/ppermute | solution.py:494
  21.5 1.2 %inner_128.1 = (bf16[2,2,14,16,128]{4,3,2,1,0:T(8,128)(2,1)S(1)}, bf16[16,16,128]{2,1,0:T(8,128)(2,1)S(1)}, bf16[2,2,14,16,128]{4,3,2,1,0:T(8,128)(2,1)S(1)}) custom-call(bf16[4,16,16,128]{3,2,1,0:T(8,128)(2,1)S(1)} %get-tuple-element.70.refs_8_.field_ref, bf16[16,16,128]{2,1,0:T(8,128)(2,1)S(1)} %get-tuple-element.69.refs_0_.strips_ref.refs_11_, ...), custom_call_target="tpu_custom_call" | custom-call | tf_op jit(solution)/shard_map/inner_128/pallas_call | solution.py:456
  23.8 1.6 %collective-permute-start.8 = (bf16[3,16,128]{2,1,0:T(8,128)(2,1)S(1)}, bf16[3,16,128]{2,1,0:T(8,128)(2,1)S(1)}, u32[]{:S(2)}, u32[]{:S(2)}) collective-permute-start(bf16[3,16,128]{2,1,0:T(8,128)(2,1)S(1)} %collective-permute-done.5.refs_2_), channel_id=1, source_target_pairs={{0,8},{8,0},{16,24},{24,16},{32,40},{40,32},{48,56},{56,48},{64,72... | collective-permute-start | bytes 36872 | tf_op jit(solution)/shard_map/ppermute | solution.py:503
  26.6 2.5 %collective-permute-start.13 = (bf16[2,2,14,16,128]{4,3,2,1,0:T(8,128)(2,1)S(1)}, bf16[2,2,14,16,128]{4,3,2,1,0:T(8,128)(2,1)S(1)}, u32[]{:S(2)}, u32[]{:S(2)}) collective-permute-start(bf16[2,2,14,16,128]{4,3,2,1,0:T(8,128)(2,1)S(1)} %inner_second.1.own_ref), channel_id=1, source_target_pairs={{0,6},{2,4},{4,2},{6,0},{1,7},{3,5},{5,3},{7,1},{8,14},{10,12},{12... | collective-permute-start | bytes 688136 | tf_op jit(solution)/shard_map/ppermute | solution.py:509
  29.1 1.0 %border_128_1.1.refs_3_.own_ref = bf16[16,16,128]{2,1,0:T(8,128)(2,1)S(1)} custom-call(bf16[16,16,128]{2,1,0:T(8,128)(2,1)S(1)} %get-tuple-element.81.strips_ref.refs_0_, bf16[16,16,128]{2,1,0:T(8,128)(2,1)S(1)} %get-tuple-element.87.refs_1_, bf16[3,16,128]{2,1,0:T(8,128)(2,1)S(1)} %collective-permute-done.5.refs_2_, ...), custom_call_target="tpu_custom_call" | custom-call | tf_op jit(solution)/shard_map/border_128_1/pallas_call | solution.py:456
  31.0 2.5 %collective-permute-start.12 = (bf16[16,16,128]{2,1,0:T(8,128)(2,1)S(1)}, bf16[16,16,128]{2,1,0:T(8,128)(2,1)S(1)}, u32[]{:S(2)}, u32[]{:S(2)}) collective-permute-start(bf16[16,16,128]{2,1,0:T(8,128)(2,1)S(1)} %border_128_1.1.refs_3_.own_ref), channel_id=1, source_target_pairs={{0,6},{2,4},{4,2},{6,0},{1,7},{3,5},{5,3},{7,1},{8,14},{10,12},{12... | collective-permute-start | bytes 196616 | tf_op jit(solution)/shard_map/ppermute | solution.py:509
  33.5 1.7 %weights.1 = (bf16[1152,128]{1,0:T(8,128)(2,1)S(1)}, bf16[1152,128]{1,0:T(8,128)(2,1)S(1)}, bf16[1536,256]{1,0:T(8,128)(2,1)S(1)}, bf16[1536,256]{1,0:T(8,128)(2...) custom-call(bf16[2,2,9,64,64]{4,3,2,1,0:T(8,128)(2,1)} %refs_0_.1, ...), custom_call_target="tpu_custom_call" | custom-call | tf_op jit(solution)/shard_map/weights/pallas_call | solution.py:456
  35.2 2.5 %collective-permute-done.12.three_ref = bf16[16,16,128]{2,1,0:T(8,128)(2,1)S(1)} collective-permute-done((bf16[16,16,128]{2,1,0:T(8,128)(2,1)S(1)}, bf16[16,16,128]{2,1,0:T(8,128)(2,1)S(1)}, u32[]{:S(2)}, u32[]{:S(2)}) %collective-permute-start.12) | collective-permute-done | bytes 65568 | tf_op jit(solution)/shard_map/ppermute | solution.py:509
  38.6 3.1 %collective-permute-start.14 = (bf16[3,16,512]{2,1,0:T(8,128)(2,1)S(1)}, bf16[3,16,512]{2,1,0:T(8,128)(2,1)S(1)}, u32[]{:S(2)}, u32[]{:S(2)}) collective-permute-start(bf16[3,16,512]{2,1,0:T(8,128)(2,1)S(1)} %get-tuple-element.111), channel_id=1, source_target_pairs={{0,240},{8,248},{16,32},{24,40},{32,16},{40,24},{48,64},{56,72},{6... | collective-permute-start | bytes 147464 | tf_op jit(solution)/shard_map/ppermute | solution.py:494
  41.7 1.5 %collective-permute-start.18 = (bf16[5,16,512]{2,1,0:T(8,128)(2,1)S(1)}, bf16[5,16,512]{2,1,0:T(8,128)(2,1)S(1)}, u32[]{:S(2)}, u32[]{:S(2)}) collective-permute-start(bf16[5,16,512]{2,1,0:T(8,128)(2,1)S(1)} %get-tuple-element.117), channel_id=1, source_target_pairs={{0,8},{8,0},{16,24},{24,16},{32,40},{40,32},{48,56},{56,48},{64,72... | collective-permute-start | bytes 245768 | tf_op jit(solution)/shard_map/ppermute | solution.py:496
  43.9 1.3 %collective-permute-done.16.two_ref = bf16[2,2,14,16,128]{4,3,2,1,0:T(8,128)(2,1)S(1)} collective-permute-done((bf16[2,2,14,16,128]{4,3,2,1,0:T(8,128)(2,1)S(1)}, bf16[2,2,14,16,128]{4,3,2,1,0:T(8,128)(2,1)S(1)}, u32[]{:S(2)}, u32[]{:S(2)}) %collective-permute-start.16) | collective-permute-done | bytes 229408 | tf_op jit(solution)/shard_map/ppermute | solution.py:509
  45.2 1.8 %mix_tiles.1 = (bf16[2,2,14,16,512]{4,3,2,1,0:T(8,128)(2,1)S(1)}, bf16[16,16,512]{2,1,0:T(8,128)(2,1)S(1)}) custom-call(bf16[2,2,14,16,128]{4,3,2,1,0:T(8,128)(2,1)S(1)} %inner_second.1.own_ref, bf16[2,2,14,16,128]{4,3,2,1,0:T(8,128)(2,1)S(1)} %collective-permute-done.15.one_ref, bf16[2,2,14,16,128]{4,3,2,1,0:T(8,128)(2,1)S(1)} %collective-permute-done.16.two_ref, ...), custom_call_target="tpu_custom_call" | custom-call | tf_op jit(solution)/shard_map/mix_tiles/pallas_call | solution.py:456
  47.0 1.3 %collective-permute-start.20 = (bf16[3,16,512]{2,1,0:T(8,128)(2,1)S(1)}, bf16[3,16,512]{2,1,0:T(8,128)(2,1)S(1)}, u32[]{:S(2)}, u32[]{:S(2)}) collective-permute-start(bf16[3,16,512]{2,1,0:T(8,128)(2,1)S(1)} %collective-permute-done.14.refs_3_), channel_id=1, source_target_pairs={{0,8},{8,0},{16,24},{24,16},{32,40},{40,32},{48,56},{56,48},{64,72... | collective-permute-start | bytes 147464 | tf_op jit(solution)/shard_map/ppermute | solution.py:503
  49.2 1.8 %border_512_0.1 = (bf16[16,16,512]{2,1,0:T(8,128)(2,1)S(1)}, bf16[3,16,512]{2,1,0:T(8,128)(2,1)S(1)}, bf16[3,16,512]{2,1,0:T(8,128)(2,1)S(1)}, bf16[5,16,512]{2,1,0:T(8,128)(2,1)S(1)}) custom-call(bf16[16,16,512]{2,1,0:T(8,128)(2,1)S(1)} %get-tuple-element.110.refs_0_.strips_ref.refs_10_, bf16[16,16,512]{2,1,0:T(8,128)(2,1)S(1)} %get-tuple-element.114.refs_1_, ...), custom_call_target="tpu_custom_call" | custom-call | tf_op jit(solution)/shard_map/border_512_0/pallas_call | solution.py:456
  51.1 3.1 %collective-permute-start.22 = (bf16[3,16,512]{2,1,0:T(8,128)(2,1)S(1)}, bf16[3,16,512]{2,1,0:T(8,128)(2,1)S(1)}, u32[]{:S(2)}, u32[]{:S(2)}) collective-permute-start(bf16[3,16,512]{2,1,0:T(8,128)(2,1)S(1)} %get-tuple-element.126), channel_id=1, source_target_pairs={{0,240},{8,248},{16,32},{24,40},{32,16},{40,24},{48,64},{56,72},{6... | collective-permute-start | bytes 147464 | tf_op jit(solution)/shard_map/ppermute | solution.py:494
  54.9 2.6 %inner_512.1 = (bf16[2,2,14,16,512]{4,3,2,1,0:T(8,128)(2,1)S(1)}, bf16[16,16,512]{2,1,0:T(8,128)(2,1)S(1)}) custom-call(bf16[2,2,14,16,512]{4,3,2,1,0:T(8,128)(2,1)S(1)} %get-tuple-element.121.field_ref.state_ref, bf16[16,16,512]{2,1,0:T(8,128)(2,1)S(1)} %get-tuple-element.110.refs_0_.strips_ref.refs_10_, ...), custom_call_target="tpu_custom_call" | custom-call | tf_op jit(solution)/shard_map/inner_512/pallas_call | solution.py:456
  57.6 3.5 %last_inner.1.refs_13_ = bf16[2,2,14,16,128]{4,3,2,1,0:T(8,128)(2,1)S(1)} custom-call(bf16[2,2,14,16,512]{4,3,2,1,0:T(8,128)(2,1)S(1)} %get-tuple-element.127.field_ref, bf16[16,16,512]{2,1,0:T(8,128)(2,1)S(1)} %get-tuple-element.119.strips_ref.refs_0_, bf16[1536,256]{1,0:T(8,128)(2,1)S(1)} %get-tuple-element.128.weight_ref, ...), custom_call_target="tpu_custom_call" | custom-call | tf_op jit(solution)/shard_map/last_inner/pallas_call | solution.py:456
  62.6 2.9 %last_border.1 = bf16[4,16,16,128]{3,2,1,0:T(8,128)(2,1)} custom-call(bf16[16,16,512]{2,1,0:T(8,128)(2,1)S(1)} %get-tuple-element.119.strips_ref.refs_0_, bf16[16,16,512]{2,1,0:T(8,128)(2,1)S(1)} %get-tuple-element.124.refs_1_, bf16[3,16,512]{2,1,0:T(8,128)(2,1)S(1)} %collective-permute-done.21.refs_2_, ...), custom_call_target="tpu_custom_call" | custom-call | tf_op jit(solution)/shard_map/last_border/pallas_call | solution.py:456
  (43 shorter events, 9.6 us)
Async XLA Ops:
  1.3 11.7 %collective-permute-start.1 = (bf16[3,16,128]{2,1,0:T(8,128)(2,1)S(1)}, bf16[3,16,128]{2,1,0:T(8,128)(2,1)S(1)}, u32[]{:S(2)}, u32[]{:S(2)}) collective-permute-start(bf16[3,16,128]{2,1,0:T(8,128)(2,1)S(1)} %get-tuple-element.73), channel_id=1, source_target_pairs={{0,240},{8,248},{16,32},{24,40},{32,16},{40,24},{48,64},{56,72},{6... | collective-permute-start | bytes 36872 | tf_op jit(solution)/shard_map/ppermute | solution.py:494
  10.4 2.6 %collective-permute-start = (bf16[3,16,128]{2,1,0:T(8,128)(2,1)S(1)}, bf16[3,16,128]{2,1,0:T(8,128)(2,1)S(1)}, u32[]{:S(2)}, u32[]{:S(2)}) collective-permute-start(bf16[3,16,128]{2,1,0:T(8,128)(2,1)S(1)} %get-tuple-element.72), channel_id=1, source_target_pairs={{0,16},{8,24},{16,0},{24,8},{32,48},{40,56},{48,32},{56,40},{64,80... | collective-permute-start | bytes 36872 | tf_op jit(solution)/shard_map/ppermute | solution.py:495
  10.5 4.7 %collective-permute-start.2 = (bf16[5,16,128]{2,1,0:T(8,128)(2,1)S(1)}, bf16[5,16,128]{2,1,0:T(8,128)(2,1)S(1)}, u32[]{:S(2)}, u32[]{:S(2)}) collective-permute-start(bf16[5,16,128]{2,1,0:T(8,128)(2,1)S(1)} %get-tuple-element.76), channel_id=1, source_target_pairs={{0,8},{8,0},{16,24},{24,16},{32,40},{40,32},{48,56},{56,48},{64,72... | collective-permute-start | bytes 61448 | tf_op jit(solution)/shard_map/ppermute | solution.py:496
  13.0 2.9 %collective-permute-start.3 = (bf16[3,16,128]{2,1,0:T(8,128)(2,1)S(1)}, bf16[3,16,128]{2,1,0:T(8,128)(2,1)S(1)}, u32[]{:S(2)}, u32[]{:S(2)}) collective-permute-start(bf16[3,16,128]{2,1,0:T(8,128)(2,1)S(1)} %collective-permute-done.refs_2_), channel_id=1, source_target_pairs={{0,8},{8,0},{16,24},{24,16},{32,40},{40,32},{48,56},{56,48},{64,72... | collective-permute-start | bytes 36872 | tf_op jit(solution)/shard_map/ppermute | solution.py:503
  17.5 6.0 %collective-permute-start.5 = (bf16[3,16,128]{2,1,0:T(8,128)(2,1)S(1)}, bf16[3,16,128]{2,1,0:T(8,128)(2,1)S(1)}, u32[]{:S(2)}, u32[]{:S(2)}) collective-permute-start(bf16[3,16,128]{2,1,0:T(8,128)(2,1)S(1)} %get-tuple-element.82), channel_id=1, source_target_pairs={{0,16},{8,24},{16,0},{24,8},{32,48},{40,56},{48,32},{56,40},{64,80... | collective-permute-start | bytes 36872 | tf_op jit(solution)/shard_map/ppermute | solution.py:495
  17.6 6.2 %collective-permute-start.6 = (bf16[3,16,128]{2,1,0:T(8,128)(2,1)S(1)}, bf16[3,16,128]{2,1,0:T(8,128)(2,1)S(1)}, u32[]{:S(2)}, u32[]{:S(2)}) collective-permute-start(bf16[3,16,128]{2,1,0:T(8,128)(2,1)S(1)} %get-tuple-element.89), channel_id=1, source_target_pairs={{0,240},{8,248},{16,32},{24,40},{32,16},{40,24},{48,64},{56,72},{6... | collective-permute-start | bytes 36872 | tf_op jit(solution)/shard_map/ppermute | solution.py:494
  21.0 4.4 %collective-permute-start.7 = (bf16[5,16,128]{2,1,0:T(8,128)(2,1)S(1)}, bf16[5,16,128]{2,1,0:T(8,128)(2,1)S(1)}, u32[]{:S(2)}, u32[]{:S(2)}) collective-permute-start(bf16[5,16,128]{2,1,0:T(8,128)(2,1)S(1)} %get-tuple-element.95), channel_id=1, source_target_pairs={{0,8},{8,0},{16,24},{24,16},{32,40},{40,32},{48,56},{56,48},{64,72... | collective-permute-start | bytes 61448 | tf_op jit(solution)/shard_map/ppermute | solution.py:496
  23.8 2.4 %collective-permute-start.8 = (bf16[3,16,128]{2,1,0:T(8,128)(2,1)S(1)}, bf16[3,16,128]{2,1,0:T(8,128)(2,1)S(1)}, u32[]{:S(2)}, u32[]{:S(2)}) collective-permute-start(bf16[3,16,128]{2,1,0:T(8,128)(2,1)S(1)} %collective-permute-done.5.refs_2_), channel_id=1, source_target_pairs={{0,8},{8,0},{16,24},{24,16},{32,40},{40,32},{48,56},{56,48},{64,72... | collective-permute-start | bytes 36872 | tf_op jit(solution)/shard_map/ppermute | solution.py:503
  26.6 11.1 %collective-permute-start.13 = (bf16[2,2,14,16,128]{4,3,2,1,0:T(8,128)(2,1)S(1)}, bf16[2,2,14,16,128]{4,3,2,1,0:T(8,128)(2,1)S(1)}, u32[]{:S(2)}, u32[]{:S(2)}) collective-permute-start(bf16[2,2,14,16,128]{4,3,2,1,0:T(8,128)(2,1)S(1)} %inner_second.1.own_ref), channel_id=1, source_target_pairs={{0,6},{2,4},{4,2},{6,0},{1,7},{3,5},{5,3},{7,1},{8,14},{10,12},{12... | collective-permute-start | bytes 688136 | tf_op jit(solution)/shard_map/ppermute | solution.py:509
  30.1 5.0 %collective-permute-start.10 = (bf16[16,16,128]{2,1,0:T(8,128)(2,1)S(1)}, bf16[16,16,128]{2,1,0:T(8,128)(2,1)S(1)}, u32[]{:S(2)}, u32[]{:S(2)}) collective-permute-start(bf16[16,16,128]{2,1,0:T(8,128)(2,1)S(1)} %border_128_1.1.refs_3_.own_ref), channel_id=1, source_target_pairs={{0,4},{2,6},{4,0},{6,2},{1,5},{3,7},{5,1},{7,3},{8,12},{10,14},{12... | collective-permute-start | bytes 196616 | tf_op jit(solution)/shard_map/ppermute | solution.py:509
  30.7 4.4 %collective-permute-start.11 = (bf16[16,16,128]{2,1,0:T(8,128)(2,1)S(1)}, bf16[16,16,128]{2,1,0:T(8,128)(2,1)S(1)}, u32[]{:S(2)}, u32[]{:S(2)}) collective-permute-start(bf16[16,16,128]{2,1,0:T(8,128)(2,1)S(1)} %border_128_1.1.refs_3_.own_ref), channel_id=1, source_target_pairs={{0,2},{2,0},{4,6},{6,4},{1,3},{3,1},{5,7},{7,5},{8,10},{10,8},{12,... | collective-permute-start | bytes 196616 | tf_op jit(solution)/shard_map/ppermute | solution.py:509
  31.0 6.7 %collective-permute-start.12 = (bf16[16,16,128]{2,1,0:T(8,128)(2,1)S(1)}, bf16[16,16,128]{2,1,0:T(8,128)(2,1)S(1)}, u32[]{:S(2)}, u32[]{:S(2)}) collective-permute-start(bf16[16,16,128]{2,1,0:T(8,128)(2,1)S(1)} %border_128_1.1.refs_3_.own_ref), channel_id=1, source_target_pairs={{0,6},{2,4},{4,2},{6,0},{1,7},{3,5},{5,3},{7,1},{8,14},{10,12},{12... | collective-permute-start | bytes 196616 | tf_op jit(solution)/shard_map/ppermute | solution.py:509
  33.5 10.4 %collective-permute-start.15 = (bf16[2,2,14,16,128]{4,3,2,1,0:T(8,128)(2,1)S(1)}, bf16[2,2,14,16,128]{4,3,2,1,0:T(8,128)(2,1)S(1)}, u32[]{:S(2)}, u32[]{:S(2)}) collective-permute-start(bf16[2,2,14,16,128]{4,3,2,1,0:T(8,128)(2,1)S(1)} %inner_second.1.own_ref), channel_id=1, source_target_pairs={{0,2},{2,0},{4,6},{6,4},{1,3},{3,1},{5,7},{7,5},{8,10},{10,8},{12,... | collective-permute-start | bytes 688136 | tf_op jit(solution)/shard_map/ppermute | solution.py:509
  37.7 7.5 %collective-permute-start.16 = (bf16[2,2,14,16,128]{4,3,2,1,0:T(8,128)(2,1)S(1)}, bf16[2,2,14,16,128]{4,3,2,1,0:T(8,128)(2,1)S(1)}, u32[]{:S(2)}, u32[]{:S(2)}) collective-permute-start(bf16[2,2,14,16,128]{4,3,2,1,0:T(8,128)(2,1)S(1)} %collective-permute-done.13.three_ref), channel_id=1, source_target_pairs={{0,2},{2,0},{4,6},{6,4},{1,3},{3,1},{5,7},{7,5},{8,10},{10,8},{12,... | collective-permute-start | bytes 688136 | tf_op jit(solution)/shard_map/ppermute | solution.py:509
  38.5 4.8 %collective-permute-start.17 = (bf16[3,16,512]{2,1,0:T(8,128)(2,1)S(1)}, bf16[3,16,512]{2,1,0:T(8,128)(2,1)S(1)}, u32[]{:S(2)}, u32[]{:S(2)}) collective-permute-start(bf16[3,16,512]{2,1,0:T(8,128)(2,1)S(1)} %get-tuple-element.115), channel_id=1, source_target_pairs={{0,16},{8,24},{16,0},{24,8},{32,48},{40,56},{48,32},{56,40},{64,80... | collective-permute-start | bytes 147464 | tf_op jit(solution)/shard_map/ppermute | solution.py:495
  38.6 8.5 %collective-permute-start.14 = (bf16[3,16,512]{2,1,0:T(8,128)(2,1)S(1)}, bf16[3,16,512]{2,1,0:T(8,128)(2,1)S(1)}, u32[]{:S(2)}, u32[]{:S(2)}) collective-permute-start(bf16[3,16,512]{2,1,0:T(8,128)(2,1)S(1)} %get-tuple-element.111), channel_id=1, source_target_pairs={{0,240},{8,248},{16,32},{24,40},{32,16},{40,24},{48,64},{56,72},{6... | collective-permute-start | bytes 147464 | tf_op jit(solution)/shard_map/ppermute | solution.py:494
  41.7 6.6 %collective-permute-start.18 = (bf16[5,16,512]{2,1,0:T(8,128)(2,1)S(1)}, bf16[5,16,512]{2,1,0:T(8,128)(2,1)S(1)}, u32[]{:S(2)}, u32[]{:S(2)}) collective-permute-start(bf16[5,16,512]{2,1,0:T(8,128)(2,1)S(1)} %get-tuple-element.117), channel_id=1, source_target_pairs={{0,8},{8,0},{16,24},{24,16},{32,40},{40,32},{48,56},{56,48},{64,72... | collective-permute-start | bytes 245768 | tf_op jit(solution)/shard_map/ppermute | solution.py:496
  43.2 5.1 %collective-permute-start.19 = (bf16[3,16,512]{2,1,0:T(8,128)(2,1)S(1)}, bf16[3,16,512]{2,1,0:T(8,128)(2,1)S(1)}, u32[]{:S(2)}, u32[]{:S(2)}) collective-permute-start(bf16[3,16,512]{2,1,0:T(8,128)(2,1)S(1)} %collective-permute-done.17.refs_2_), channel_id=1, source_target_pairs={{0,8},{8,0},{16,24},{24,16},{32,40},{40,32},{48,56},{56,48},{64,72... | collective-permute-start | bytes 147464 | tf_op jit(solution)/shard_map/ppermute | solution.py:503
  47.0 2.2 %collective-permute-start.20 = (bf16[3,16,512]{2,1,0:T(8,128)(2,1)S(1)}, bf16[3,16,512]{2,1,0:T(8,128)(2,1)S(1)}, u32[]{:S(2)}, u32[]{:S(2)}) collective-permute-start(bf16[3,16,512]{2,1,0:T(8,128)(2,1)S(1)} %collective-permute-done.14.refs_3_), channel_id=1, source_target_pairs={{0,8},{8,0},{16,24},{24,16},{32,40},{40,32},{48,56},{56,48},{64,72... | collective-permute-start | bytes 147464 | tf_op jit(solution)/shard_map/ppermute | solution.py:503
  51.0 10.1 %collective-permute-start.21 = (bf16[3,16,512]{2,1,0:T(8,128)(2,1)S(1)}, bf16[3,16,512]{2,1,0:T(8,128)(2,1)S(1)}, u32[]{:S(2)}, u32[]{:S(2)}) collective-permute-start(bf16[3,16,512]{2,1,0:T(8,128)(2,1)S(1)} %get-tuple-element.120), channel_id=1, source_target_pairs={{0,16},{8,24},{16,0},{24,8},{32,48},{40,56},{48,32},{56,40},{64,80... | collective-permute-start | bytes 147464 | tf_op jit(solution)/shard_map/ppermute | solution.py:495
  51.1 10.0 %collective-permute-start.22 = (bf16[3,16,512]{2,1,0:T(8,128)(2,1)S(1)}, bf16[3,16,512]{2,1,0:T(8,128)(2,1)S(1)}, u32[]{:S(2)}, u32[]{:S(2)}) collective-permute-start(bf16[3,16,512]{2,1,0:T(8,128)(2,1)S(1)} %get-tuple-element.126), channel_id=1, source_target_pairs={{0,240},{8,248},{16,32},{24,40},{32,16},{40,24},{48,64},{56,72},{6... | collective-permute-start | bytes 147464 | tf_op jit(solution)/shard_map/ppermute | solution.py:494
  54.3 7.5 %collective-permute-start.23 = (bf16[5,16,512]{2,1,0:T(8,128)(2,1)S(1)}, bf16[5,16,512]{2,1,0:T(8,128)(2,1)S(1)}, u32[]{:S(2)}, u32[]{:S(2)}) collective-permute-start(bf16[5,16,512]{2,1,0:T(8,128)(2,1)S(1)} %get-tuple-element.130), channel_id=1, source_target_pairs={{0,8},{8,0},{16,24},{24,16},{32,40},{40,32},{48,56},{56,48},{64,72... | collective-permute-start | bytes 245768 | tf_op jit(solution)/shard_map/ppermute | solution.py:496
  61.1 1.3 %collective-permute-start.24 = (bf16[3,16,512]{2,1,0:T(8,128)(2,1)S(1)}, bf16[3,16,512]{2,1,0:T(8,128)(2,1)S(1)}, u32[]{:S(2)}, u32[]{:S(2)}) collective-permute-start(bf16[3,16,512]{2,1,0:T(8,128)(2,1)S(1)} %collective-permute-done.21.refs_2_), channel_id=1, source_target_pairs={{0,8},{8,0},{16,24},{24,16},{32,40},{40,32},{48,56},{56,48},{64,72... | collective-permute-start | bytes 147464 | tf_op jit(solution)/shard_map/ppermute | solution.py:503
  61.2 1.4 %collective-permute-start.25 = (bf16[3,16,512]{2,1,0:T(8,128)(2,1)S(1)}, bf16[3,16,512]{2,1,0:T(8,128)(2,1)S(1)}, u32[]{:S(2)}, u32[]{:S(2)}) collective-permute-start(bf16[3,16,512]{2,1,0:T(8,128)(2,1)S(1)} %collective-permute-done.22.refs_3_), channel_id=1, source_target_pairs={{0,8},{8,0},{16,24},{24,16},{32,40},{40,32},{48,56},{56,48},{64,72... | collective-permute-start | bytes 147464 | tf_op jit(solution)/shard_map/ppermute | solution.py:503
  (3 other events, 7.4 us)

commit v6 on v4

--- a/solution.py
+++ b/solution.py
@@ -564,19 +564,19 @@
         second_inner_kernel, "inner_second", [V] * 5, [V], arrays(tiles_shape(thin)), tile_scratch(thin),
         (inner, inner_edge, wide2, tiled, before),
     )
-    received, inner_ring, field = receive(sent, (inner_ring,), (field,))
+    narrow3, narrow4, wide3, wide4, mix_in, mix_out = call(
+        weights_kernel, "weights", [H] * 3 + [V], [V] * 6,
+        arrays(*shape_w, mix_in.shape, mix_out.shape),
+        [pltpu.VMEM(conv_weight.shape[1:], BF16), pltpu.SemaphoreType.DMA((3,))],
+        (conv_weight, mix_in, mix_out, inner_edge),
+    )
+    received, inner_ring, field, mix_in = receive(sent, (inner_ring,), (field, mix_in))
     *received, field = lax.optimization_barrier((*received, field))
     one, three = from_level(field, 1), from_level(field, 3)
     (edge,) = border(True, False, inner_edge, inner_ring, received, narrow2, (strips,))
 
     parts = [from_level(edge, d) for d in (2, 1, 3)]
-    narrow3, narrow4, wide1, wide2, mix_in, mix_out = call(
-        weights_kernel, "weights", [H] * 3 + [V], [V] * 6,
-        arrays(*shape_w, mix_in.shape, mix_out.shape),
-        [pltpu.VMEM(conv_weight.shape[1:], BF16), pltpu.SemaphoreType.DMA((3,))],
-        (conv_weight, mix_in, mix_out, edge),
-    )
-    *parts, mix_in, three = lax.optimization_barrier((*parts, mix_in, three))
+    *parts, three = lax.optimization_barrier((*parts, three))
     edge_parts = [edge, parts[1], parts[0], parts[2]]
     fields = [field, one, from_level(three, 1), three]
     strips, *messages = call(
@@ -595,11 +595,11 @@
     inner_edge, *messages = border(False, True, strips, ring1, received, narrow3)
 
     sent = send(*messages)
-    inner, inner_ring = interior(field, strips, wide1, tiled)
+    inner, inner_ring = interior(field, strips, wide3, tiled)
     tiles = call(
         functools.partial(last_inner_kernel, 1), "last_inner",
         [V] * 7, V, arrays(tiles_shape(thin))[0], tile_scratch(wide),
-        (inner, inner_edge, wide2, tiled, field, mix_in, mix_out),
+        (inner, inner_edge, wide4, tiled, field, mix_in, mix_out),
     )
     received, inner_ring, tiles = receive(sent, (inner_ring,), (tiles,))
     return call(

time: 65.7 us -> 65.7 us (level)
  starting transfers between devices: 34.7 us -> 33.8 us
  waiting for transfers between devices: 8.34 us -> 9.18 us
    ppermute x6, waiting for transfers between devices: 3.85 us -> 5.37 us  [from_level(): lax.ppermute(shard, 'level', [(i, i ^ distance) for i in range(levels)])]
    ppermute x4, starting transfers between devices: 4.41 us -> 3.1 us  [receive(): lax.ppermute(near, 'face', pairs)]
where the time goes in v6:
time: 65.7 us; the launch traced here: 65.5 us
  starting transfers between devices  33.8 us (51%)
  Pallas kernels  22.3 us (34%)
  waiting for transfers between devices  9.18 us (14%)
    pallas_call x13, Pallas kernels, call(): pl.pallas_call(kernel, name=name, in_specs=in_specs, out_specs=out_specs,...  22.3 us
    ppermute x4, starting transfers between devices, send(): from_far = lax.ppermute(far, 'face', apart)  19 us
    ppermute x6, starting transfers between devices, from_level(): lax.ppermute(shard, 'level', [(i, i ^ distance) for i in range(levels)])  5.82 us
    ppermute x6, waiting for transfers between devices, from_level(): lax.ppermute(shard, 'level', [(i, i ^ distance) for i in range(levels)])  5.37 us
    ppermute x4, starting transfers between devices, send(): lax.ppermute(to_pair, 'face', [(i, i ^ 1) for i in range(faces)])  3.54 us
    ppermute x4, starting transfers between devices, receive(): lax.ppermute(near, 'face', pairs)  3.1 us
    ppermute x4, waiting for transfers between devices, receive(): lax.ppermute(near, 'face', pairs)  2.21 us
    ppermute x4, starting transfers between devices, receive(): lax.ppermute(far, 'face', pairs)  2.1 us
  transfers between devices with their start and end apart: 26, of which 10 were waited for; matrix products, arithmetic and copies ran while one was open for 0% of the time, Pallas kernels for 23%

profile of v6, /device:TPU:1, one launch (start us, length us, event | category | flops | bytes accessed | tf_op | source)
XLA Modules:
  0.0 65.5 jit_solution(7015226064351307976)
XLA Ops:
  0.0 1.3 %first.1 = (bf16[16,16,128]{2,1,0:T(8,128)(2,1)S(1)}, bf16[3,16,128]{2,1,0:T(8,128)(2,1)S(1)}, bf16[3,16,128]{2,1,0:T(8,128)(2,1)S(1)}, bf16[5,16,128]{2,1,0:T(8...) custom-call(bf16[4,16,16,128]{3,2,1,0:T(8,128)(2,1)} %state_ref.1, s32[4,128]{1,0:T(4,128)} %bitcast.2), custom_call_target="tpu_custom_call" | custom-call | tf_op jit(solution)/shard_map/first/pallas_call | solution.py:450
  1.3 9.1 %collective-permute-start.1 = (bf16[3,16,128]{2,1,0:T(8,128)(2,1)S(1)}, bf16[3,16,128]{2,1,0:T(8,128)(2,1)S(1)}, u32[]{:S(2)}, u32[]{:S(2)}) collective-permute-start(bf16[3,16,128]{2,1,0:T(8,128)(2,1)S(1)} %get-tuple-element.73), channel_id=1, source_target_pairs={{0,240},{8,248},{16,32},{24,40},{32,16},{40,24},{48,64},{56,72},{6... | collective-permute-start | bytes 36872 | tf_op jit(solution)/shard_map/ppermute | solution.py:488
  10.4 1.0 %collective-permute-start.2 = (bf16[5,16,128]{2,1,0:T(8,128)(2,1)S(1)}, bf16[5,16,128]{2,1,0:T(8,128)(2,1)S(1)}, u32[]{:S(2)}, u32[]{:S(2)}) collective-permute-start(bf16[5,16,128]{2,1,0:T(8,128)(2,1)S(1)} %get-tuple-element.76), channel_id=1, source_target_pairs={{0,8},{8,0},{16,24},{24,16},{32,40},{40,32},{48,56},{56,48},{64,72... | collective-permute-start | bytes 61448 | tf_op jit(solution)/shard_map/ppermute | solution.py:490
  11.4 1.6 %side.1 = (bf16[4,80,464]{2,1,0:T(8,128)(2,1)S(1)}, bf16[1152,128]{1,0:T(8,128)(2,1)S(1)}, bf16[1152,128]{1,0:T(8,128)(2,1)S(1)}, bf16[1536,256]{1,0:T(8,128)(2,...) custom-call(s32[4,128]{1,0:T(4,128)} %bitcast.3, ...), custom_call_target="tpu_custom_call" | custom-call | tf_op jit(solution)/shard_map/side/pallas_call | solution.py:450
  13.0 2.1 %collective-permute-start.3 = (bf16[3,16,128]{2,1,0:T(8,128)(2,1)S(1)}, bf16[3,16,128]{2,1,0:T(8,128)(2,1)S(1)}, u32[]{:S(2)}, u32[]{:S(2)}) collective-permute-start(bf16[3,16,128]{2,1,0:T(8,128)(2,1)S(1)} %collective-permute-done.refs_2_), channel_id=1, source_target_pairs={{0,8},{8,0},{16,24},{24,16},{32,40},{40,32},{48,56},{56,48},{64,72... | collective-permute-start | bytes 36872 | tf_op jit(solution)/shard_map/ppermute | solution.py:497
  16.3 1.2 %border_128_0.1 = (bf16[16,16,128]{2,1,0:T(8,128)(2,1)S(1)}, bf16[3,16,128]{2,1,0:T(8,128)(2,1)S(1)}, bf16[3,16,128]{2,1,0:T(8,128)(2,1)S(1)}, bf16[5,16,128]{2,1,0:T(8,128)(2,1)S(1)}) custom-call(bf16[16,16,128]{2,1,0:T(8,128)(2,1)S(1)} %get-tuple-element.69.refs_0_.strips_ref.refs_11_, bf16[16,16,128]{2,1,0:T(8,128)(2,1)S(1)} %get-tuple-element.71.refs_1_, ...), custom_call_target="tpu_custom_call" | custom-call | tf_op jit(solution)/shard_map/border_128_0/pallas_call | solution.py:450
  17.6 3.4 %collective-permute-start.6 = (bf16[3,16,128]{2,1,0:T(8,128)(2,1)S(1)}, bf16[3,16,128]{2,1,0:T(8,128)(2,1)S(1)}, u32[]{:S(2)}, u32[]{:S(2)}) collective-permute-start(bf16[3,16,128]{2,1,0:T(8,128)(2,1)S(1)} %get-tuple-element.89), channel_id=1, source_target_pairs={{0,240},{8,248},{16,32},{24,40},{32,16},{40,24},{48,64},{56,72},{6... | collective-permute-start | bytes 36872 | tf_op jit(solution)/shard_map/ppermute | solution.py:488
  21.5 1.2 %inner_128.1 = (bf16[2,2,14,16,128]{4,3,2,1,0:T(8,128)(2,1)S(1)}, bf16[16,16,128]{2,1,0:T(8,128)(2,1)S(1)}, bf16[2,2,14,16,128]{4,3,2,1,0:T(8,128)(2,1)S(1)}) custom-call(bf16[4,16,16,128]{3,2,1,0:T(8,128)(2,1)S(1)} %get-tuple-element.70.refs_8_.field_ref, bf16[16,16,128]{2,1,0:T(8,128)(2,1)S(1)} %get-tuple-element.69.refs_0_.strips_ref.refs_11_, ...), custom_call_target="tpu_custom_call" | custom-call | tf_op jit(solution)/shard_map/inner_128/pallas_call | solution.py:450
  22.6 1.7 %weights.1 = (bf16[1152,128]{1,0:T(8,128)(2,1)S(1)}, bf16[1152,128]{1,0:T(8,128)(2,1)S(1)}, bf16[1536,256]{1,0:T(8,128)(2,1)S(1)}, bf16[1536,256]{1,0:T(8,128)(2...) custom-call(bf16[2,2,9,64,64]{4,3,2,1,0:T(8,128)(2,1)} %refs_0_.1, ...), custom_call_target="tpu_custom_call" | custom-call | tf_op jit(solution)/shard_map/weights/pallas_call | solution.py:450
  26.6 2.5 %collective-permute-start.13 = (bf16[2,2,14,16,128]{4,3,2,1,0:T(8,128)(2,1)S(1)}, bf16[2,2,14,16,128]{4,3,2,1,0:T(8,128)(2,1)S(1)}, u32[]{:S(2)}, u32[]{:S(2)}) collective-permute-start(bf16[2,2,14,16,128]{4,3,2,1,0:T(8,128)(2,1)S(1)} %inner_second.1.own_ref), channel_id=1, source_target_pairs={{0,6},{2,4},{4,2},{6,0},{1,7},{3,5},{5,3},{7,1},{8,14},{10,12},{12... | collective-permute-start | bytes 688136 | tf_op jit(solution)/shard_map/ppermute | solution.py:503
  29.1 1.0 %border_128_1.1.own_ref = bf16[16,16,128]{2,1,0:T(8,128)(2,1)S(1)} custom-call(bf16[16,16,128]{2,1,0:T(8,128)(2,1)S(1)} %get-tuple-element.81.strips_ref.refs_3_.refs_0_, bf16[16,16,128]{2,1,0:T(8,128)(2,1)S(1)} %get-tuple-element.87.refs_1_, bf16[3,16,128]{2,1,0:T(8,128)(2,1)S(1)} %collective-permute-done.5.refs_2_, ...), custom_call_target="tpu_custom_call" | custom-call | tf_op jit(solution)/shard_map/border_128_1/pallas_call | solution.py:450
  31.0 2.5 %collective-permute-start.12 = (bf16[16,16,128]{2,1,0:T(8,128)(2,1)S(1)}, bf16[16,16,128]{2,1,0:T(8,128)(2,1)S(1)}, u32[]{:S(2)}, u32[]{:S(2)}) collective-permute-start(bf16[16,16,128]{2,1,0:T(8,128)(2,1)S(1)} %border_128_1.1.own_ref), channel_id=1, source_target_pairs={{0,6},{2,4},{4,2},{6,0},{1,7},{3,5},{5,3},{7,1},{8,14},{10,12},{12... | collective-permute-start | bytes 196616 | tf_op jit(solution)/shard_map/ppermute | solution.py:503
  33.5 1.5 %collective-permute-done.10.two_ref = bf16[16,16,128]{2,1,0:T(8,128)(2,1)S(1)} collective-permute-done((bf16[16,16,128]{2,1,0:T(8,128)(2,1)S(1)}, bf16[16,16,128]{2,1,0:T(8,128)(2,1)S(1)}, u32[]{:S(2)}, u32[]{:S(2)}) %collective-permute-start.10) | collective-permute-done | bytes 65568 | tf_op jit(solution)/shard_map/ppermute | solution.py:503
  34.9 2.6 %collective-permute-done.12.three_ref = bf16[16,16,128]{2,1,0:T(8,128)(2,1)S(1)} collective-permute-done((bf16[16,16,128]{2,1,0:T(8,128)(2,1)S(1)}, bf16[16,16,128]{2,1,0:T(8,128)(2,1)S(1)}, u32[]{:S(2)}, u32[]{:S(2)}) %collective-permute-start.12) | collective-permute-done | bytes 65568 | tf_op jit(solution)/shard_map/ppermute | solution.py:503
  38.4 3.3 %collective-permute-start.14 = (bf16[3,16,512]{2,1,0:T(8,128)(2,1)S(1)}, bf16[3,16,512]{2,1,0:T(8,128)(2,1)S(1)}, u32[]{:S(2)}, u32[]{:S(2)}) collective-permute-start(bf16[3,16,512]{2,1,0:T(8,128)(2,1)S(1)} %get-tuple-element.111), channel_id=1, source_target_pairs={{0,240},{8,248},{16,32},{24,40},{32,16},{40,24},{48,64},{56,72},{6... | collective-permute-start | bytes 147464 | tf_op jit(solution)/shard_map/ppermute | solution.py:488
  41.7 1.5 %collective-permute-start.18 = (bf16[5,16,512]{2,1,0:T(8,128)(2,1)S(1)}, bf16[5,16,512]{2,1,0:T(8,128)(2,1)S(1)}, u32[]{:S(2)}, u32[]{:S(2)}) collective-permute-start(bf16[5,16,512]{2,1,0:T(8,128)(2,1)S(1)} %get-tuple-element.117), channel_id=1, source_target_pairs={{0,8},{8,0},{16,24},{24,16},{32,40},{40,32},{48,56},{56,48},{64,72... | collective-permute-start | bytes 245768 | tf_op jit(solution)/shard_map/ppermute | solution.py:490
  43.9 1.3 %collective-permute-done.16.two_ref = bf16[2,2,14,16,128]{4,3,2,1,0:T(8,128)(2,1)S(1)} collective-permute-done((bf16[2,2,14,16,128]{4,3,2,1,0:T(8,128)(2,1)S(1)}, bf16[2,2,14,16,128]{4,3,2,1,0:T(8,128)(2,1)S(1)}, u32[]{:S(2)}, u32[]{:S(2)}) %collective-permute-start.16) | collective-permute-done | bytes 229408 | tf_op jit(solution)/shard_map/ppermute | solution.py:503
  45.2 1.8 %mix_tiles.1 = (bf16[2,2,14,16,512]{4,3,2,1,0:T(8,128)(2,1)S(1)}, bf16[16,16,512]{2,1,0:T(8,128)(2,1)S(1)}) custom-call(bf16[2,2,14,16,128]{4,3,2,1,0:T(8,128)(2,1)S(1)} %inner_second.1.own_ref, bf16[2,2,14,16,128]{4,3,2,1,0:T(8,128)(2,1)S(1)} %collective-permute-done.15.one_ref, bf16[2,2,14,16,128]{4,3,2,1,0:T(8,128)(2,1)S(1)} %collective-permute-done.16.two_ref, ...), custom_call_target="tpu_custom_call" | custom-call | tf_op jit(solution)/shard_map/mix_tiles/pallas_call | solution.py:450
  47.0 1.3 %collective-permute-start.20 = (bf16[3,16,512]{2,1,0:T(8,128)(2,1)S(1)}, bf16[3,16,512]{2,1,0:T(8,128)(2,1)S(1)}, u32[]{:S(2)}, u32[]{:S(2)}) collective-permute-start(bf16[3,16,512]{2,1,0:T(8,128)(2,1)S(1)} %collective-permute-done.14.refs_3_), channel_id=1, source_target_pairs={{0,8},{8,0},{16,24},{24,16},{32,40},{40,32},{48,56},{56,48},{64,72... | collective-permute-start | bytes 147464 | tf_op jit(solution)/shard_map/ppermute | solution.py:497
  49.2 1.8 %border_512_0.1 = (bf16[16,16,512]{2,1,0:T(8,128)(2,1)S(1)}, bf16[3,16,512]{2,1,0:T(8,128)(2,1)S(1)}, bf16[3,16,512]{2,1,0:T(8,128)(2,1)S(1)}, bf16[5,16,512]{2,1,0:T(8,128)(2,1)S(1)}) custom-call(bf16[16,16,512]{2,1,0:T(8,128)(2,1)S(1)} %get-tuple-element.110.refs_0_.strips_ref.refs_10_, bf16[16,16,512]{2,1,0:T(8,128)(2,1)S(1)} %get-tuple-element.114.refs_1_, ...), custom_call_target="tpu_custom_call" | custom-call | tf_op jit(solution)/shard_map/border_512_0/pallas_call | solution.py:450
  51.1 3.1 %collective-permute-start.22 = (bf16[3,16,512]{2,1,0:T(8,128)(2,1)S(1)}, bf16[3,16,512]{2,1,0:T(8,128)(2,1)S(1)}, u32[]{:S(2)}, u32[]{:S(2)}) collective-permute-start(bf16[3,16,512]{2,1,0:T(8,128)(2,1)S(1)} %get-tuple-element.126), channel_id=1, source_target_pairs={{0,240},{8,248},{16,32},{24,40},{32,16},{40,24},{48,64},{56,72},{6... | collective-permute-start | bytes 147464 | tf_op jit(solution)/shard_map/ppermute | solution.py:488
  54.9 2.6 %inner_512.1 = (bf16[2,2,14,16,512]{4,3,2,1,0:T(8,128)(2,1)S(1)}, bf16[16,16,512]{2,1,0:T(8,128)(2,1)S(1)}) custom-call(bf16[2,2,14,16,512]{4,3,2,1,0:T(8,128)(2,1)S(1)} %get-tuple-element.121.field_ref.state_ref, bf16[16,16,512]{2,1,0:T(8,128)(2,1)S(1)} %get-tuple-element.110.refs_0_.strips_ref.refs_10_, ...), custom_call_target="tpu_custom_call" | custom-call | tf_op jit(solution)/shard_map/inner_512/pallas_call | solution.py:450
  57.6 3.5 %last_inner.1.refs_13_ = bf16[2,2,14,16,128]{4,3,2,1,0:T(8,128)(2,1)S(1)} custom-call(bf16[2,2,14,16,512]{4,3,2,1,0:T(8,128)(2,1)S(1)} %get-tuple-element.127.field_ref, bf16[16,16,512]{2,1,0:T(8,128)(2,1)S(1)} %get-tuple-element.119.strips_ref.refs_0_, bf16[1536,256]{1,0:T(8,128)(2,1)S(1)} %get-tuple-element.128.weight_ref, ...), custom_call_target="tpu_custom_call" | custom-call | tf_op jit(solution)/shard_map/last_inner/pallas_call | solution.py:450
  62.6 2.9 %last_border.1 = bf16[4,16,16,128]{3,2,1,0:T(8,128)(2,1)} custom-call(bf16[16,16,512]{2,1,0:T(8,128)(2,1)S(1)} %get-tuple-element.119.strips_ref.refs_0_, bf16[16,16,512]{2,1,0:T(8,128)(2,1)S(1)} %get-tuple-element.124.refs_1_, bf16[3,16,512]{2,1,0:T(8,128)(2,1)S(1)} %collective-permute-done.21.refs_2_, ...), custom_call_target="tpu_custom_call" | custom-call | tf_op jit(solution)/shard_map/last_border/pallas_call | solution.py:450
  (43 shorter events, 9.5 us)
Async XLA Ops:
  1.3 11.7 %collective-permute-start.1 = (bf16[3,16,128]{2,1,0:T(8,128)(2,1)S(1)}, bf16[3,16,128]{2,1,0:T(8,128)(2,1)S(1)}, u32[]{:S(2)}, u32[]{:S(2)}) collective-permute-start(bf16[3,16,128]{2,1,0:T(8,128)(2,1)S(1)} %get-tuple-element.73), channel_id=1, source_target_pairs={{0,240},{8,248},{16,32},{24,40},{32,16},{40,24},{48,64},{56,72},{6... | collective-permute-start | bytes 36872 | tf_op jit(solution)/shard_map/ppermute | solution.py:488
  10.4 2.6 %collective-permute-start = (bf16[3,16,128]{2,1,0:T(8,128)(2,1)S(1)}, bf16[3,16,128]{2,1,0:T(8,128)(2,1)S(1)}, u32[]{:S(2)}, u32[]{:S(2)}) collective-permute-start(bf16[3,16,128]{2,1,0:T(8,128)(2,1)S(1)} %get-tuple-element.72), channel_id=1, source_target_pairs={{0,16},{8,24},{16,0},{24,8},{32,48},{40,56},{48,32},{56,40},{64,80... | collective-permute-start | bytes 36872 | tf_op jit(solution)/shard_map/ppermute | solution.py:489
  10.4 4.7 %collective-permute-start.2 = (bf16[5,16,128]{2,1,0:T(8,128)(2,1)S(1)}, bf16[5,16,128]{2,1,0:T(8,128)(2,1)S(1)}, u32[]{:S(2)}, u32[]{:S(2)}) collective-permute-start(bf16[5,16,128]{2,1,0:T(8,128)(2,1)S(1)} %get-tuple-element.76), channel_id=1, source_target_pairs={{0,8},{8,0},{16,24},{24,16},{32,40},{40,32},{48,56},{56,48},{64,72... | collective-permute-start | bytes 61448 | tf_op jit(solution)/shard_map/ppermute | solution.py:490
  13.0 2.9 %collective-permute-start.3 = (bf16[3,16,128]{2,1,0:T(8,128)(2,1)S(1)}, bf16[3,16,128]{2,1,0:T(8,128)(2,1)S(1)}, u32[]{:S(2)}, u32[]{:S(2)}) collective-permute-start(bf16[3,16,128]{2,1,0:T(8,128)(2,1)S(1)} %collective-permute-done.refs_2_), channel_id=1, source_target_pairs={{0,8},{8,0},{16,24},{24,16},{32,40},{40,32},{48,56},{56,48},{64,72... | collective-permute-start | bytes 36872 | tf_op jit(solution)/shard_map/ppermute | solution.py:497
  17.5 7.7 %collective-permute-start.5 = (bf16[3,16,128]{2,1,0:T(8,128)(2,1)S(1)}, bf16[3,16,128]{2,1,0:T(8,128)(2,1)S(1)}, u32[]{:S(2)}, u32[]{:S(2)}) collective-permute-start(bf16[3,16,128]{2,1,0:T(8,128)(2,1)S(1)} %get-tuple-element.82), channel_id=1, source_target_pairs={{0,16},{8,24},{16,0},{24,8},{32,48},{40,56},{48,32},{56,40},{64,80... | collective-permute-start | bytes 36872 | tf_op jit(solution)/shard_map/ppermute | solution.py:489
  17.6 7.6 %collective-permute-start.6 = (bf16[3,16,128]{2,1,0:T(8,128)(2,1)S(1)}, bf16[3,16,128]{2,1,0:T(8,128)(2,1)S(1)}, u32[]{:S(2)}, u32[]{:S(2)}) collective-permute-start(bf16[3,16,128]{2,1,0:T(8,128)(2,1)S(1)} %get-tuple-element.89), channel_id=1, source_target_pairs={{0,240},{8,248},{16,32},{24,40},{32,16},{40,24},{48,64},{56,72},{6... | collective-permute-start | bytes 36872 | tf_op jit(solution)/shard_map/ppermute | solution.py:488
  21.0 4.7 %collective-permute-start.7 = (bf16[5,16,128]{2,1,0:T(8,128)(2,1)S(1)}, bf16[5,16,128]{2,1,0:T(8,128)(2,1)S(1)}, u32[]{:S(2)}, u32[]{:S(2)}) collective-permute-start(bf16[5,16,128]{2,1,0:T(8,128)(2,1)S(1)} %get-tuple-element.96), channel_id=1, source_target_pairs={{0,8},{8,0},{16,24},{24,16},{32,40},{40,32},{48,56},{56,48},{64,72... | collective-permute-start | bytes 61448 | tf_op jit(solution)/shard_map/ppermute | solution.py:490
  25.2 1.3 %collective-permute-start.8 = (bf16[3,16,128]{2,1,0:T(8,128)(2,1)S(1)}, bf16[3,16,128]{2,1,0:T(8,128)(2,1)S(1)}, u32[]{:S(2)}, u32[]{:S(2)}) collective-permute-start(bf16[3,16,128]{2,1,0:T(8,128)(2,1)S(1)} %collective-permute-done.5.refs_2_), channel_id=1, source_target_pairs={{0,8},{8,0},{16,24},{24,16},{32,40},{40,32},{48,56},{56,48},{64,72... | collective-permute-start | bytes 36872 | tf_op jit(solution)/shard_map/ppermute | solution.py:497
  26.6 10.9 %collective-permute-start.13 = (bf16[2,2,14,16,128]{4,3,2,1,0:T(8,128)(2,1)S(1)}, bf16[2,2,14,16,128]{4,3,2,1,0:T(8,128)(2,1)S(1)}, u32[]{:S(2)}, u32[]{:S(2)}) collective-permute-start(bf16[2,2,14,16,128]{4,3,2,1,0:T(8,128)(2,1)S(1)} %inner_second.1.own_ref), channel_id=1, source_target_pairs={{0,6},{2,4},{4,2},{6,0},{1,7},{3,5},{5,3},{7,1},{8,14},{10,12},{12... | collective-permute-start | bytes 688136 | tf_op jit(solution)/shard_map/ppermute | solution.py:503
  30.1 4.8 %collective-permute-start.10 = (bf16[16,16,128]{2,1,0:T(8,128)(2,1)S(1)}, bf16[16,16,128]{2,1,0:T(8,128)(2,1)S(1)}, u32[]{:S(2)}, u32[]{:S(2)}) collective-permute-start(bf16[16,16,128]{2,1,0:T(8,128)(2,1)S(1)} %border_128_1.1.own_ref), channel_id=1, source_target_pairs={{0,4},{2,6},{4,0},{6,2},{1,5},{3,7},{5,1},{7,3},{8,12},{10,14},{12... | collective-permute-start | bytes 196616 | tf_op jit(solution)/shard_map/ppermute | solution.py:503
  30.7 4.2 %collective-permute-start.11 = (bf16[16,16,128]{2,1,0:T(8,128)(2,1)S(1)}, bf16[16,16,128]{2,1,0:T(8,128)(2,1)S(1)}, u32[]{:S(2)}, u32[]{:S(2)}) collective-permute-start(bf16[16,16,128]{2,1,0:T(8,128)(2,1)S(1)} %border_128_1.1.own_ref), channel_id=1, source_target_pairs={{0,2},{2,0},{4,6},{6,4},{1,3},{3,1},{5,7},{7,5},{8,10},{10,8},{12,... | collective-permute-start | bytes 196616 | tf_op jit(solution)/shard_map/ppermute | solution.py:503
  31.0 6.5 %collective-permute-start.12 = (bf16[16,16,128]{2,1,0:T(8,128)(2,1)S(1)}, bf16[16,16,128]{2,1,0:T(8,128)(2,1)S(1)}, u32[]{:S(2)}, u32[]{:S(2)}) collective-permute-start(bf16[16,16,128]{2,1,0:T(8,128)(2,1)S(1)} %border_128_1.1.own_ref), channel_id=1, source_target_pairs={{0,6},{2,4},{4,2},{6,0},{1,7},{3,5},{5,3},{7,1},{8,14},{10,12},{12... | collective-permute-start | bytes 196616 | tf_op jit(solution)/shard_map/ppermute | solution.py:503
  33.5 10.4 %collective-permute-start.15 = (bf16[2,2,14,16,128]{4,3,2,1,0:T(8,128)(2,1)S(1)}, bf16[2,2,14,16,128]{4,3,2,1,0:T(8,128)(2,1)S(1)}, u32[]{:S(2)}, u32[]{:S(2)}) collective-permute-start(bf16[2,2,14,16,128]{4,3,2,1,0:T(8,128)(2,1)S(1)} %inner_second.1.own_ref), channel_id=1, source_target_pairs={{0,2},{2,0},{4,6},{6,4},{1,3},{3,1},{5,7},{7,5},{8,10},{10,8},{12,... | collective-permute-start | bytes 688136 | tf_op jit(solution)/shard_map/ppermute | solution.py:503
  37.5 7.7 %collective-permute-start.16 = (bf16[2,2,14,16,128]{4,3,2,1,0:T(8,128)(2,1)S(1)}, bf16[2,2,14,16,128]{4,3,2,1,0:T(8,128)(2,1)S(1)}, u32[]{:S(2)}, u32[]{:S(2)}) collective-permute-start(bf16[2,2,14,16,128]{4,3,2,1,0:T(8,128)(2,1)S(1)} %collective-permute-done.13.three_ref), channel_id=1, source_target_pairs={{0,2},{2,0},{4,6},{6,4},{1,3},{3,1},{5,7},{7,5},{8,10},{10,8},{12,... | collective-permute-start | bytes 688136 | tf_op jit(solution)/shard_map/ppermute | solution.py:503
  38.3 4.9 %collective-permute-start.17 = (bf16[3,16,512]{2,1,0:T(8,128)(2,1)S(1)}, bf16[3,16,512]{2,1,0:T(8,128)(2,1)S(1)}, u32[]{:S(2)}, u32[]{:S(2)}) collective-permute-start(bf16[3,16,512]{2,1,0:T(8,128)(2,1)S(1)} %get-tuple-element.115), channel_id=1, source_target_pairs={{0,16},{8,24},{16,0},{24,8},{32,48},{40,56},{48,32},{56,40},{64,80... | collective-permute-start | bytes 147464 | tf_op jit(solution)/shard_map/ppermute | solution.py:489
  38.4 8.7 %collective-permute-start.14 = (bf16[3,16,512]{2,1,0:T(8,128)(2,1)S(1)}, bf16[3,16,512]{2,1,0:T(8,128)(2,1)S(1)}, u32[]{:S(2)}, u32[]{:S(2)}) collective-permute-start(bf16[3,16,512]{2,1,0:T(8,128)(2,1)S(1)} %get-tuple-element.111), channel_id=1, source_target_pairs={{0,240},{8,248},{16,32},{24,40},{32,16},{40,24},{48,64},{56,72},{6... | collective-permute-start | bytes 147464 | tf_op jit(solution)/shard_map/ppermute | solution.py:488
  41.7 6.6 %collective-permute-start.18 = (bf16[5,16,512]{2,1,0:T(8,128)(2,1)S(1)}, bf16[5,16,512]{2,1,0:T(8,128)(2,1)S(1)}, u32[]{:S(2)}, u32[]{:S(2)}) collective-permute-start(bf16[5,16,512]{2,1,0:T(8,128)(2,1)S(1)} %get-tuple-element.117), channel_id=1, source_target_pairs={{0,8},{8,0},{16,24},{24,16},{32,40},{40,32},{48,56},{56,48},{64,72... | collective-permute-start | bytes 245768 | tf_op jit(solution)/shard_map/ppermute | solution.py:490
  43.2 5.1 %collective-permute-start.19 = (bf16[3,16,512]{2,1,0:T(8,128)(2,1)S(1)}, bf16[3,16,512]{2,1,0:T(8,128)(2,1)S(1)}, u32[]{:S(2)}, u32[]{:S(2)}) collective-permute-start(bf16[3,16,512]{2,1,0:T(8,128)(2,1)S(1)} %collective-permute-done.17.refs_2_), channel_id=1, source_target_pairs={{0,8},{8,0},{16,24},{24,16},{32,40},{40,32},{48,56},{56,48},{64,72... | collective-permute-start | bytes 147464 | tf_op jit(solution)/shard_map/ppermute | solution.py:497
  47.0 2.2 %collective-permute-start.20 = (bf16[3,16,512]{2,1,0:T(8,128)(2,1)S(1)}, bf16[3,16,512]{2,1,0:T(8,128)(2,1)S(1)}, u32[]{:S(2)}, u32[]{:S(2)}) collective-permute-start(bf16[3,16,512]{2,1,0:T(8,128)(2,1)S(1)} %collective-permute-done.14.refs_3_), channel_id=1, source_target_pairs={{0,8},{8,0},{16,24},{24,16},{32,40},{40,32},{48,56},{56,48},{64,72... | collective-permute-start | bytes 147464 | tf_op jit(solution)/shard_map/ppermute | solution.py:497
  51.0 10.1 %collective-permute-start.21 = (bf16[3,16,512]{2,1,0:T(8,128)(2,1)S(1)}, bf16[3,16,512]{2,1,0:T(8,128)(2,1)S(1)}, u32[]{:S(2)}, u32[]{:S(2)}) collective-permute-start(bf16[3,16,512]{2,1,0:T(8,128)(2,1)S(1)} %get-tuple-element.120), channel_id=1, source_target_pairs={{0,16},{8,24},{16,0},{24,8},{32,48},{40,56},{48,32},{56,40},{64,80... | collective-permute-start | bytes 147464 | tf_op jit(solution)/shard_map/ppermute | solution.py:489
  51.1 10.0 %collective-permute-start.22 = (bf16[3,16,512]{2,1,0:T(8,128)(2,1)S(1)}, bf16[3,16,512]{2,1,0:T(8,128)(2,1)S(1)}, u32[]{:S(2)}, u32[]{:S(2)}) collective-permute-start(bf16[3,16,512]{2,1,0:T(8,128)(2,1)S(1)} %get-tuple-element.126), channel_id=1, source_target_pairs={{0,240},{8,248},{16,32},{24,40},{32,16},{40,24},{48,64},{56,72},{6... | collective-permute-start | bytes 147464 | tf_op jit(solution)/shard_map/ppermute | solution.py:488
  54.3 7.5 %collective-permute-start.23 = (bf16[5,16,512]{2,1,0:T(8,128)(2,1)S(1)}, bf16[5,16,512]{2,1,0:T(8,128)(2,1)S(1)}, u32[]{:S(2)}, u32[]{:S(2)}) collective-permute-start(bf16[5,16,512]{2,1,0:T(8,128)(2,1)S(1)} %get-tuple-element.130), channel_id=1, source_target_pairs={{0,8},{8,0},{16,24},{24,16},{32,40},{40,32},{48,56},{56,48},{64,72... | collective-permute-start | bytes 245768 | tf_op jit(solution)/shard_map/ppermute | solution.py:490
  61.1 1.3 %collective-permute-start.24 = (bf16[3,16,512]{2,1,0:T(8,128)(2,1)S(1)}, bf16[3,16,512]{2,1,0:T(8,128)(2,1)S(1)}, u32[]{:S(2)}, u32[]{:S(2)}) collective-permute-start(bf16[3,16,512]{2,1,0:T(8,128)(2,1)S(1)} %collective-permute-done.21.refs_2_), channel_id=1, source_target_pairs={{0,8},{8,0},{16,24},{24,16},{32,40},{40,32},{48,56},{56,48},{64,72... | collective-permute-start | bytes 147464 | tf_op jit(solution)/shard_map/ppermute | solution.py:497
  61.2 1.4 %collective-permute-start.25 = (bf16[3,16,512]{2,1,0:T(8,128)(2,1)S(1)}, bf16[3,16,512]{2,1,0:T(8,128)(2,1)S(1)}, u32[]{:S(2)}, u32[]{:S(2)}) collective-permute-start(bf16[3,16,512]{2,1,0:T(8,128)(2,1)S(1)} %collective-permute-done.22.refs_3_), channel_id=1, source_target_pairs={{0,8},{8,0},{16,24},{24,16},{32,40},{40,32},{48,56},{56,48},{64,72... | collective-permute-start | bytes 147464 | tf_op jit(solution)/shard_map/ppermute | solution.py:497
  (3 other events, 7.4 us)
